TPU v7x, 32 devices: a whole 2x2x4 slice. The times are simulated.
32 devices in a mesh: req: 4 (over z), seq: 8 (over y, x, core).
Axes of the slice: x: 2, y: 2, z: 4, core: 2. Of those that a mesh axis runs over, the one named last changes fastest.
Arguments:
- q_nope: bfloat16 [2, 8, 128, 128], P(None, None, 'req'), may hold values from -16 to 16
- q_rope: bfloat16 [2, 8, 128, 64], P(None, None, 'req'), may hold values from -16 to 16
- w_uk: bfloat16 [128, 128, 512], P('req'), may hold values from -0.5 to 0.5
- w_uv: bfloat16 [128, 512, 128], P('req'), may hold values from -0.25 to 0.25
- latent_cache: bfloat16 [8, 49152, 512], P('req', 'seq'), may hold values from -120 to 120, as said below
- rope_cache: bfloat16 [8, 49152, 64], P('req', 'seq'), may hold values from -6 to 6
- positions: int32 [8, 49152], P('req', 'seq'), may hold values from 0 to 98303, as said below
- new_latent: bfloat16 [2, 8, 512], replicated, may hold values from -12 to 12
- new_rope: bfloat16 [2, 8, 64], replicated, may hold values from -6 to 6
- new_pos: int32 [8], replicated, may hold values from 98304 to 102399
- lengths: int32 [8], replicated, may hold values from 8192 to 49152, as said below
- assignment: int32 [8], replicated, may hold values from 0 to 7, each once
Outputs:
- attn_out: bfloat16 [2, 8, 128, 128], P(None, None, 'req')
Inputs may be any that keep to these rules, and one draw needn't show every extreme that they name: lengths are given by request; the longest request uses all 49152 rows. Within each slot the positions rise strictly along the rows, by 1 or 2 a row, starting at 0 or 1; some slot rises by 2 on every row and ends at the largest value, some slot starts at 0. `new_pos`: each request's new positions exceed every cached position. `assignment`: a permutation; slots g * 2 to (g + 1) * 2 - 1 form request group g. `latent_cache`: entries lie within the given bounds.
All inputs are finite; a program needn't handle non-finite values.
Results may differ from a plain program's by a relative error of at most 0.0085.
The roundings to bfloat16 on the way count: a program that leaves them out, or rounds other values in their place, can miss the bound.
Values may be sent and summed in bfloat16 or wider, within the bound.
No kernel may reach another device: no remote copies, remote signals or barrier semaphores. Data moves between devices by JAX's collectives and lax.ppermute only.
A program may use at most 192 MiB of HBM per device.

v0:
```python
import math

import jax
import jax.numpy as jnp
from jax import lax
from jax.sharding import PartitionSpec as P

DR = 64
DN = 128


def merged(shard, axis, combine):
    everything = jax.tree.map(lambda part: lax.all_gather(part, axis), shard)
    first = jax.tree.map(lambda part: part[0], everything)

    def step(k, so_far):
        return combine(so_far, jax.tree.map(lambda part: part[k], everything))

    return lax.fori_loop(1, lax.axis_size(axis), step, first)


def rotate(values, position):
    half_width = values.shape[-1] // 2
    frequency = jnp.exp(
        jnp.arange(half_width, dtype=jnp.float32) * (-2.0 * math.log(10000.0) / values.shape[-1])
    )
    angles = position.astype(jnp.float32)[..., None] * frequency
    cosine = jnp.cos(angles)
    sine_part = jnp.sin(angles)
    former = values[..., :half_width]
    latter = values[..., half_width:]
    return jnp.concatenate(
        [former * cosine - latter * sine_part, latter * cosine + former * sine_part], axis=-1
    )


def combine_parts(former, latter):
    row_top = jnp.maximum(former[0], latter[0])
    former_scale = jnp.exp(former[0] - row_top)
    latter_scale = jnp.exp(latter[0] - row_top)
    return (
        row_top,
        former[1] * former_scale + latter[1] * latter_scale,
        former[2] * former_scale[..., None] + latter[2] * latter_scale[..., None],
    )


def body(
    q_nope,
    q_rope,
    w_uk,
    w_uv,
    latent_cache,
    rope_cache,
    positions,
    new_latent,
    new_rope,
    new_pos,
    lengths,
    assignment,
):
    step_count = q_nope.shape[0]
    request_count = q_nope.shape[1]
    heads_local = q_nope.shape[2]
    group_count = lax.axis_size("req")
    per_group = request_count // group_count
    group_index = lax.axis_index("req")
    shard_index = lax.axis_index("seq")
    capacity = latent_cache.shape[1]
    lat_width = w_uk.shape[2]
    rope_width = q_rope.shape[3]
    head_total = heads_local * group_count
    score_scale = 1.0 / math.sqrt(DN + DR)
    step_ids = jnp.arange(step_count, dtype=jnp.int32)
    ordered_nope = q_nope[:, assignment]
    q_latent = jnp.einsum(
        "srhn,hnl->srhl", ordered_nope, w_uk, preferred_element_type=jnp.float32
    ).astype(jnp.bfloat16)
    query_pos = new_pos[assignment][None, :] + step_ids[:, None]
    q_rotated = rotate(q_rope[:, assignment].astype(jnp.float32), query_pos[:, :, None]).astype(
        jnp.bfloat16
    )
    my_requests = lax.dynamic_slice_in_dim(assignment, group_index * per_group, per_group)
    my_lengths = lengths[my_requests]
    global_rows = shard_index * capacity + jnp.arange(capacity, dtype=jnp.int32)
    valid_rows = global_rows[None, :] < my_lengths[:, None]
    rotated_keys = rotate(rope_cache.astype(jnp.float32), positions).astype(jnp.bfloat16)
    new_latents = new_latent[:, my_requests]
    new_keys = rotate(
        new_rope[:, my_requests].astype(jnp.float32),
        new_pos[my_requests][None, :] + step_ids[:, None],
    ).astype(jnp.bfloat16)

    def attend(lat_query, rope_query, step_list):
        scores = (
            jnp.einsum(
                "sghl,gcl->sghc", lat_query, latent_cache, preferred_element_type=jnp.float32
            )
            + jnp.einsum(
                "sghd,gcd->sghc", rope_query, rotated_keys, preferred_element_type=jnp.float32
            )
        ) * score_scale
        new_scores = (
            jnp.einsum("sghl,ugl->sghu", lat_query, new_latents, preferred_element_type=jnp.float32)
            + jnp.einsum("sghd,ugd->sghu", rope_query, new_keys, preferred_element_type=jnp.float32)
        ) * score_scale
        new_valid = (step_ids[None, :] <= step_list[:, None]) & (shard_index == 0)
        cache_mask = valid_rows[None, :, None, :]
        new_mask = new_valid[:, None, None, :]
        local_top = jnp.maximum(
            jnp.max(jnp.where(cache_mask, scores, -1e30), axis=3),
            jnp.max(jnp.where(new_mask, new_scores, -1e30), axis=3),
        )
        cache_weights = jnp.where(cache_mask, jnp.exp(scores - local_top[..., None]), 0.0)
        new_weights = jnp.where(new_mask, jnp.exp(new_scores - local_top[..., None]), 0.0)
        totals = jnp.sum(cache_weights, axis=3) + jnp.sum(new_weights, axis=3)
        output_sum = jnp.einsum(
            "sghc,gcl->sghl",
            cache_weights.astype(jnp.bfloat16),
            latent_cache,
            preferred_element_type=jnp.float32,
        ) + jnp.einsum(
            "sghu,ugl->sghl",
            new_weights.astype(jnp.bfloat16),
            new_latents,
            preferred_element_type=jnp.float32,
        )
        merged_top, merged_totals, merged_sums = merged(
            (local_top, totals, output_sum), "seq", combine_parts
        )
        return (merged_sums / merged_totals[..., None]).astype(jnp.bfloat16)

    def run_steps(lat_block, rope_block, step_list):
        block_steps = lat_block.shape[0]
        arrived_lat, arrived_rope = (
            lax.all_to_all(
                lat_block.reshape(block_steps, request_count, heads_local * lat_width),
                "req",
                split_axis=1,
                concat_axis=2,
                tiled=True,
            ),
            lax.all_to_all(
                rope_block.reshape(block_steps, request_count, heads_local * rope_width),
                "req",
                split_axis=1,
                concat_axis=2,
                tiled=True,
            ),
        )
        attended = attend(
            arrived_lat.reshape(block_steps, per_group, head_total, lat_width),
            arrived_rope.reshape(block_steps, per_group, head_total, rope_width),
            step_list,
        )
        returned = lax.all_to_all(
            attended.reshape(block_steps, per_group, head_total * lat_width),
            "req",
            split_axis=2,
            concat_axis=1,
            tiled=True,
        )
        return jnp.einsum(
            "srhl,hlv->srhv",
            returned.reshape(block_steps, request_count, heads_local, lat_width),
            w_uv,
            preferred_element_type=jnp.float32,
        ).astype(jnp.bfloat16)

    by_slot = jnp.concatenate(
        [
            run_steps(
                q_latent[step_index : step_index + 1],
                q_rotated[step_index : step_index + 1],
                step_ids[step_index : step_index + 1],
            )
            for step_index in range(step_count)
        ],
        axis=0,
    )
    return jnp.zeros_like(by_slot).at[:, assignment].set(by_slot)


def solution(mesh):
    in_specs = (
        P(None, None, "req", None),
        P(None, None, "req", None),
        P("req", None, None),
        P("req", None, None),
        P("req", "seq", None),
        P("req", "seq", None),
        P("req", "seq"),
        P(),
        P(),
        P(),
        P(),
        P(),
    )
    out_specs = P(None, None, "req", None)
    return jax.shard_map(body, mesh=mesh, in_specs=in_specs, out_specs=out_specs, check_vma=False)
```

profile of v0, /device:TPU:0, one launch (start us, length us, event | category | flops | bytes accessed | tf_op | source)
XLA Modules:
  0.0 1335.2 jit_solution(1434700971722142927)
XLA Ops:
  7.3 1.3 gather_fusion.3
  8.7 1.5 gather_fusion.2
  12.8 6.3 all-to-all-start.4
  20.5 1.3 gather_fusion.6
  21.9 1.3 gather_fusion
  23.2 1.3 gather_fusion.5
  25.9 2.8 fusion.49
  29.3 6.3 fusion.35
  38.9 2.2 reduce.23
  41.0 0.9 reshape.539
  42.3 2.2 reduce.21
  45.4 5.1 all-to-all-start.1
  50.7 5.4 all-to-all-done.1
  56.2 3.4 all-to-all-start
  60.1 3.6 fusion.58
  63.8 2.5 all-to-all-done
  66.3 3.4 all-to-all-start.3
  70.0 3.6 fusion.59
  73.9 1.5 bitcast_reduce_fusion.5
  76.8 1.5 bitcast_reduce_fusion.4
  79.0 13.2 fusion.15
  92.4 15.2 %select_reduce_fusion.1 = (f32[2,128]{1,0:T(2,128)S(1)}, f32[2,128]{1,0:T(2,128)S(1)}, f32[2,6144,1,128]{1,3,0,2:T(8,128)}) fusion(pred[2,6144]{1,0:T(4,128)(4,1)S(1)} %broadcast_compare_fusion, f32[2,6144,1,128]{1,3,0,2:T(8,128)} %fusion.15, f32[2,6144,128]{1,2,0:T(8,128)} %fusion.58, bf16[2,128,512]{2,1,0:T(8,128)(2,1)S(1)} %reshape.405, ...), kind=kOutput, calls=%fused_computation.45 | convolution fusion | flops 1620049408 | bytes 31733760 | tf_op jit(solution)/shard_map/sghl,gcl->sghc/dot_general | solution.py:96
  107.6 8.3 fusion.41
  116.0 1.1 fusion.47
  118.2 8.4 fusion.44
  126.5 1.1 fusion.48
  127.8 14.9 %bitcast_reduce_fusion.1 = (f32[2,128]{1,0:T(2,128)S(1)}, f32[2,128]{1,0:T(2,128)S(1)}) fusion(f32[2,6144,1,128]{1,3,0,2:T(8,128)} %get-tuple-element.487, f32[2,128]{1,0:T(2,128)S(1)} %max.58, pred[2,6144]{1,0:T(4,128)(4,1)S(1)} %broadcast_compare_fusion, f32[2,6144,1,128]{1,3,0,2:T(8,128)} %fusion.15, f32[2,128]{1,0:T(2,128)S(1)} %max.60), kind=kLoop, calls=%fused_computation.41 | loop fusion | flops 9436672 | bytes 12599296 | tf_op jit(solution)/shard_map/reduce_sum | solution.py:116
  142.7 8.7 all-gather.9
  151.5 8.8 all-gather.7
  160.3 7.9 all-gather.6
  168.2 8.8 all-gather.8
  177.1 1.1 slice.111
  178.1 9.2 while.39
  178.2 1.4 fusion.113
  179.7 1.2 fusion.113
  181.0 1.2 fusion.113
  182.2 1.2 fusion.113
  183.5 1.2 fusion.113
  184.8 1.2 fusion.113
  186.1 1.2 fusion.113
  187.7 50.3 %copy.131 = bf16[1,2,65536]{1,0,2:T(2,128)(2,1)} copy(bf16[1,2,65536]{2,1,0:T(2,128)(2,1)S(1)} %reshape.418) | data formatting | bytes 524288 | tf_op jit(solution)/shard_map/reshape | solution.py:157
  237.9 355.8 %reduce.24 = bf16[65536,2]{1,0:T(8,128)(2,1)} reduce(bf16[65536,1,2]{2,1,0:T(2,128)(2,1)} %bitcast.255, bf16[]{:T(256)} %broadcast.260), dimensions={1}, to_apply=%bitcast.209.reduce_sub_computation | reduce | bytes 524290
  593.7 37.1 %reshape.545 = bf16[4,2,16384]{2,1,0:T(2,128)(2,1)} reshape(bf16[65536,2]{1,0:T(8,128)(2,1)} %reduce.24) | data formatting | bytes 524288
  630.9 5.0 all-to-all-start.5
  635.9 1.1 slice.107
  637.0 9.1 while.38
  637.1 1.2 fusion.110
  638.4 1.2 fusion.110
  639.7 1.2 fusion.110
  641.0 1.2 fusion.110
  642.3 1.2 fusion.110
  643.6 1.2 fusion.110
  644.8 1.2 fusion.110
  646.4 50.3 %copy.114 = bf16[1,2,65536]{1,0,2:T(2,128)(2,1)} copy(bf16[1,2,65536]{2,1,0:T(2,128)(2,1)S(1)} %reshape.410) | data formatting | bytes 524288 | tf_op jit(solution)/shard_map/reshape | solution.py:157
  696.7 355.8 %reduce.25 = bf16[65536,2]{1,0:T(8,128)(2,1)} reduce(bf16[65536,1,2]{2,1,0:T(2,128)(2,1)} %bitcast.254, bf16[]{:T(256)} %broadcast.260), dimensions={1}, to_apply=%bitcast.211.reduce_sub_computation | reduce | bytes 524290
  1052.5 37.1 %reshape.547 = bf16[4,2,16384]{2,1,0:T(2,128)(2,1)} reshape(bf16[65536,2]{1,0:T(8,128)(2,1)} %reduce.25) | data formatting | bytes 524288
  1089.5 5.3 all-to-all-start.2
  1094.9 50.8 %reshape.546 = bf16[65536,1,2]{2,1,0:T(2,128)(2,1)} reshape(bf16[4,2,16384]{2,1,0:T(2,128)(2,1)S(1)} %all-to-all-done.5) | data formatting | bytes 524288
  1145.7 60.8 %copy.132 = bf16[1,2,65536]{2,1,0:T(2,128)(2,1)S(1)} copy(bf16[1,2,65536]{1,0,2:T(2,128)(2,1)} %bitcast.256) | data formatting | bytes 524288 | tf_op jit(solution)/shard_map/all_to_all | solution.py:156
  1207.2 50.8 %reshape.548 = bf16[65536,1,2]{2,1,0:T(2,128)(2,1)} reshape(bf16[4,2,16384]{2,1,0:T(2,128)(2,1)S(1)} %all-to-all-done.2) | data formatting | bytes 524288
  1258.0 60.9 %copy.115 = bf16[1,2,65536]{2,1,0:T(2,128)(2,1)S(1)} copy(bf16[1,2,65536]{1,0,2:T(2,128)(2,1)} %bitcast.257) | data formatting | bytes 524288 | tf_op jit(solution)/shard_map/all_to_all | solution.py:156
  1319.5 2.9 fusion.53
  1322.4 2.9 fusion.52
  1326.0 2.1 scatter_fusion
  (143 shorter events, 19.3 us)
Async XLA Ops:
  6.5 18.7 %copy-start = (bf16[2,8,32,128]{3,2,1,0:T(8,128)(2,1)S(1)}, bf16[2,8,32,128]{3,2,1,0:T(8,128)(2,1)}, u32[]{:S(2)}) copy-start(bf16[2,8,32,128]{3,2,1,0:T(8,128)(2,1)} %param.16) | copy-start | bytes 393220
  6.5 22.2 %copy-start.2 = (bf16[2,6144,64]{1,2,0:T(8,128)(2,1)S(1)}, bf16[2,6144,64]{1,2,0:T(8,128)(2,1)}, u32[]{:S(2)}) copy-start(bf16[2,6144,64]{1,2,0:T(8,128)(2,1)} %param.21) | copy-start | bytes 4718596
  7.3 1.3 copy-start.4
  12.8 32.6 %all-to-all-start.4 = ((bf16[4,2,2048]{2,1,0:T(2,128)(2,1)}), bf16[4,2,2048]{2,1,0:T(2,128)(2,1)S(1)}, u32[]{:S(2)}, u32[]{:S(2)}) async-start(bf16[4,2,2048]{2,1,0:T(2,128)(2,1)} %reshape.541), calls=%async_computation.4 | async-start | bytes 65536 | tf_op jit(solution)/shard_map/all_to_all | solution.py:143
  28.7 7.6 copy-start.3
  45.4 10.7 all-to-all-start.1
  56.2 10.2 all-to-all-start
  66.3 10.2 all-to-all-start.3
  69.7 107.3 %all-gather.15.cloned.1.call-start = ((), (), s32[]{:S(2)}) async-start(), calls=%async_computation.7 | async-start | bytes 4718592 | tf_op jit(solution)/shard_map/all_gather | solution.py:13
  117.1 518.8 %all-gather.13.cloned.1.call-start = ((), (), s32[]{:S(2)}) async-start(), calls=%async_computation.6 | async-start | bytes 4718592 | tf_op jit(solution)/shard_map/all_gather | solution.py:13
  630.9 458.7 %all-to-all-start.5 = ((bf16[4,2,16384]{2,1,0:T(2,128)(2,1)}), bf16[4,2,16384]{2,1,0:T(2,128)(2,1)S(1)}, u32[]{:S(2)}, u32[]{:S(2)}) async-start(bf16[4,2,16384]{2,1,0:T(2,128)(2,1)} %reshape.545), calls=%async_computation.5 | async-start | bytes 524288 | tf_op jit(solution)/shard_map/all_to_all | solution.py:156
  1089.5 117.6 %all-to-all-start.2 = ((bf16[4,2,16384]{2,1,0:T(2,128)(2,1)}), bf16[4,2,16384]{2,1,0:T(2,128)(2,1)S(1)}, u32[]{:S(2)}, u32[]{:S(2)}) async-start(bf16[4,2,16384]{2,1,0:T(2,128)(2,1)} %reshape.547), calls=%async_computation.2 | async-start | bytes 524288 | tf_op jit(solution)/shard_map/all_to_all | solution.py:156
  1258.0 70.2 %copy-start.1 = (bf16[2,8,32,128]{3,2,1,0:T(8,128)(2,1)S(1)}, bf16[2,8,32,128]{3,2,1,0:T(8,128)(2,1)}, u32[]{:S(2)}) copy-start(bf16[2,8,32,128]{3,2,1,0:T(8,128)(2,1)} %param.16) | copy-start | bytes 393220
  1318.8 7.2 copy-start.5
Sparse Core Ops, SparseCore 0:
  117.3 37.7 all-gather.14
  156.9 36.7 all-gather.12
where the time goes:
time: 1340 us
  other arithmetic  762 us (57%)
  local copies, waits for them, and re-layouts  423 us (32%)
  matrix products  64 us (5%)
  blocking collectives  34.2 us (3%)
  starting transfers between devices  28.9 us (2%)
  between operations  14.1 us (1%)
    unnamed x8, other arithmetic  718 us
    unnamed x25, local copies, waits for them, and re-layouts  180 us
    all_to_all x6, local copies, waits for them, and re-layouts, run_steps(): lax.all_to_all(attended.reshape(block_steps, per_group, head_total * lat_...  123 us
    reshape x4, local copies, waits for them, and re-layouts, run_steps(): attended.reshape(block_steps, per_group, head_total * lat_width)  101 us
    all_gather x4, blocking collectives, merged(): everything = jax.tree.map(lambda part: lax.all_gather(part, axis), shard)  34.2 us
    dot_general x2, matrix products, attend(): jnp.einsum('sghl,gcl->sghc', lat_query, latent_cache, preferred_element_t...  28.4 us
  transfers between devices with their start and end apart: 8, of which 3 were waited for; matrix products, arithmetic and copies ran while one was open for 81% of the time, Pallas kernels for 0%

commit v1 on v0

v1 whole, which is shorter than its diff:
```python
import functools
import math

import jax
import jax.numpy as jnp
import numpy as np
from jax import lax
from jax.experimental import pallas as pl
from jax.experimental.pallas import tpu as pltpu
from jax.sharding import Mesh
from jax.sharding import PartitionSpec as P

DR = 64
DN = 128
LANES = 128
LOW = -1e30
EXPO = math.log2(math.e) / math.sqrt(DN + DR)
BF = jnp.bfloat16
F32 = jnp.float32
VMEM = pl.BlockSpec(memory_space=pltpu.VMEM)
SMEM = pl.BlockSpec(memory_space=pltpu.SMEM)
ANY = pl.BlockSpec(memory_space=pl.ANY)


def turn_rates(width):
    half = width // 2
    slope = np.float32(-2.0 * math.log(10000.0) / width)
    frequency = np.exp(np.arange(half, dtype=np.float32) * slope).astype(np.float64)
    return np.round(frequency / (2.0 * math.pi) * 2.0**32).astype(np.int64).astype(np.int32)


def sin_cos(phase):
    x = phase.astype(F32) * np.float32(math.pi * 2.0**-32)
    z = x * x
    s = np.float32(2.7525562e-06)
    for c in (-0.00019840874, 0.0083333310, -0.16666667, 1.0):
        s = s * z + np.float32(c)
    s = s * x
    c = np.float32(-2.6051615e-07)
    for k in (2.4760495e-05, -0.0013888378, 0.041666638, -0.5, 1.0):
        c = c * z + np.float32(k)
    return 2.0 * s * c, 1.0 - 2.0 * s * s


def split3(x):
    a = x.astype(BF)
    r = x - a.astype(F32)
    b = r.astype(BF)
    return a.astype(F32), b.astype(F32), r - b.astype(F32)


def stat_lanes(rows, values):
    lane = lax.broadcasted_iota(jnp.int32, (rows, LANES), 1)
    tile = jnp.zeros((rows, LANES), F32)
    for i, v in enumerate(values):
        tile = jnp.where(lane == i, v, tile)
    return tile


def absorb_kernel(dims, assign, new_pos, qn, qr, rate, w_hbm, *rest):
    R, J, T, HC, DL = dims
    outs, wbuf, sem = rest[:R], rest[R], rest[R + 1]
    g, c = lax.axis_index("req"), lax.axis_index("core")
    piece = HC // 4
    copies = []
    for i in range(4):
        copies.append(
            pltpu.make_async_copy(
                w_hbm.at[pl.ds(c * HC + i * piece, piece)],
                wbuf.at[pl.ds(i * piece, piece)],
                sem.at[i],
            )
        )
        copies[-1].start()
    tokens = [(k, j, t) for k in range(R) for j in range(J) for t in range(T)]
    who = [assign[(g ^ k) * J + j] for k, j, t in tokens]
    half = pl.ds(pl.multiple_of(c * HC, HC), HC)
    x = jnp.stack([qn[t, who[i], half, :].astype(F32) for i, (k, j, t) in enumerate(tokens)])
    x = jnp.swapaxes(x, 0, 1).astype(BF)
    row = lax.broadcasted_iota(jnp.int32, (len(tokens), DR), 0)
    pos = jnp.zeros((len(tokens), DR), jnp.int32)
    for i, (k, j, t) in enumerate(tokens):
        pos = jnp.where(row == i, new_pos[who[i]] + t, pos)
    sine, cosine = sin_cos(pos * rate[...])
    lane = lax.broadcasted_iota(jnp.int32, (len(tokens), DR), 1)
    sine = jnp.where(lane < DR // 2, -sine, sine)
    one = (lax.broadcasted_iota(jnp.int32, (HC, LANES - DR), 1) == 0).astype(F32)
    for i, (k, j, t) in enumerate(tokens):
        v = qr[t, who[i], half, :].astype(F32)
        swapped = jnp.concatenate([v[:, DR // 2 :], v[:, : DR // 2]], axis=1)
        turned = v * cosine[i : i + 1] + swapped * sine[i : i + 1]
        outs[k][j, t, :, DL:] = jnp.concatenate([turned, one], axis=1).astype(BF)
    ys = []
    for h in range(HC):
        if h % piece == 0:
            copies[h // piece].wait()
        ys.append(jnp.dot(x[h], wbuf[h], preferred_element_type=F32))
    y = jnp.swapaxes(jnp.stack(ys), 0, 1).astype(BF)
    for i, (k, j, t) in enumerate(tokens):
        outs[k][j, t, :, :DL] = y[i]


def rope_kernel(dims, block, assign, lengths, pos, rope, rate, out):
    J, CAP = dims
    g = lax.axis_index("req")
    shard = lax.axis_index("chip") * lax.axis_size("core") + lax.axis_index("core")
    half = DR // 2
    first = shard * CAP + pl.program_id(0) * block
    where_row = first + lax.broadcasted_iota(jnp.int32, (1, block), 1)
    sub = lax.broadcasted_iota(jnp.int32, (LANES - DR, block), 0)
    for j in range(J):
        sine, cosine = sin_cos(pos[j : j + 1, :] * rate[...])
        a = rope[j, :half, :].astype(F32)
        b = rope[j, half:, :].astype(F32)
        out[j, :half, :] = (a * cosine - b * sine).astype(BF)
        out[j, half:DR, :] = (b * cosine + a * sine).astype(BF)
        bad = where_row >= lengths[assign[g * J + j]]
        out[j, DR:, :] = jnp.where((sub == 0) & bad, LOW, 0.0).astype(BF)


def attend_kernel(
    dims, B, assign, new_pos, own, other, keys, new_lat, new_rope, rate, c_hbm,
    send, keep, q, cbuf, sbuf, acc, csem,
):
    R, J, T, HC, DL, CAP = dims
    nb = CAP // B
    NQ = T * R * 2 * HC
    g, c = lax.axis_index("req"), lax.axis_index("core")
    first_shard = (lax.axis_index("chip") == 0) & (c == 0)

    def fetch(j, i):
        rows = pl.ds(i * B, B)
        return pltpu.make_async_copy(c_hbm.at[j, rows], cbuf.at[j, rows], csem.at[j, i])

    for j in range(J):
        for i in range(nb):
            fetch(j, i).start()
    for j in range(J):
        for t in range(T):
            for k in range(R):
                mine, theirs = own[k, j, t], other[k, j, t]
                base = (t * R + k) * 2 * HC
                q[j, base : base + HC, :] = jnp.where(c == 0, mine, theirs)
                q[j, base + HC : base + 2 * HC, :] = jnp.where(c == 0, theirs, mine)
    nt = (((1,), (1,)), ((), ()))

    def score(j, i):
        rows = pl.ds(i * B, B)
        return lax.dot_general(
            q[j, :, :DL], cbuf[j, rows], nt, preferred_element_type=F32
        ) + jnp.dot(q[j, :, DL:], keys[j, :, rows], preferred_element_type=F32)

    for j in range(J):
        r = assign[g * J + j]
        fetch(j, 0).wait()
        sbuf[0] = score(j, 0)
        pick = lax.broadcasted_iota(jnp.int32, new_lat.shape[1:], 0) == r
        lat = [
            jnp.sum(jnp.where(pick, new_lat[u].astype(F32), 0.0), axis=0, keepdims=True)
            for u in range(T)
        ]
        pick = lax.broadcasted_iota(jnp.int32, new_rope.shape[1:], 0) == r
        rop = [
            jnp.sum(jnp.where(pick, new_rope[u].astype(F32), 0.0), axis=0, keepdims=True)
            for u in range(T)
        ]
        lat = jnp.concatenate(lat + [jnp.zeros((LANES - T, DL), F32)], axis=0).astype(BF)
        rop = jnp.concatenate(rop + [jnp.zeros((8 - T, DR), F32)], axis=0)
        step = lax.broadcasted_iota(jnp.int32, (8, DR), 0)
        lane = lax.broadcasted_iota(jnp.int32, (8, DR), 1)
        sine, cosine = sin_cos((new_pos[r] + step) * rate[:8])
        sine = jnp.where(lane < DR // 2, -sine, sine)
        swapped = jnp.concatenate([rop[:, DR // 2 :], rop[:, : DR // 2]], axis=1)
        rop = rop * cosine + swapped * sine
        rop = jnp.concatenate([rop, jnp.zeros((8, LANES - DR), F32)], axis=1)
        rop = jnp.concatenate([rop, jnp.zeros((LANES - 8, LANES), F32)], axis=0).astype(BF)
        s = lax.dot_general(q[j, :, :DL], lat, nt, preferred_element_type=F32)
        s = s + lax.dot_general(q[j, :, DL:], rop, nt, preferred_element_type=F32)
        u = lax.broadcasted_iota(jnp.int32, (NQ, LANES), 1)
        t_of = lax.broadcasted_iota(jnp.int32, (NQ, LANES), 0) // (NQ // T)
        valid = (u <= t_of) & (u < T) & first_shard
        m = jnp.max(jnp.where(valid, s, LOW), axis=1, keepdims=True)
        p = jnp.where(valid, jnp.exp2(s * EXPO - m * EXPO), 0.0)
        l = jnp.sum(p, axis=1, keepdims=True)
        acc[...] = jnp.dot(p.astype(BF), lat, preferred_element_type=F32)
        for i in range(nb):
            if i + 1 < nb:
                fetch(j, i + 1).wait()
                sbuf[(i + 1) % 2] = score(j, i + 1)
            s = sbuf[i % 2]
            top = jnp.maximum(m, jnp.max(s, axis=1, keepdims=True))
            shrink = jnp.exp2((m - top) * EXPO)
            p = jnp.exp2(s * EXPO - top * EXPO)
            l = l * shrink + jnp.sum(p, axis=1, keepdims=True)
            acc[...] = acc[...] * shrink + jnp.dot(
                p.astype(BF), cbuf[j, pl.ds(i * B, B)], preferred_element_type=F32
            )
            m = top
        whole = stat_lanes(NQ, (m, l))
        parts = stat_lanes(NQ, split3(m) + split3(l))
        for t in range(T):
            for k in range(R):
                base = (t * R + k) * 2 * HC
                lo, hi = slice(base, base + HC), slice(base + HC, base + 2 * HC)
                keep[j, t, k, :, :DL] = jnp.where(c == 0, acc[lo], acc[hi])
                send[j, t, k, :, :DL] = jnp.where(c == 0, acc[hi], acc[lo]).astype(BF)
                keep[j, t, k, :, DL:] = jnp.where(c == 0, whole[lo], whole[hi])
                send[j, t, k, :, DL:] = jnp.where(c == 0, parts[hi], parts[lo]).astype(BF)


def pair_kernel(dims, keep, got, out):
    R, J, T, HC, HS, CH, DL = dims
    g = lax.axis_index("req")
    HB = HC // HS
    for j in range(J):
        for t in range(T):
            for k in range(R):
                a = keep[j, t, k]
                b = got[j, t, k].astype(F32)
                ma, la = a[:, DL : DL + 1], a[:, DL + 1 : DL + 2]
                mb = b[:, DL : DL + 1] + b[:, DL + 1 : DL + 2] + b[:, DL + 2 : DL + 3]
                lb = b[:, DL + 3 : DL + 4] + b[:, DL + 4 : DL + 5] + b[:, DL + 5 : DL + 6]
                m = jnp.maximum(ma, mb)
                wa, wb = jnp.exp2((ma - m) * EXPO), jnp.exp2((mb - m) * EXPO)
                o = (a[:, :DL] * wa + b[:, :DL] * wb).astype(BF)
                st = stat_lanes(HC, split3(m) + split3(la * wa + lb * wb)).astype(BF)
                for s in range(HS):
                    at = (g ^ k) * CH + (j * T + t) * HS + s
                    out[at, :, :DL] = o[s * HB : (s + 1) * HB]
                    out[at, :, DL:] = st[s * HB : (s + 1) * HB]


def value_kernel(dims, got, w_hbm, out, wbuf, sem):
    R, CH, HC, HS, HB, DL, DV, JT = dims
    c = lax.axis_index("core")
    part = lax.rem(lax.axis_index("chip"), HS)
    first = c * HC + part * HB
    fetch = pltpu.make_async_copy(w_hbm.at[pl.ds(first, HB)], wbuf, sem)
    fetch.start()
    rows = []
    for r in range(R):
        x = [got[r * CH + i].astype(F32) for i in range(CH)]
        ms = [v[:, DL : DL + 1] + v[:, DL + 1 : DL + 2] + v[:, DL + 2 : DL + 3] for v in x]
        ls = [v[:, DL + 3 : DL + 4] + v[:, DL + 4 : DL + 5] + v[:, DL + 5 : DL + 6] for v in x]
        m = functools.reduce(jnp.maximum, ms)
        ws = [jnp.exp2((v - m) * EXPO) for v in ms]
        total = sum(w * l for w, l in zip(ws, ls))
        o = sum(w * v[:, :DL] for w, v in zip(ws, x))
        rows.append((o / total).astype(BF).astype(F32))
    x = jnp.swapaxes(jnp.stack(rows), 0, 1).astype(BF)
    fetch.wait()
    ys = [jnp.dot(x[h], wbuf[h], preferred_element_type=F32) for h in range(HB)]
    out[...] = jnp.swapaxes(jnp.stack(ys), 0, 1).astype(BF)


def place_kernel(dims, assign, got, out):
    R, J, T, HC, HS, HB, CH = dims
    for chip in range(CH):
        jt, s = divmod(chip, HS)
        j, t = divmod(jt, T)
        for c in range(2):
            for r in range(R):
                out[t, assign[r * J + j], pl.ds(c * HC + s * HB, HB), :] = got[chip * 2 + c, r]


def body(
    q_nope, q_rope, w_uk, w_uv, latent_cache, rope_cache, positions,
    new_latent, new_rope, new_pos, lengths, assignment,
):
    T, REQS, HL, _ = q_nope.shape
    DL, DV = w_uk.shape[2], w_uv.shape[2]
    J, CAP = latent_cache.shape[:2]
    R, CH = lax.axis_size("req"), lax.axis_size("chip")
    HC = HL // 2
    HS = CH // (J * T)
    HB = HC // HS
    W = DL + LANES
    rates = turn_rates(DR)
    rate_row = jnp.asarray(np.tile(np.concatenate([rates, rates])[None], (R * J * T, 1)))
    rate_col = jnp.asarray(rates[:, None])
    big = pltpu.CompilerParams(vmem_limit_bytes=56 << 20)

    blocks = pl.pallas_call(
        functools.partial(absorb_kernel, (R, J, T, HC, DL)),
        out_shape=[jax.ShapeDtypeStruct((J, T, HC, W), BF)] * R,
        in_specs=[SMEM, SMEM, VMEM, VMEM, VMEM, ANY],
        out_specs=[VMEM] * R,
        scratch_shapes=[pltpu.VMEM((HC, DN, DL), BF), pltpu.SemaphoreType.DMA((4,))],
        compiler_params=big,
        name="absorb",
    )(assignment, new_pos, q_nope, q_rope, rate_row, w_uk)
    arrived = [blocks[0]] + [
        lax.ppermute(blocks[k], "req", [(i, i ^ k) for i in range(R)]) for k in range(1, R)
    ]
    own = jnp.stack(arrived)
    other = lax.ppermute(own, "core", [(0, 1), (1, 0)])

    KB = CAP // 3
    keys = pl.pallas_call(
        functools.partial(rope_kernel, (J, CAP), KB),
        out_shape=jax.ShapeDtypeStruct((J, LANES, CAP), BF),
        grid=(3,),
        in_specs=[
            SMEM,
            SMEM,
            pl.BlockSpec((J, KB), lambda i: (0, i)),
            pl.BlockSpec((J, DR, KB), lambda i: (0, 0, i)),
            pl.BlockSpec((DR // 2, 1), lambda i: (0, 0)),
        ],
        out_specs=pl.BlockSpec((J, LANES, KB), lambda i: (0, 0, i)),
        compiler_params=big,
        name="rope",
    )(assignment, lengths, positions, jnp.swapaxes(rope_cache, 1, 2), rate_col)

    B = 1024
    NQ = T * R * HL
    send, keep = pl.pallas_call(
        functools.partial(attend_kernel, (R, J, T, HC, DL, CAP), B),
        out_shape=[
            jax.ShapeDtypeStruct((J, T, R, HC, W), BF),
            jax.ShapeDtypeStruct((J, T, R, HC, W), F32),
        ],
        in_specs=[SMEM, SMEM, VMEM, VMEM, VMEM, VMEM, VMEM, VMEM, ANY],
        out_specs=[VMEM, VMEM],
        scratch_shapes=[
            pltpu.VMEM((J, NQ, W), BF),
            pltpu.VMEM((J, CAP, DL), BF),
            pltpu.VMEM((2, NQ, B), F32),
            pltpu.VMEM((NQ, DL), F32),
            pltpu.SemaphoreType.DMA((J, CAP // B)),
        ],
        compiler_params=big,
        name="attend",
    )(assignment, new_pos, own, other, keys, new_latent, new_rope, rate_row, latent_cache)
    got = lax.ppermute(send, "core", [(0, 1), (1, 0)])
    paired = pl.pallas_call(
        functools.partial(pair_kernel, (R, J, T, HC, HS, CH, DL)),
        out_shape=jax.ShapeDtypeStruct((R * CH, HB, W), BF),
        in_specs=[VMEM, VMEM],
        out_specs=VMEM,
        compiler_params=big,
        name="pair",
    )(keep, got)
    shares = lax.all_to_all(paired, ("req", "chip"), 0, 0)
    values = pl.pallas_call(
        functools.partial(value_kernel, (R, CH, HC, HS, HB, DL, DV, J * T)),
        out_shape=jax.ShapeDtypeStruct((R, HB, DV), BF),
        in_specs=[VMEM, ANY],
        out_specs=VMEM,
        scratch_shapes=[pltpu.VMEM((HB, DL, DV), BF), pltpu.SemaphoreType.DMA],
        compiler_params=big,
        name="value",
    )(shares, w_uv)
    gathered = lax.all_gather(values, ("chip", "core"))
    return pl.pallas_call(
        functools.partial(place_kernel, (R, J, T, HC, HS, HB, CH)),
        out_shape=jax.ShapeDtypeStruct((T, REQS, HL, DV), BF),
        in_specs=[SMEM, VMEM],
        out_specs=VMEM,
        compiler_params=big,
        name="place",
    )(assignment, gathered)


def solution(mesh):
    groups, shards = mesh.shape["req"], mesh.shape["seq"]
    cut = Mesh(mesh.devices.reshape(groups, shards // 2, 2), ("req", "chip", "core"))
    seq = ("chip", "core")
    in_specs = (
        P(None, None, "req", None),
        P(None, None, "req", None),
        P("req", None, None),
        P("req", None, None),
        P("req", seq, None),
        P("req", seq, None),
        P("req", seq),
        P(),
        P(),
        P(),
        P(),
        P(),
    )
    out_specs = P(None, None, "req", None)
    return jax.shard_map(body, mesh=cut, in_specs=in_specs, out_specs=out_specs, check_vma=False)
```

time: 1340 us -> 78.9 us (0.06)
  other arithmetic: 762 us -> 0.94 us
  local copies, waits for them, and re-layouts: 423 us -> 1.43 us
  matrix products: 64 us -> 0 us
  Pallas kernels: 0 us -> 33.7 us
  starting transfers between devices: 28.9 us -> 6.28 us
  between operations: 14.1 us -> 0.06 us
    unnamed x8 -> x0, other arithmetic: 718 us -> none
    unnamed x25 -> x6, local copies, waits for them, and re-layouts: 180 us -> 1.43 us
    all_to_all x18 -> x0, local copies, waits for them, and re-layouts: 127 us -> none  [the longest x6 123 us: run_steps(): lax.all_to_all(attended.reshape(block_steps, per_group, head_total * lat_...]
    reshape x8 -> x0, local copies, waits for them, and re-layouts: 102 us -> none  [the longest x4 101 us: run_steps(): attended.reshape(block_steps, per_group, head_total * lat_width)]
    dot_general x15 -> x0, matrix products: 64 us -> none  [the longest x2 28.4 us: attend(): jnp.einsum('sghl,gcl->sghc', lat_query, latent_cache, preferred_element_t...]
    pallas_call x0 -> x6, Pallas kernels: none -> 33.7 us  [the longest x1 15.8 us: body(): pl.pallas_call(functools.partial(attend_kernel, (R, J, T, HC, DL, CAP), B...]
    all_to_all x6 -> x0, starting transfers between devices: 28.6 us -> none  [the longest x2 11.4 us: run_steps(): lax.all_to_all(rope_block.reshape(block_steps, request_count, heads_local...]
    all_gather x4 -> x1, blocking collectives: 34.2 us -> 9.97 us  [body(): gathered = lax.all_gather(values, ('chip', 'core'))]
  transfers between devices with their start and end apart: 8 -> 5, of which waited for: 3 -> 3; matrix products, arithmetic and copies ran while one was open for 81% -> 0% of each run, Pallas kernels for 0% -> 7%
where the time goes in v1:
time: 78.9 us; the launch traced here: 78.4 us
  Pallas kernels  33.7 us (43%)
  blocking collectives  27.7 us (35%)
  waiting for transfers between devices  8.28 us (10%)
  starting transfers between devices  6.28 us (8%)
  local copies, waits for them, and re-layouts  1.43 us (2%)
  other arithmetic  0.94 us (1%)
    all_to_all x1, blocking collectives, body(): shares = lax.all_to_all(paired, ('req', 'chip'), 0, 0)  17.7 us
    pallas_call x1, Pallas kernels, body(): pl.pallas_call(functools.partial(attend_kernel, (R, J, T, HC, DL, CAP), B...  15.8 us
    all_gather x1, blocking collectives, body(): gathered = lax.all_gather(values, ('chip', 'core'))  9.97 us
    ppermute x3, waiting for transfers between devices, body(): lax.ppermute(blocks[k], 'req', [(i, i ^ k) for i in range(R)])  6.81 us
    pallas_call x1, Pallas kernels, body(): pl.pallas_call(functools.partial(rope_kernel, (J, CAP), KB), out_shape=ja...  5.71 us
    ppermute x3, starting transfers between devices, body(): lax.ppermute(blocks[k], 'req', [(i, i ^ k) for i in range(R)])  5.68 us
    pallas_call x1, Pallas kernels, body(): pl.pallas_call(functools.partial(value_kernel, (R, CH, HC, HS, HB, DL, DV...  3.58 us
    pallas_call x1, Pallas kernels, body(): pl.pallas_call(functools.partial(absorb_kernel, (R, J, T, HC, DL)), out_s...  3.58 us
  transfers between devices with their start and end apart: 5, of which 3 were waited for; matrix products, arithmetic and copies ran while one was open for 0% of the time, Pallas kernels for 7%

profile of v1, /device:TPU:0, one launch (start us, length us, event | category | flops | bytes accessed | tf_op | source)
XLA Modules:
  0.0 78.4 jit_solution(16201447835293800637)
XLA Ops:
  0.0 3.6 %absorb.1 = (bf16[2,2,16,640]{3,2,1,0:T(8,128)(2,1)}, bf16[2,2,16,640]{3,2,1,0:T(8,128)(2,1)}, bf16[2,2,16,640]{3,2,1,0:T(8,128)(2,1)}, bf16[2,2,16,640]{3,2,1,0:T(8,128)(2,1)}) custom-call(s32[8]{0:T(128)} %assign.7, s32[8]{0:T(128)} %new_pos.3, bf16[2,8,32,128]{3,2,1,0:T(8,128)(2,1)} %qn.1, bf16[2,8,32,64]{3,2,1,0:T(8,128)(2,1)} %qr.1, ...), custom_call_target="tpu_custom_call" | custom-call | tf_op jit(solution)/shard_map/absorb/pallas_call | solution.py:283
  3.6 3.1 %collective-permute-start = (bf16[2,2,16,640]{3,2,1,0:T(8,128)(2,1)}, bf16[2,2,16,640]{3,2,1,0:T(8,128)(2,1)S(1)}, u32[]{:S(2)}, u32[]{:S(2)}) collective-permute-start(bf16[2,2,16,640]{3,2,1,0:T(8,128)(2,1)} %get-tuple-element.12), channel_id=1, source_target_pairs={{0,8},{8,0},{16,24},{24,16},{1,9},{9,1},{17,25},{25,17},{2,10},{10... | collective-permute-start | bytes 245768 | tf_op jit(solution)/shard_map/ppermute | solution.py:293
  6.7 2.6 %collective-permute-start.1 = (bf16[2,2,16,640]{3,2,1,0:T(8,128)(2,1)}, bf16[2,2,16,640]{3,2,1,0:T(8,128)(2,1)S(1)}, u32[]{:S(2)}, u32[]{:S(2)}) collective-permute-start(bf16[2,2,16,640]{3,2,1,0:T(8,128)(2,1)} %get-tuple-element.13), channel_id=1, source_target_pairs={{0,16},{8,24},{16,0},{24,8},{1,17},{9,25},{17,1},{25,9},{2,18},{10... | collective-permute-start | bytes 245768 | tf_op jit(solution)/shard_map/ppermute | solution.py:293
  9.3 0.0 collective-permute-start.2
  9.3 0.1 collective-permute-done
  9.3 6.7 %collective-permute-done.1 = bf16[2,2,16,640]{3,2,1,0:T(8,128)(2,1)S(1)} collective-permute-done((bf16[2,2,16,640]{3,2,1,0:T(8,128)(2,1)}, bf16[2,2,16,640]{3,2,1,0:T(8,128)(2,1)S(1)}, u32[]{:S(2)}, u32[]{:S(2)}) %collective-permute-start.1) | collective-permute-done | bytes 81952 | tf_op jit(solution)/shard_map/ppermute | solution.py:293
  16.1 0.0 collective-permute-done.2
  16.1 0.9 %pad_maximum_fusion.own = bf16[4,2,2,16,640]{4,3,2,1,0:T(8,128)(2,1)S(1)} fusion(bf16[1,2,2,16,640]{4,3,2,1,0:T(8,128)(2,1)S(1)} %bitcast.11, bf16[1,2,2,16,640]{4,3,2,1,0:T(8,128)(2,1)S(1)} %bitcast.10, bf16[1,2,2,16,640]{4,3,2,1,0:T(8,128)(2,1)S(1)} %bitcast.9, bf16[1,2,2,16,640]{4,3,2,1,0:T(8,128)(2,1)} %bitcast.8), kind=kLoop, calls=%fused_computation | loop fusion | flops 491520 | bytes 655360 | tf_op jit(solution)/shard_map/stack | solution.py:295
  17.0 0.0 copy-start
  17.0 0.1 collective-permute-start.3
  17.1 5.7 %rope.1.keys = bf16[2,128,6144]{2,1,0:T(8,128)(2,1)} custom-call(s32[8]{0:T(128)} %assign.7, s32[8]{0:T(128)} %lengths.1, s32[2,6144]{1,0:T(2,128)} %pos.1, bf16[2,64,6144]{2,1,0:T(8,128)(2,1)} %bitcast.6, s32[32,1]{1,0:T(8,128)} %constant.5.clone.rate), custom_call_target="tpu_custom_call" | custom-call | tf_op jit(solution)/shard_map/rope/pallas_call | solution.py:299
  22.8 0.0 collective-permute-done.3.other
  22.8 0.0 copy-done
  22.8 0.0 copy-start.2
  22.8 0.7 copy-done.2
  23.6 15.8 %attend.1 = (bf16[2,2,4,16,640]{4,3,2,1,0:T(8,128)(2,1)}, f32[2,2,4,16,640]{4,3,2,1,0:T(8,128)}) custom-call(s32[8]{0:T(128)} %assign.7, s32[8]{0:T(128)} %new_pos.3, bf16[4,2,2,16,640]{4,3,2,1,0:T(8,128)(2,1)} %copy-done, bf16[4,2,2,16,640]{4,3,2,1,0:T(8,128)(2,1)} %copy-done.2, bf16[2,128,6144]{2,1,0:T(8,128)(2,1)} %rope.1.keys, ...), custom_call_target="tpu_custom_call" | custom-call | tf_op jit(solution)/shard_map/attend/pallas_call | solution.py:317
  39.3 0.5 collective-permute-start.4
  39.9 1.5 %collective-permute-done.4.got = bf16[2,2,4,16,640]{4,3,2,1,0:T(8,128)(2,1)S(1)} collective-permute-done((bf16[2,2,4,16,640]{4,3,2,1,0:T(8,128)(2,1)}, bf16[2,2,4,16,640]{4,3,2,1,0:T(8,128)(2,1)S(1)}, u32[]{:S(2)}, u32[]{:S(2)}) %collective-permute-start.4) | collective-permute-done | bytes 327712 | tf_op jit(solution)/shard_map/ppermute | solution.py:335
  41.3 0.0 copy-start.1
  41.3 0.7 copy-done.1
  42.0 3.5 %pair.1 = bf16[16,16,640]{2,1,0:T(8,128)(2,1)} custom-call(f32[2,2,4,16,640]{4,3,2,1,0:T(8,128)} %get-tuple-element.15.keep, bf16[2,2,4,16,640]{4,3,2,1,0:T(8,128)(2,1)} %copy-done.1), custom_call_target="tpu_custom_call" | custom-call | tf_op jit(solution)/shard_map/pair/pallas_call | solution.py:336
  45.5 17.7 %all_to_all.5.got = bf16[16,16,640]{2,1,0:T(8,128)(2,1)} all-to-all(bf16[16,16,640]{2,1,0:T(8,128)(2,1)} %pair.1), channel_id=1, replica_groups=mesh['req'=4,'chip'=4,'core'=2] {'req','chip'}, dimensions={0} | all-to-all | bytes 655360 | tf_op jit(solution)/shard_map/all_to_all | solution.py:344
  63.2 3.6 %value.1 = bf16[4,16,128]{2,1,0:T(8,128)(2,1)} custom-call(bf16[16,16,640]{2,1,0:T(8,128)(2,1)} %all_to_all.5.got, bf16[32,512,128]{2,1,0:T(8,128)(2,1)} %w_hbm.3), custom_call_target="tpu_custom_call" | custom-call | tf_op jit(solution)/shard_map/value/pallas_call | solution.py:345
  66.8 10.0 %all-gather = bf16[32,16,128]{2,1,0:T(8,128)(2,1)} all-gather(bf16[4,16,128]{2,1,0:T(8,128)(2,1)} %value.1), channel_id=2, replica_groups=mesh['req'=4,'chip'=4,'core'=2] {'chip','core'}, dimensions={0}, use_global_device_ids=true | all-gather | bytes 147456 | tf_op jit(solution)/shard_map/all_gather | solution.py:354
  76.8 1.6 %place.1 = bf16[2,8,32,128]{3,2,1,0:T(8,128)(2,1)} custom-call(s32[8]{0:T(128)} %assign.7, bf16[8,4,16,128]{3,2,1,0:T(8,128)(2,1)} %bitcast.7), custom_call_target="tpu_custom_call" | custom-call | tf_op jit(solution)/shard_map/place/pallas_call | solution.py:355
Async XLA Ops:
  3.6 5.7 %collective-permute-start = (bf16[2,2,16,640]{3,2,1,0:T(8,128)(2,1)}, bf16[2,2,16,640]{3,2,1,0:T(8,128)(2,1)S(1)}, u32[]{:S(2)}, u32[]{:S(2)}) collective-permute-start(bf16[2,2,16,640]{3,2,1,0:T(8,128)(2,1)} %get-tuple-element.12), channel_id=1, source_target_pairs={{0,8},{8,0},{16,24},{24,16},{1,9},{9,1},{17,25},{25,17},{2,10},{10... | collective-permute-start | bytes 245768 | tf_op jit(solution)/shard_map/ppermute | solution.py:293
  6.7 9.4 %collective-permute-start.1 = (bf16[2,2,16,640]{3,2,1,0:T(8,128)(2,1)}, bf16[2,2,16,640]{3,2,1,0:T(8,128)(2,1)S(1)}, u32[]{:S(2)}, u32[]{:S(2)}) collective-permute-start(bf16[2,2,16,640]{3,2,1,0:T(8,128)(2,1)} %get-tuple-element.13), channel_id=1, source_target_pairs={{0,16},{8,24},{16,0},{24,8},{1,17},{9,25},{17,1},{25,9},{2,18},{10... | collective-permute-start | bytes 245768 | tf_op jit(solution)/shard_map/ppermute | solution.py:293
  9.3 6.8 %collective-permute-start.2 = (bf16[2,2,16,640]{3,2,1,0:T(8,128)(2,1)}, bf16[2,2,16,640]{3,2,1,0:T(8,128)(2,1)S(1)}, u32[]{:S(2)}, u32[]{:S(2)}) collective-permute-start(bf16[2,2,16,640]{3,2,1,0:T(8,128)(2,1)} %get-tuple-element.14), channel_id=1, source_target_pairs={{0,24},{8,16},{16,8},{24,0},{1,25},{9,17},{17,9},{25,1},{2,26},{10... | collective-permute-start | bytes 245768 | tf_op jit(solution)/shard_map/ppermute | solution.py:293
  17.0 5.8 %copy-start = (bf16[4,2,2,16,640]{4,3,2,1,0:T(8,128)(2,1)}, bf16[4,2,2,16,640]{4,3,2,1,0:T(8,128)(2,1)S(1)}, u32[]{:S(2)}) copy-start(bf16[4,2,2,16,640]{4,3,2,1,0:T(8,128)(2,1)S(1)} %pad_maximum_fusion.own) | copy-start | bytes 983044
  17.0 5.8 %collective-permute-start.3 = (bf16[4,2,2,16,640]{4,3,2,1,0:T(8,128)(2,1)S(1)}, bf16[4,2,2,16,640]{4,3,2,1,0:T(8,128)(2,1)S(1)}, u32[]{:S(2)}, u32[]{:S(2)}) collective-permute-start(bf16[4,2,2,16,640]{4,3,2,1,0:T(8,128)(2,1)S(1)} %pad_maximum_fusion.own), channel_id=1, source_target_pairs={{0,1},{1,0},{2,3},{3,2},{4,5},{5,4},{6,7},{7,6},{8,9},{9,8},{10,11... | collective-permute-start | bytes 983048 | tf_op jit(solution)/shard_map/ppermute | solution.py:296
  22.8 0.7 copy-start.2
  39.3 2.0 %collective-permute-start.4 = (bf16[2,2,4,16,640]{4,3,2,1,0:T(8,128)(2,1)}, bf16[2,2,4,16,640]{4,3,2,1,0:T(8,128)(2,1)S(1)}, u32[]{:S(2)}, u32[]{:S(2)}) collective-permute-start(bf16[2,2,4,16,640]{4,3,2,1,0:T(8,128)(2,1)} %get-tuple-element.16), channel_id=1, source_target_pairs={{0,1},{1,0},{2,3},{3,2},{4,5},{5,4},{6,7},{7,6},{8,9},{9,8},{10,11... | collective-permute-start | bytes 983048 | tf_op jit(solution)/shard_map/ppermute | solution.py:335
  41.3 0.7 copy-start.1

commit v2 on v1

--- a/solution.py
+++ b/solution.py
@@ -15,11 +15,17 @@
 LANES = 128
 LOW = -1e30
 EXPO = math.log2(math.e) / math.sqrt(DN + DR)
+KEYS = 80
 BF = jnp.bfloat16
 F32 = jnp.float32
 VMEM = pl.BlockSpec(memory_space=pltpu.VMEM)
 SMEM = pl.BlockSpec(memory_space=pltpu.SMEM)
 ANY = pl.BlockSpec(memory_space=pl.ANY)
+HBM = pl.BlockSpec(memory_space=pltpu.HBM)
+
+
+def in_hbm(x):
+    return pltpu.with_memory_space_constraint(x, pltpu.HBM)
 
 
 def turn_rates(width):
@@ -100,45 +106,56 @@
         outs[k][j, t, :, :DL] = y[i]
 
 
-def rope_kernel(dims, block, assign, lengths, pos, rope, rate, out):
+def prepare_kernel(dims, cuts, assign, lengths, pos, rope, rate, c_hbm, out, c_out, sem):
     J, CAP = dims
     g = lax.axis_index("req")
     shard = lax.axis_index("chip") * lax.axis_size("core") + lax.axis_index("core")
     half = DR // 2
-    first = shard * CAP + pl.program_id(0) * block
-    where_row = first + lax.broadcasted_iota(jnp.int32, (1, block), 1)
-    sub = lax.broadcasted_iota(jnp.int32, (LANES - DR, block), 0)
+    block = CAP // cuts
+    copies = []
     for j in range(J):
-        sine, cosine = sin_cos(pos[j : j + 1, :] * rate[...])
-        a = rope[j, :half, :].astype(F32)
-        b = rope[j, half:, :].astype(F32)
-        out[j, :half, :] = (a * cosine - b * sine).astype(BF)
-        out[j, half:DR, :] = (b * cosine + a * sine).astype(BF)
-        bad = where_row >= lengths[assign[g * J + j]]
-        out[j, DR:, :] = jnp.where((sub == 0) & bad, LOW, 0.0).astype(BF)
+        for i in range(cuts):
+            rows = pl.ds(i * block, block)
+            copies.append(
+                pltpu.make_async_copy(c_hbm.at[j, rows], c_out.at[j, rows], sem.at[j, i])
+            )
+            copies[-1].start()
+    sub = lax.broadcasted_iota(jnp.int32, (KEYS - DR, block), 0)
+    turn = rate[...]
+    for j in range(J):
+        end = lengths[assign[g * J + j]] - shard * CAP
+
+        def rotate(i, carry):
+            at = pl.ds(pl.multiple_of(i * block, LANES), block)
+            sine, cosine = sin_cos(pos[j : j + 1, at] * turn)
+            a = rope[j, :half, at].astype(F32)
+            b = rope[j, half:, at].astype(F32)
+            out[j, :half, at] = (a * cosine - b * sine).astype(BF)
+            out[j, half:DR, at] = (b * cosine + a * sine).astype(BF)
+            bad = i * block + lax.broadcasted_iota(jnp.int32, (1, block), 1) >= end
+            out[j, DR:, at] = jnp.where((sub == 0) & bad, LOW, 0.0).astype(BF)
+            return carry
+
+        lax.fori_loop(0, cuts, rotate, 0)
+    for copy in copies:
+        copy.wait()
 
 
 def attend_kernel(
-    dims, B, assign, new_pos, own, other, keys, new_lat, new_rope, rate, c_hbm,
-    send, keep, q, cbuf, sbuf, acc, csem,
+    dims, B, assign, new_pos, new_lat, new_rope, rate, keys, cbuf, *rest
 ):
     R, J, T, HC, DL, CAP = dims
+    own, other = rest[:R], rest[R : 2 * R]
+    send, keep, q, sbuf, acc = rest[2 * R :]
     nb = CAP // B
     NQ = T * R * 2 * HC
     g, c = lax.axis_index("req"), lax.axis_index("core")
     first_shard = (lax.axis_index("chip") == 0) & (c == 0)
 
-    def fetch(j, i):
-        rows = pl.ds(i * B, B)
-        return pltpu.make_async_copy(c_hbm.at[j, rows], cbuf.at[j, rows], csem.at[j, i])
-
-    for j in range(J):
-        for i in range(nb):
-            fetch(j, i).start()
     for j in range(J):
         for t in range(T):
             for k in range(R):
-                mine, theirs = own[k, j, t], other[k, j, t]
+                mine, theirs = own[k][j, t], other[k][j, t]
                 base = (t * R + k) * 2 * HC
                 q[j, base : base + HC, :] = jnp.where(c == 0, mine, theirs)
                 q[j, base + HC : base + 2 * HC, :] = jnp.where(c == 0, theirs, mine)
@@ -148,11 +165,12 @@
         rows = pl.ds(i * B, B)
         return lax.dot_general(
             q[j, :, :DL], cbuf[j, rows], nt, preferred_element_type=F32
-        ) + jnp.dot(q[j, :, DL:], keys[j, :, rows], preferred_element_type=F32)
+        ) + jnp.dot(
+            q[j, :, DL : DL + KEYS], keys[j, :, rows], preferred_element_type=F32
+        )
 
     for j in range(J):
         r = assign[g * J + j]
-        fetch(j, 0).wait()
         sbuf[0] = score(j, 0)
         pick = lax.broadcasted_iota(jnp.int32, new_lat.shape[1:], 0) == r
         lat = [
@@ -185,7 +203,6 @@
         acc[...] = jnp.dot(p.astype(BF), lat, preferred_element_type=F32)
         for i in range(nb):
             if i + 1 < nb:
-                fetch(j, i + 1).wait()
                 sbuf[(i + 1) % 2] = score(j, i + 1)
             s = sbuf[i % 2]
             top = jnp.maximum(m, jnp.max(s, axis=1, keepdims=True))
@@ -208,48 +225,49 @@
                 send[j, t, k, :, DL:] = jnp.where(c == 0, parts[hi], parts[lo]).astype(BF)
 
 
+def stats_of(x, DL):
+    m = x[:, DL : DL + 1] + x[:, DL + 1 : DL + 2] + x[:, DL + 2 : DL + 3]
+    return m, x[:, DL + 3 : DL + 4] + x[:, DL + 4 : DL + 5] + x[:, DL + 5 : DL + 6]
+
+
 def pair_kernel(dims, keep, got, out):
     R, J, T, HC, HS, CH, DL = dims
     g = lax.axis_index("req")
     HB = HC // HS
     for j in range(J):
         for t in range(T):
+            a = jnp.concatenate([keep[j, t, k] for k in range(R)], axis=0)
+            b = jnp.concatenate([got[j, t, k] for k in range(R)], axis=0).astype(F32)
+            ma, la = a[:, DL : DL + 1], a[:, DL + 1 : DL + 2]
+            mb, lb = stats_of(b[:, :], DL)
+            m = jnp.maximum(ma, mb)
+            wa, wb = jnp.exp2((ma - m) * EXPO), jnp.exp2((mb - m) * EXPO)
+            o = (a[:, :DL] * wa + b[:, :DL] * wb).astype(BF)
+            st = stat_lanes(R * HC, split3(m) + split3(la * wa + lb * wb)).astype(BF)
             for k in range(R):
-                a = keep[j, t, k]
-                b = got[j, t, k].astype(F32)
-                ma, la = a[:, DL : DL + 1], a[:, DL + 1 : DL + 2]
-                mb = b[:, DL : DL + 1] + b[:, DL + 1 : DL + 2] + b[:, DL + 2 : DL + 3]
-                lb = b[:, DL + 3 : DL + 4] + b[:, DL + 4 : DL + 5] + b[:, DL + 5 : DL + 6]
-                m = jnp.maximum(ma, mb)
-                wa, wb = jnp.exp2((ma - m) * EXPO), jnp.exp2((mb - m) * EXPO)
-                o = (a[:, :DL] * wa + b[:, :DL] * wb).astype(BF)
-                st = stat_lanes(HC, split3(m) + split3(la * wa + lb * wb)).astype(BF)
                 for s in range(HS):
                     at = (g ^ k) * CH + (j * T + t) * HS + s
-                    out[at, :, :DL] = o[s * HB : (s + 1) * HB]
-                    out[at, :, DL:] = st[s * HB : (s + 1) * HB]
-
-
-def value_kernel(dims, got, w_hbm, out, wbuf, sem):
+                    rows = slice(k * HC + s * HB, k * HC + (s + 1) * HB)
+                    out[at, :, :DL] = o[rows]
+                    out[at, :, DL:] = st[rows]
+
+
+def value_kernel(dims, got, w, out):
     R, CH, HC, HS, HB, DL, DV, JT = dims
     c = lax.axis_index("core")
     part = lax.rem(lax.axis_index("chip"), HS)
     first = c * HC + part * HB
-    fetch = pltpu.make_async_copy(w_hbm.at[pl.ds(first, HB)], wbuf, sem)
-    fetch.start()
-    rows = []
-    for r in range(R):
-        x = [got[r * CH + i].astype(F32) for i in range(CH)]
-        ms = [v[:, DL : DL + 1] + v[:, DL + 1 : DL + 2] + v[:, DL + 2 : DL + 3] for v in x]
-        ls = [v[:, DL + 3 : DL + 4] + v[:, DL + 4 : DL + 5] + v[:, DL + 5 : DL + 6] for v in x]
-        m = functools.reduce(jnp.maximum, ms)
-        ws = [jnp.exp2((v - m) * EXPO) for v in ms]
-        total = sum(w * l for w, l in zip(ws, ls))
-        o = sum(w * v[:, :DL] for w, v in zip(ws, x))
-        rows.append((o / total).astype(BF).astype(F32))
-    x = jnp.swapaxes(jnp.stack(rows), 0, 1).astype(BF)
-    fetch.wait()
-    ys = [jnp.dot(x[h], wbuf[h], preferred_element_type=F32) for h in range(HB)]
+    x = [
+        jnp.concatenate([got[r * CH + i] for r in range(R)], axis=0).astype(F32) for i in range(CH)
+    ]
+    ms, ls = zip(*[stats_of(v, DL) for v in x])
+    m = functools.reduce(jnp.maximum, ms)
+    ws = [jnp.exp2((v - m) * EXPO) for v in ms]
+    total = sum(w_ * l for w_, l in zip(ws, ls))
+    o = sum(w_ * v[:, :DL] for w_, v in zip(ws, x)) / total
+    o = o.astype(BF).astype(F32).reshape(R, HB, DL)
+    x = jnp.swapaxes(o, 0, 1).astype(BF)
+    ys = [jnp.dot(x[h], w[first + h], preferred_element_type=F32) for h in range(HB)]
     out[...] = jnp.swapaxes(jnp.stack(ys), 0, 1).astype(BF)
 
 
@@ -278,39 +296,40 @@
     rates = turn_rates(DR)
     rate_row = jnp.asarray(np.tile(np.concatenate([rates, rates])[None], (R * J * T, 1)))
     rate_col = jnp.asarray(rates[:, None])
-    big = pltpu.CompilerParams(vmem_limit_bytes=56 << 20)
+    assignment, new_pos, lengths = in_hbm(assignment), in_hbm(new_pos), in_hbm(lengths)
+    big = pltpu.CompilerParams(vmem_limit_bytes=8 << 20)
 
     blocks = pl.pallas_call(
         functools.partial(absorb_kernel, (R, J, T, HC, DL)),
         out_shape=[jax.ShapeDtypeStruct((J, T, HC, W), BF)] * R,
-        in_specs=[SMEM, SMEM, VMEM, VMEM, VMEM, ANY],
+        in_specs=[SMEM, SMEM, VMEM, VMEM, VMEM, HBM],
         out_specs=[VMEM] * R,
         scratch_shapes=[pltpu.VMEM((HC, DN, DL), BF), pltpu.SemaphoreType.DMA((4,))],
         compiler_params=big,
         name="absorb",
-    )(assignment, new_pos, q_nope, q_rope, rate_row, w_uk)
+    )(assignment, new_pos, in_hbm(q_nope), in_hbm(q_rope), in_hbm(rate_row), in_hbm(w_uk))
     arrived = [blocks[0]] + [
         lax.ppermute(blocks[k], "req", [(i, i ^ k) for i in range(R)]) for k in range(1, R)
     ]
-    own = jnp.stack(arrived)
-    other = lax.ppermute(own, "core", [(0, 1), (1, 0)])
-
-    KB = CAP // 3
-    keys = pl.pallas_call(
-        functools.partial(rope_kernel, (J, CAP), KB),
-        out_shape=jax.ShapeDtypeStruct((J, LANES, CAP), BF),
-        grid=(3,),
-        in_specs=[
-            SMEM,
-            SMEM,
-            pl.BlockSpec((J, KB), lambda i: (0, i)),
-            pl.BlockSpec((J, DR, KB), lambda i: (0, 0, i)),
-            pl.BlockSpec((DR // 2, 1), lambda i: (0, 0)),
+    cuts = CAP // 512
+    keys, cached = pl.pallas_call(
+        functools.partial(prepare_kernel, (J, CAP), cuts),
+        out_shape=[
+            jax.ShapeDtypeStruct((J, KEYS, CAP), BF),
+            jax.ShapeDtypeStruct((J, CAP, DL), BF),
         ],
-        out_specs=pl.BlockSpec((J, LANES, KB), lambda i: (0, 0, i)),
-        compiler_params=big,
-        name="rope",
-    )(assignment, lengths, positions, jnp.swapaxes(rope_cache, 1, 2), rate_col)
+        in_specs=[SMEM, SMEM, VMEM, VMEM, VMEM, HBM],
+        out_specs=[VMEM, VMEM],
+        scratch_shapes=[pltpu.SemaphoreType.DMA((J, cuts))],
+        compiler_params=pltpu.CompilerParams(vmem_limit_bytes=8 << 20),
+        cost_estimate=pl.CostEstimate(
+            flops=0, bytes_accessed=4 * J * CAP * DL, transcendentals=0
+        ),
+        name="prepare",
+    )(assignment, lengths, positions, jnp.swapaxes(rope_cache, 1, 2), rate_col, in_hbm(latent_cache))
+
+    own, keys, cached = lax.optimization_barrier((arrived, keys, cached))
+    other = [lax.ppermute(v, "core", [(0, 1), (1, 0)]) for v in own]
 
     B = 1024
     NQ = T * R * HL
@@ -320,18 +339,16 @@
             jax.ShapeDtypeStruct((J, T, R, HC, W), BF),
             jax.ShapeDtypeStruct((J, T, R, HC, W), F32),
         ],
-        in_specs=[SMEM, SMEM, VMEM, VMEM, VMEM, VMEM, VMEM, VMEM, ANY],
+        in_specs=[SMEM, SMEM] + [VMEM] * (5 + 2 * R),
         out_specs=[VMEM, VMEM],
         scratch_shapes=[
             pltpu.VMEM((J, NQ, W), BF),
-            pltpu.VMEM((J, CAP, DL), BF),
             pltpu.VMEM((2, NQ, B), F32),
             pltpu.VMEM((NQ, DL), F32),
-            pltpu.SemaphoreType.DMA((J, CAP // B)),
         ],
-        compiler_params=big,
+        compiler_params=pltpu.CompilerParams(vmem_limit_bytes=16 << 20),
         name="attend",
-    )(assignment, new_pos, own, other, keys, new_latent, new_rope, rate_row, latent_cache)
+    )(assignment, new_pos, new_latent, new_rope, rate_row, keys, cached, *own, *other)
     got = lax.ppermute(send, "core", [(0, 1), (1, 0)])
     paired = pl.pallas_call(
         functools.partial(pair_kernel, (R, J, T, HC, HS, CH, DL)),
@@ -345,9 +362,8 @@
     values = pl.pallas_call(
         functools.partial(value_kernel, (R, CH, HC, HS, HB, DL, DV, J * T)),
         out_shape=jax.ShapeDtypeStruct((R, HB, DV), BF),
-        in_specs=[VMEM, ANY],
+        in_specs=[VMEM, VMEM],
         out_specs=VMEM,
-        scratch_shapes=[pltpu.VMEM((HB, DL, DV), BF), pltpu.SemaphoreType.DMA],
         compiler_params=big,
         name="value",
     )(shares, w_uv)

time: 78.9 us -> 59.3 us (0.75)
  Pallas kernels: 33.7 us -> 22.3 us
  waiting for transfers between devices: 8.28 us -> 3.14 us
  local copies, waits for them, and re-layouts: 1.43 us -> 0.03 us
  blocking collectives: 27.7 us -> 26.3 us
  other arithmetic: 0.94 us -> 0 us
  starting transfers between devices: 6.28 us -> 7.12 us
    ppermute x3, waiting for transfers between devices: 6.81 us -> 0.94 us  [body(): lax.ppermute(blocks[k], 'req', [(i, i ^ k) for i in range(R)])]
    pallas_call x1, Pallas kernels: 15.8 us -> 10.9 us  [body(): pl.pallas_call(functools.partial(attend_kernel, (R, J, T, HC, DL, CAP), B...]
    pallas_call x1, Pallas kernels: 3.58 us -> 0.65 us  [body(): pl.pallas_call(functools.partial(value_kernel, (R, CH, HC, HS, HB, DL, DV...]
    pallas_call x1, Pallas kernels: 3.49 us -> 0.81 us  [body(): pl.pallas_call(functools.partial(pair_kernel, (R, J, T, HC, HS, CH, DL)),...]
    all_gather x1, blocking collectives: 9.97 us -> 8.49 us  [body(): gathered = lax.all_gather(values, ('chip', 'core'))]
    unnamed x6 -> x14, local copies, waits for them, and re-layouts: 1.43 us -> 0.03 us
    ppermute x1 -> x4, starting transfers between devices: 0.07 us -> 1.02 us  [body(): other = [lax.ppermute(v, 'core', [(0, 1), (1, 0)]) for v in own]]
    another operation x1 -> x0, other arithmetic: 0.94 us -> none  [body(): own = jnp.stack(arrived)]
  transfers between devices with their start and end apart: 5 -> 8, of which waited for: 3 -> 6; matrix products, arithmetic and copies ran while one was open for 0% -> 0% of each run, Pallas kernels for 7% -> 9%
where the time goes in v2:
time: 59.3 us; the launch traced here: 59 us
  blocking collectives  26.3 us (44%)
  Pallas kernels  22.3 us (38%)
  starting transfers between devices  7.12 us (12%)
  waiting for transfers between devices  3.14 us (5%)
    all_to_all x1, blocking collectives, body(): shares = lax.all_to_all(paired, ('req', 'chip'), 0, 0)  17.9 us
    pallas_call x1, Pallas kernels, body(): pl.pallas_call(functools.partial(attend_kernel, (R, J, T, HC, DL, CAP), B...  10.9 us
    all_gather x1, blocking collectives, body(): gathered = lax.all_gather(values, ('chip', 'core'))  8.49 us
    ppermute x3, starting transfers between devices, body(): lax.ppermute(blocks[k], 'req', [(i, i ^ k) for i in range(R)])  5.69 us
    pallas_call x1, Pallas kernels, body(): pl.pallas_call(functools.partial(prepare_kernel, (J, CAP), cuts), out_sha...  5.59 us
    pallas_call x1, Pallas kernels, body(): pl.pallas_call(functools.partial(absorb_kernel, (R, J, T, HC, DL)), out_s...  3.02 us
    pallas_call x1, Pallas kernels, body(): pl.pallas_call(functools.partial(place_kernel, (R, J, T, HC, HS, HB, CH))...  1.34 us
    ppermute x1, waiting for transfers between devices, body(): got = lax.ppermute(send, 'core', [(0, 1), (1, 0)])  1.28 us
  transfers between devices with their start and end apart: 8, of which 6 were waited for; matrix products, arithmetic and copies ran while one was open for 0% of the time, Pallas kernels for 9%

profile of v2, /device:TPU:0, one launch (start us, length us, event | category | flops | bytes accessed | tf_op | source)
XLA Modules:
  0.0 59.0 jit_solution(6833981432878478961)
XLA Ops:
  0.0 0.0 copy-start.5
  0.0 0.0 copy-start.2
  0.0 0.0 copy-start.1
  0.0 3.0 %absorb.1 = (bf16[2,2,16,640]{3,2,1,0:T(8,128)(2,1)S(1)}, bf16[2,2,16,640]{3,2,1,0:T(8,128)(2,1)S(1)}, bf16[2,2,16,640]{3,2,1,0:T(8,128)(2,1)S(1)}, bf16[2,2,16,640]{3,2,1,0:T(8,128)(2,1)S(1)}) custom-call(s32[8]{0:T(128)} %assign.7, s32[8]{0:T(128)} %new_pos.3, bf16[2,8,32,128]{3,2,1,0:T(8,128)(2,1)} %qn.1, bf16[2,8,32,64]{3,2,1,0:T(8,128)(2,1)} %qr.1, ...), custom_call_target="tpu_custom_call" | custom-call | tf_op jit(solution)/shard_map/absorb/pallas_call | solution.py:302
  3.0 3.1 %collective-permute-start = (bf16[2,2,16,640]{3,2,1,0:T(8,128)(2,1)S(1)}, bf16[2,2,16,640]{3,2,1,0:T(8,128)(2,1)S(1)}, u32[]{:S(2)}, u32[]{:S(2)}) collective-permute-start(bf16[2,2,16,640]{3,2,1,0:T(8,128)(2,1)S(1)} %get-tuple-element.20), channel_id=1, source_target_pairs={{0,8},{8,0},{16,24},{24,16},{1,9},{9,1},{17,25},{25,17},{2,10},{10... | collective-permute-start | bytes 245768 | tf_op jit(solution)/shard_map/ppermute | solution.py:312
  6.1 2.6 %collective-permute-start.1 = (bf16[2,2,16,640]{3,2,1,0:T(8,128)(2,1)S(1)}, bf16[2,2,16,640]{3,2,1,0:T(8,128)(2,1)S(1)}, u32[]{:S(2)}, u32[]{:S(2)}) collective-permute-start(bf16[2,2,16,640]{3,2,1,0:T(8,128)(2,1)S(1)} %get-tuple-element.21), channel_id=1, source_target_pairs={{0,16},{8,24},{16,0},{24,8},{1,17},{9,25},{17,1},{25,9},{2,18},{10... | collective-permute-start | bytes 245768 | tf_op jit(solution)/shard_map/ppermute | solution.py:312
  8.7 0.0 collective-permute-start.2
  8.7 0.0 copy-done.5
  8.7 0.0 copy-done.2
  8.7 0.0 copy-done.1
  8.7 0.0 copy-start.3
  8.8 0.0 copy-start.4
  8.8 0.0 copy-start.6
  8.8 5.6 %prepare.1 = (bf16[2,80,6144]{2,1,0:T(8,128)(2,1)S(1)}, bf16[2,6144,512]{2,1,0:T(8,128)(2,1)S(1)}) custom-call(s32[8]{0:T(128)} %assign.7, s32[8]{0:T(128)} %lengths.1, s32[2,6144]{1,0:T(2,128)S(1)} %copy-done.2, bf16[2,64,6144]{2,1,0:T(8,128)(2,1)S(1)} %bitcast.2, s32[32,1]{1,0:T(8,128)S(1)} %copy-done.5, bf16[2,6144,512]{2,1,0:T(8,128)(2,1)} %c_hbm.1), custom_call_target="tpu_custom_call" | custom-call | bytes 25165824 | tf_op jit(solution)/shard_map/prepare/pallas_call | solution.py:315
  14.4 0.0 collective-permute-done.rest_1_
  14.4 0.9 %collective-permute-done.1.rest_2_ = bf16[2,2,16,640]{3,2,1,0:T(8,128)(2,1)S(1)} collective-permute-done((bf16[2,2,16,640]{3,2,1,0:T(8,128)(2,1)S(1)}, bf16[2,2,16,640]{3,2,1,0:T(8,128)(2,1)S(1)}, u32[]{:S(2)}, u32[]{:S(2)}) %collective-permute-start.1) | collective-permute-done | bytes 81952 | tf_op jit(solution)/shard_map/ppermute | solution.py:312
  15.3 0.0 collective-permute-done.2.rest_3_
  15.3 0.0 collective-permute-start.3
  15.3 0.5 collective-permute-start.4
  15.8 0.0 collective-permute-start.5
  15.8 0.5 collective-permute-start.6
  16.3 0.3 collective-permute-done.3.rest_4_
  16.6 0.2 collective-permute-done.4.rest_5_
  16.8 0.4 collective-permute-done.5.rest_6_
  17.1 0.2 collective-permute-done.6.rest_7_
  17.3 0.0 copy-done.3
  17.3 0.0 copy-done.4
  17.3 0.0 copy-done.6
  17.3 0.0 copy-start
  17.3 10.9 %attend.1 = (bf16[2,2,4,16,640]{4,3,2,1,0:T(8,128)(2,1)S(1)}, f32[2,2,4,16,640]{4,3,2,1,0:T(8,128)S(1)}) custom-call(s32[8]{0:T(128)} %assign.7, s32[8]{0:T(128)} %new_pos.3, bf16[2,8,512]{2,1,0:T(8,128)(2,1)S(1)} %copy-done.4, bf16[2,8,64]{2,1,0:T(8,128)(2,1)S(1)} %copy-done.6, s32[16,64]{1,0:T(8,128)S(1)} %copy-done.3, ...), custom_call_target="tpu_custom_call" | custom-call | tf_op jit(solution)/shard_map/attend/pallas_call | solution.py:336
  28.2 0.4 collective-permute-start.7
  28.6 1.3 %collective-permute-done.7.got = bf16[2,2,4,16,640]{4,3,2,1,0:T(8,128)(2,1)S(1)} collective-permute-done((bf16[2,2,4,16,640]{4,3,2,1,0:T(8,128)(2,1)S(1)}, bf16[2,2,4,16,640]{4,3,2,1,0:T(8,128)(2,1)S(1)}, u32[]{:S(2)}, u32[]{:S(2)}) %collective-permute-start.7) | collective-permute-done | bytes 327712 | tf_op jit(solution)/shard_map/ppermute | solution.py:352
  29.9 0.8 %pair.1 = bf16[16,16,640]{2,1,0:T(8,128)(2,1)S(1)} custom-call(f32[2,2,4,16,640]{4,3,2,1,0:T(8,128)S(1)} %get-tuple-element.31.keep, bf16[2,2,4,16,640]{4,3,2,1,0:T(8,128)(2,1)S(1)} %collective-permute-done.7.got), custom_call_target="tpu_custom_call" | custom-call | tf_op jit(solution)/shard_map/pair/pallas_call | solution.py:353
  30.7 17.9 %all_to_all.5.got = bf16[16,16,640]{2,1,0:T(8,128)(2,1)S(1)} all-to-all(bf16[16,16,640]{2,1,0:T(8,128)(2,1)S(1)} %pair.1), channel_id=1, replica_groups=mesh['req'=4,'chip'=4,'core'=2] {'req','chip'}, dimensions={0} | all-to-all | bytes 655360 | tf_op jit(solution)/shard_map/all_to_all | solution.py:361
  48.5 0.0 copy-done
  48.5 0.7 %value.1 = bf16[4,16,128]{2,1,0:T(8,128)(2,1)S(1)} custom-call(bf16[16,16,640]{2,1,0:T(8,128)(2,1)S(1)} %all_to_all.5.got, bf16[32,512,128]{2,1,0:T(8,128)(2,1)S(1)} %copy-done), custom_call_target="tpu_custom_call" | custom-call | tf_op jit(solution)/shard_map/value/pallas_call | solution.py:362
  49.2 8.5 %all-gather = bf16[32,16,128]{2,1,0:T(8,128)(2,1)S(1)} all-gather(bf16[4,16,128]{2,1,0:T(8,128)(2,1)S(1)} %value.1), channel_id=2, replica_groups=mesh['req'=4,'chip'=4,'core'=2] {'chip','core'}, dimensions={0}, use_global_device_ids=true | all-gather | bytes 147456 | tf_op jit(solution)/shard_map/all_gather | solution.py:370
  57.7 1.3 %place.1 = bf16[2,8,32,128]{3,2,1,0:T(8,128)(2,1)} custom-call(s32[8]{0:T(128)} %assign.7, bf16[8,4,16,128]{3,2,1,0:T(8,128)(2,1)S(1)} %bitcast.3), custom_call_target="tpu_custom_call" | custom-call | tf_op jit(solution)/shard_map/place/pallas_call | solution.py:371
Async XLA Ops:
  0.0 8.7 %copy-start.5 = (s32[32,1]{1,0:T(8,128)S(1)}, s32[32,1]{1,0:T(8,128)}, u32[]{:S(2)}) copy-start(s32[32,1]{1,0:T(8,128)} %constant.5.clone.rate) | copy-start | bytes 388
  0.0 8.7 %copy-start.2 = (s32[2,6144]{1,0:T(2,128)S(1)}, s32[2,6144]{1,0:T(2,128)}, u32[]{:S(2)}) copy-start(s32[2,6144]{1,0:T(2,128)} %pos.1) | copy-start | bytes 147460
  0.0 8.7 %copy-start.1 = (bf16[2,6144,64]{1,2,0:T(8,128)(2,1)S(1)}, bf16[2,6144,64]{1,2,0:T(8,128)(2,1)}, u32[]{:S(2)}) copy-start(bf16[2,6144,64]{1,2,0:T(8,128)(2,1)} %param.19) | copy-start | bytes 4718596
  3.0 11.3 %collective-permute-start = (bf16[2,2,16,640]{3,2,1,0:T(8,128)(2,1)S(1)}, bf16[2,2,16,640]{3,2,1,0:T(8,128)(2,1)S(1)}, u32[]{:S(2)}, u32[]{:S(2)}) collective-permute-start(bf16[2,2,16,640]{3,2,1,0:T(8,128)(2,1)S(1)} %get-tuple-element.20), channel_id=1, source_target_pairs={{0,8},{8,0},{16,24},{24,16},{1,9},{9,1},{17,25},{25,17},{2,10},{10... | collective-permute-start | bytes 245768 | tf_op jit(solution)/shard_map/ppermute | solution.py:312
  6.1 9.2 %collective-permute-start.1 = (bf16[2,2,16,640]{3,2,1,0:T(8,128)(2,1)S(1)}, bf16[2,2,16,640]{3,2,1,0:T(8,128)(2,1)S(1)}, u32[]{:S(2)}, u32[]{:S(2)}) collective-permute-start(bf16[2,2,16,640]{3,2,1,0:T(8,128)(2,1)S(1)} %get-tuple-element.21), channel_id=1, source_target_pairs={{0,16},{8,24},{16,0},{24,8},{1,17},{9,25},{17,1},{25,9},{2,18},{10... | collective-permute-start | bytes 245768 | tf_op jit(solution)/shard_map/ppermute | solution.py:312
  8.7 6.6 %collective-permute-start.2 = (bf16[2,2,16,640]{3,2,1,0:T(8,128)(2,1)S(1)}, bf16[2,2,16,640]{3,2,1,0:T(8,128)(2,1)S(1)}, u32[]{:S(2)}, u32[]{:S(2)}) collective-permute-start(bf16[2,2,16,640]{3,2,1,0:T(8,128)(2,1)S(1)} %get-tuple-element.22), channel_id=1, source_target_pairs={{0,24},{8,16},{16,8},{24,0},{1,25},{9,17},{17,9},{25,1},{2,26},{10... | collective-permute-start | bytes 245768 | tf_op jit(solution)/shard_map/ppermute | solution.py:312
  8.7 8.5 %copy-start.3 = (s32[16,64]{1,0:T(8,128)S(1)}, s32[16,64]{1,0:T(8,128)}, u32[]{:S(2)}) copy-start(s32[16,64]{1,0:T(8,128)} %constant.4.clone.rate) | copy-start | bytes 12292
  8.8 8.5 %copy-start.4 = (bf16[2,8,512]{2,1,0:T(8,128)(2,1)S(1)}, bf16[2,8,512]{2,1,0:T(8,128)(2,1)}, u32[]{:S(2)}) copy-start(bf16[2,8,512]{2,1,0:T(8,128)(2,1)} %new_lat.1) | copy-start | bytes 49156
  8.8 8.5 %copy-start.6 = (bf16[2,8,64]{2,1,0:T(8,128)(2,1)S(1)}, bf16[2,8,64]{2,1,0:T(8,128)(2,1)}, u32[]{:S(2)}) copy-start(bf16[2,8,64]{2,1,0:T(8,128)(2,1)} %new_rope.1) | copy-start | bytes 6148
  15.3 1.3 %collective-permute-start.3 = (bf16[2,2,16,640]{3,2,1,0:T(8,128)(2,1)S(1)}, bf16[2,2,16,640]{3,2,1,0:T(8,128)(2,1)S(1)}, u32[]{:S(2)}, u32[]{:S(2)}) collective-permute-start(bf16[2,2,16,640]{3,2,1,0:T(8,128)(2,1)S(1)} %get-tuple-element.27.rest_0_), channel_id=1, source_target_pairs={{0,1},{1,0},{2,3},{3,2},{4,5},{5,4},{6,7},{7,6},{8,9},{9,8},{10,11... | collective-permute-start | bytes 245768 | tf_op jit(solution)/shard_map/ppermute | solution.py:332
  15.3 1.4 %collective-permute-start.4 = (bf16[2,2,16,640]{3,2,1,0:T(8,128)(2,1)S(1)}, bf16[2,2,16,640]{3,2,1,0:T(8,128)(2,1)S(1)}, u32[]{:S(2)}, u32[]{:S(2)}) collective-permute-start(bf16[2,2,16,640]{3,2,1,0:T(8,128)(2,1)S(1)} %collective-permute-done.rest_1_), channel_id=1, source_target_pairs={{0,1},{1,0},{2,3},{3,2},{4,5},{5,4},{6,7},{7,6},{8,9},{9,8},{10,11... | collective-permute-start | bytes 245768 | tf_op jit(solution)/shard_map/ppermute | solution.py:332
  15.8 1.3 %collective-permute-start.5 = (bf16[2,2,16,640]{3,2,1,0:T(8,128)(2,1)S(1)}, bf16[2,2,16,640]{3,2,1,0:T(8,128)(2,1)S(1)}, u32[]{:S(2)}, u32[]{:S(2)}) collective-permute-start(bf16[2,2,16,640]{3,2,1,0:T(8,128)(2,1)S(1)} %collective-permute-done.1.rest_2_), channel_id=1, source_target_pairs={{0,1},{1,0},{2,3},{3,2},{4,5},{5,4},{6,7},{7,6},{8,9},{9,8},{10,11... | collective-permute-start | bytes 245768 | tf_op jit(solution)/shard_map/ppermute | solution.py:332
  15.8 1.4 %collective-permute-start.6 = (bf16[2,2,16,640]{3,2,1,0:T(8,128)(2,1)S(1)}, bf16[2,2,16,640]{3,2,1,0:T(8,128)(2,1)S(1)}, u32[]{:S(2)}, u32[]{:S(2)}) collective-permute-start(bf16[2,2,16,640]{3,2,1,0:T(8,128)(2,1)S(1)} %collective-permute-done.2.rest_3_), channel_id=1, source_target_pairs={{0,1},{1,0},{2,3},{3,2},{4,5},{5,4},{6,7},{7,6},{8,9},{9,8},{10,11... | collective-permute-start | bytes 245768 | tf_op jit(solution)/shard_map/ppermute | solution.py:332
  17.3 31.2 %copy-start = (bf16[32,512,128]{2,1,0:T(8,128)(2,1)S(1)}, bf16[32,512,128]{2,1,0:T(8,128)(2,1)}, u32[]{:S(2)}) copy-start(bf16[32,512,128]{2,1,0:T(8,128)(2,1)} %w.1) | copy-start | bytes 12582916
  28.2 1.7 %collective-permute-start.7 = (bf16[2,2,4,16,640]{4,3,2,1,0:T(8,128)(2,1)S(1)}, bf16[2,2,4,16,640]{4,3,2,1,0:T(8,128)(2,1)S(1)}, u32[]{:S(2)}, u32[]{:S(2)}) collective-permute-start(bf16[2,2,4,16,640]{4,3,2,1,0:T(8,128)(2,1)S(1)} %get-tuple-element.32), channel_id=1, source_target_pairs={{0,1},{1,0},{2,3},{3,2},{4,5},{5,4},{6,7},{7,6},{8,9},{9,8},{10,11... | collective-permute-start | bytes 983048 | tf_op jit(solution)/shard_map/ppermute | solution.py:352

commit v3 on v2

--- a/solution.py
+++ b/solution.py
@@ -26,6 +26,15 @@
 
 def in_hbm(x):
     return pltpu.with_memory_space_constraint(x, pltpu.HBM)
+
+
+def hop(x, axis, n):
+    size = lax.axis_size(axis)
+    return lax.ppermute(x, axis, [(i, i ^ n) for i in range(size)])
+
+
+def hops(blocks, axis):
+    return [hop(blocks[k], axis, k) for k in reversed(range(1, len(blocks)))]
 
 
 def turn_rates(width):
@@ -145,7 +154,7 @@
     dims, B, assign, new_pos, new_lat, new_rope, rate, keys, cbuf, *rest
 ):
     R, J, T, HC, DL, CAP = dims
-    own, other = rest[:R], rest[R : 2 * R]
+    own, other = rest[:R][::-1], rest[R : 2 * R][::-1]
     send, keep, q, sbuf, acc = rest[2 * R :]
     nb = CAP // B
     NQ = T * R * 2 * HC
@@ -169,9 +178,9 @@
             q[j, :, DL : DL + KEYS], keys[j, :, rows], preferred_element_type=F32
         )
 
+    sbuf[0] = score(0, 0)
     for j in range(J):
         r = assign[g * J + j]
-        sbuf[0] = score(j, 0)
         pick = lax.broadcasted_iota(jnp.int32, new_lat.shape[1:], 0) == r
         lat = [
             jnp.sum(jnp.where(pick, new_lat[u].astype(F32), 0.0), axis=0, keepdims=True)
@@ -200,16 +209,17 @@
         m = jnp.max(jnp.where(valid, s, LOW), axis=1, keepdims=True)
         p = jnp.where(valid, jnp.exp2(s * EXPO - m * EXPO), 0.0)
         l = jnp.sum(p, axis=1, keepdims=True)
-        acc[...] = jnp.dot(p.astype(BF), lat, preferred_element_type=F32)
+        acc[j] = jnp.dot(p.astype(BF), lat, preferred_element_type=F32)
         for i in range(nb):
-            if i + 1 < nb:
-                sbuf[(i + 1) % 2] = score(j, i + 1)
-            s = sbuf[i % 2]
+            at = j * nb + i
+            if at + 1 < J * nb:
+                sbuf[(at + 1) % 2] = score((at + 1) // nb, (at + 1) % nb)
+            s = sbuf[at % 2]
             top = jnp.maximum(m, jnp.max(s, axis=1, keepdims=True))
             shrink = jnp.exp2((m - top) * EXPO)
             p = jnp.exp2(s * EXPO - top * EXPO)
             l = l * shrink + jnp.sum(p, axis=1, keepdims=True)
-            acc[...] = acc[...] * shrink + jnp.dot(
+            acc[j] = acc[j] * shrink + jnp.dot(
                 p.astype(BF), cbuf[j, pl.ds(i * B, B)], preferred_element_type=F32
             )
             m = top
@@ -219,8 +229,8 @@
             for k in range(R):
                 base = (t * R + k) * 2 * HC
                 lo, hi = slice(base, base + HC), slice(base + HC, base + 2 * HC)
-                keep[j, t, k, :, :DL] = jnp.where(c == 0, acc[lo], acc[hi])
-                send[j, t, k, :, :DL] = jnp.where(c == 0, acc[hi], acc[lo]).astype(BF)
+                keep[j, t, k, :, :DL] = jnp.where(c == 0, acc[j, lo], acc[j, hi])
+                send[j, t, k, :, :DL] = jnp.where(c == 0, acc[j, hi], acc[j, lo]).astype(BF)
                 keep[j, t, k, :, DL:] = jnp.where(c == 0, whole[lo], whole[hi])
                 send[j, t, k, :, DL:] = jnp.where(c == 0, parts[hi], parts[lo]).astype(BF)
 
@@ -230,55 +240,80 @@
     return m, x[:, DL + 3 : DL + 4] + x[:, DL + 4 : DL + 5] + x[:, DL + 5 : DL + 6]
 
 
-def pair_kernel(dims, keep, got, out):
+def pair_kernel(dims, keep, got, *outs):
     R, J, T, HC, HS, CH, DL = dims
-    g = lax.axis_index("req")
     HB = HC // HS
-    for j in range(J):
-        for t in range(T):
-            a = jnp.concatenate([keep[j, t, k] for k in range(R)], axis=0)
-            b = jnp.concatenate([got[j, t, k] for k in range(R)], axis=0).astype(F32)
-            ma, la = a[:, DL : DL + 1], a[:, DL + 1 : DL + 2]
-            mb, lb = stats_of(b[:, :], DL)
-            m = jnp.maximum(ma, mb)
-            wa, wb = jnp.exp2((ma - m) * EXPO), jnp.exp2((mb - m) * EXPO)
-            o = (a[:, :DL] * wa + b[:, :DL] * wb).astype(BF)
-            st = stat_lanes(R * HC, split3(m) + split3(la * wa + lb * wb)).astype(BF)
-            for k in range(R):
-                for s in range(HS):
-                    at = (g ^ k) * CH + (j * T + t) * HS + s
-                    rows = slice(k * HC + s * HB, k * HC + (s + 1) * HB)
-                    out[at, :, :DL] = o[rows]
-                    out[at, :, DL:] = st[rows]
-
-
-def value_kernel(dims, got, w, out):
-    R, CH, HC, HS, HB, DL, DV, JT = dims
-    c = lax.axis_index("core")
-    part = lax.rem(lax.axis_index("chip"), HS)
-    first = c * HC + part * HB
-    x = [
-        jnp.concatenate([got[r * CH + i] for r in range(R)], axis=0).astype(F32) for i in range(CH)
-    ]
-    ms, ls = zip(*[stats_of(v, DL) for v in x])
+    chip = lax.axis_index("chip")
+    for n in range(CH):
+        token = (chip ^ n) // HS
+        j, t = token // T, lax.rem(token, T)
+        part = lax.rem(chip ^ n, HS)
+
+        def chosen(ref, k):
+            v = ref[j, t, k].astype(F32)
+            rows = v[:HB]
+            for s in range(1, HS):
+                rows = jnp.where(part == s, v[s * HB : (s + 1) * HB], rows)
+            return rows
+
+        a = jnp.concatenate([chosen(keep, k) for k in range(R)], axis=0)
+        b = jnp.concatenate([chosen(got, k) for k in range(R)], axis=0)
+        ma, la = a[:, DL : DL + 1], a[:, DL + 1 : DL + 2]
+        mb, lb = stats_of(b, DL)
+        m = jnp.maximum(ma, mb)
+        wa, wb = jnp.exp2((ma - m) * EXPO), jnp.exp2((mb - m) * EXPO)
+        o = a[:, :DL] * wa + b[:, :DL] * wb
+        l = la * wa + lb * wb
+        outs[n][:, :DL] = o.astype(outs[n].dtype)
+        tile = stat_lanes(R * HB, (m, l) if n == 0 else split3(m) + split3(l))
+        outs[n][:, DL:] = tile.astype(outs[n].dtype)
+
+
+def combine_kernel(dims, *rest):
+    R, HB, DL = dims
+    outs = rest[len(rest) - R :]
+    *got, own = rest[: len(rest) - R]
+    x = [own[...]] + [v[...].astype(F32) for v in got]
+    ms, ls = zip(*[(x[0][:, DL : DL + 1], x[0][:, DL + 1 : DL + 2])] + [stats_of(v, DL) for v in x[1:]])
     m = functools.reduce(jnp.maximum, ms)
     ws = [jnp.exp2((v - m) * EXPO) for v in ms]
     total = sum(w_ * l for w_, l in zip(ws, ls))
-    o = sum(w_ * v[:, :DL] for w_, v in zip(ws, x)) / total
-    o = o.astype(BF).astype(F32).reshape(R, HB, DL)
-    x = jnp.swapaxes(o, 0, 1).astype(BF)
+    o = (sum(w_ * v[:, :DL] for w_, v in zip(ws, x)) / total).astype(BF)
+    for k in range(R):
+        outs[k][...] = o[k * HB : (k + 1) * HB]
+
+
+def value_kernel(dims, w, *rest):
+    R, HC, HS, HB = dims
+    got, out = rest[:R][::-1], rest[R]
+    first = lax.axis_index("core") * HC + lax.rem(lax.axis_index("chip"), HS) * HB
+    x = jnp.stack([v[...].astype(F32) for v in got])
+    x = jnp.swapaxes(x, 0, 1).astype(BF)
     ys = [jnp.dot(x[h], w[first + h], preferred_element_type=F32) for h in range(HB)]
     out[...] = jnp.swapaxes(jnp.stack(ys), 0, 1).astype(BF)
 
 
-def place_kernel(dims, assign, got, out):
+def place_kernel(dims, assign, *rest):
     R, J, T, HC, HS, HB, CH = dims
-    for chip in range(CH):
-        jt, s = divmod(chip, HS)
-        j, t = divmod(jt, T)
-        for c in range(2):
-            for r in range(R):
-                out[t, assign[r * J + j], pl.ds(c * HC + s * HB, HB), :] = got[chip * 2 + c, r]
+    blocks, out = rest[: 2 * CH], rest[2 * CH]
+    g, chip, c = lax.axis_index("req"), lax.axis_index("chip"), lax.axis_index("core")
+    for n in range(CH):
+        token = (chip ^ n) // HS
+        j, t = token // T, lax.rem(token, T)
+        for b in range(2):
+            block = blocks[2 * (CH - 1 - n) + b]
+            first = (c ^ b) * HC + lax.rem(chip ^ n, HS) * HB
+            for k in range(R):
+                request = assign[(g ^ k) * J + j]
+                if HS == 1:
+                    rows = pl.ds(pl.multiple_of(first, HB), HB)
+                    out[t, request, rows, :] = block[k]
+                    continue
+                for at in range(0, 2 * HC, HB):
+
+                    @pl.when(first == at)
+                    def _():
+                        out[t, request, at : at + HB, :] = block[k]
 
 
 def body(
@@ -308,9 +343,9 @@
         compiler_params=big,
         name="absorb",
     )(assignment, new_pos, in_hbm(q_nope), in_hbm(q_rope), in_hbm(rate_row), in_hbm(w_uk))
-    arrived = [blocks[0]] + [
-        lax.ppermute(blocks[k], "req", [(i, i ^ k) for i in range(R)]) for k in range(1, R)
-    ]
+    arrived = hops(blocks, "req")
+    near = hop(blocks[0], "core", 1)
+
     cuts = CAP // 512
     keys, cached = pl.pallas_call(
         functools.partial(prepare_kernel, (J, CAP), cuts),
@@ -328,8 +363,9 @@
         name="prepare",
     )(assignment, lengths, positions, jnp.swapaxes(rope_cache, 1, 2), rate_col, in_hbm(latent_cache))
 
-    own, keys, cached = lax.optimization_barrier((arrived, keys, cached))
-    other = [lax.ppermute(v, "core", [(0, 1), (1, 0)]) for v in own]
+    arrived, keys, cached = lax.optimization_barrier((arrived, keys, cached))
+    own = arrived + [blocks[0]]
+    other = [hop(v, "core", 1) for v in arrived] + [near]
 
     B = 1024
     NQ = T * R * HL
@@ -344,38 +380,49 @@
         scratch_shapes=[
             pltpu.VMEM((J, NQ, W), BF),
             pltpu.VMEM((2, NQ, B), F32),
-            pltpu.VMEM((NQ, DL), F32),
+            pltpu.VMEM((J, NQ, DL), F32),
         ],
         compiler_params=pltpu.CompilerParams(vmem_limit_bytes=16 << 20),
         name="attend",
     )(assignment, new_pos, new_latent, new_rope, rate_row, keys, cached, *own, *other)
-    got = lax.ppermute(send, "core", [(0, 1), (1, 0)])
-    paired = pl.pallas_call(
+    got = hop(send, "core", 1)
+    pieces = pl.pallas_call(
         functools.partial(pair_kernel, (R, J, T, HC, HS, CH, DL)),
-        out_shape=jax.ShapeDtypeStruct((R * CH, HB, W), BF),
+        out_shape=[jax.ShapeDtypeStruct((R * HB, W), BF if n else F32) for n in range(CH)],
         in_specs=[VMEM, VMEM],
-        out_specs=VMEM,
+        out_specs=[VMEM] * CH,
         compiler_params=big,
         name="pair",
     )(keep, got)
-    shares = lax.all_to_all(paired, ("req", "chip"), 0, 0)
+    shares = hops(pieces, "chip") + [pieces[0]]
+    latents = pl.pallas_call(
+        functools.partial(combine_kernel, (R, HB, DL)),
+        out_shape=[jax.ShapeDtypeStruct((HB, DL), BF)] * R,
+        in_specs=[VMEM] * CH,
+        out_specs=[VMEM] * R,
+        compiler_params=big,
+        name="combine",
+    )(*shares)
+    returned = hops(latents, "req") + [latents[0]]
     values = pl.pallas_call(
-        functools.partial(value_kernel, (R, CH, HC, HS, HB, DL, DV, J * T)),
+        functools.partial(value_kernel, (R, HC, HS, HB)),
         out_shape=jax.ShapeDtypeStruct((R, HB, DV), BF),
-        in_specs=[VMEM, VMEM],
+        in_specs=[VMEM] * (1 + R),
         out_specs=VMEM,
         compiler_params=big,
         name="value",
-    )(shares, w_uv)
-    gathered = lax.all_gather(values, ("chip", "core"))
+    )(w_uv, *returned)
+    gathered = []
+    for block in hops([values] * CH, "chip") + [values]:
+        gathered += [block, hop(block, "core", 1)]
     return pl.pallas_call(
         functools.partial(place_kernel, (R, J, T, HC, HS, HB, CH)),
         out_shape=jax.ShapeDtypeStruct((T, REQS, HL, DV), BF),
-        in_specs=[SMEM, VMEM],
+        in_specs=[SMEM] + [VMEM] * (2 * CH),
         out_specs=VMEM,
         compiler_params=big,
         name="place",
-    )(assignment, gathered)
+    )(assignment, *gathered)
 
 
 def solution(mesh):

time: 59.3 us -> 56.2 us (0.948)
  blocking collectives: 26.3 us -> 0 us
  waiting for transfers between devices: 3.14 us -> 15.4 us
  starting transfers between devices: 7.12 us -> 18.2 us
    all_to_all x1 -> x0, blocking collectives: 17.9 us -> none  [body(): shares = lax.all_to_all(paired, ('req', 'chip'), 0, 0)]
    ppermute x8 -> x21, waiting for transfers between devices: 3.14 us -> 15.4 us  [hop(): return lax.ppermute(x, axis, [(i, i ^ n) for i in range(size)])]
    ppermute x8 -> x21, starting transfers between devices: 7.12 us -> 18.2 us  [hop(): return lax.ppermute(x, axis, [(i, i ^ n) for i in range(size)])]
    all_gather x1 -> x0, blocking collectives: 8.49 us -> none  [body(): gathered = lax.all_gather(values, ('chip', 'core'))]
  transfers between devices with their start and end apart: 8 -> 21, of which waited for: 6 -> 14; matrix products, arithmetic and copies ran while one was open for 0% -> 0% of each run, Pallas kernels for 9% -> 10%
where the time goes in v3:
time: 56.2 us; the launch traced here: 56 us
  Pallas kernels  22.3 us (40%)
  starting transfers between devices  18.2 us (32%)
  waiting for transfers between devices  15.4 us (27%)
    ppermute x21, starting transfers between devices, hop(): return lax.ppermute(x, axis, [(i, i ^ n) for i in range(size)])  18.2 us
    ppermute x21, waiting for transfers between devices, hop(): return lax.ppermute(x, axis, [(i, i ^ n) for i in range(size)])  15.4 us
    pallas_call x1, Pallas kernels, body(): pl.pallas_call(functools.partial(attend_kernel, (R, J, T, HC, DL, CAP), B...  10.9 us
    pallas_call x1, Pallas kernels, body(): pl.pallas_call(functools.partial(prepare_kernel, (J, CAP), cuts), out_sha...  5.59 us
    pallas_call x1, Pallas kernels, body(): pl.pallas_call(functools.partial(absorb_kernel, (R, J, T, HC, DL)), out_s...  3.02 us
    pallas_call x1, Pallas kernels, body(): pl.pallas_call(functools.partial(place_kernel, (R, J, T, HC, HS, HB, CH))...  1.43 us
  transfers between devices with their start and end apart: 21, of which 14 were waited for; matrix products, arithmetic and copies ran while one was open for 0% of the time, Pallas kernels for 10%

profile of v3, /device:TPU:0, one launch (start us, length us, event | category | flops | bytes accessed | tf_op | source)
XLA Modules:
  0.0 56.0 jit_solution(3676223092233992471)
XLA Ops:
  0.0 0.0 copy-start.5
  0.0 0.0 copy-start.2
  0.0 0.0 copy-start.1
  0.0 3.0 %absorb.1 = (bf16[2,2,16,640]{3,2,1,0:T(8,128)(2,1)S(1)}, bf16[2,2,16,640]{3,2,1,0:T(8,128)(2,1)S(1)}, bf16[2,2,16,640]{3,2,1,0:T(8,128)(2,1)S(1)}, bf16[2,2,16,640]{3,2,1,0:T(8,128)(2,1)S(1)}) custom-call(s32[8]{0:T(128)} %assign.7, s32[8]{0:T(128)} %new_pos.3, bf16[2,8,32,128]{3,2,1,0:T(8,128)(2,1)} %qn.1, bf16[2,8,32,64]{3,2,1,0:T(8,128)(2,1)} %qr.1, ...), custom_call_target="tpu_custom_call" | custom-call | tf_op jit(solution)/shard_map/absorb/pallas_call | solution.py:337
  3.0 5.1 %collective-permute-start = (bf16[2,2,16,640]{3,2,1,0:T(8,128)(2,1)S(1)}, bf16[2,2,16,640]{3,2,1,0:T(8,128)(2,1)S(1)}, u32[]{:S(2)}, u32[]{:S(2)}) collective-permute-start(bf16[2,2,16,640]{3,2,1,0:T(8,128)(2,1)S(1)} %get-tuple-element.26), channel_id=1, source_target_pairs={{0,24},{8,16},{16,8},{24,0},{1,25},{9,17},{17,9},{25,1},{2,26},{10... | collective-permute-start | bytes 245768 | tf_op jit(solution)/shard_map/ppermute | solution.py:33
  8.2 0.0 collective-permute-start.1
  8.2 0.6 %collective-permute-start.2 = (bf16[2,2,16,640]{3,2,1,0:T(8,128)(2,1)S(1)}, bf16[2,2,16,640]{3,2,1,0:T(8,128)(2,1)S(1)}, u32[]{:S(2)}, u32[]{:S(2)}) collective-permute-start(bf16[2,2,16,640]{3,2,1,0:T(8,128)(2,1)S(1)} %get-tuple-element.28), channel_id=1, source_target_pairs={{0,8},{8,0},{16,24},{24,16},{1,9},{9,1},{17,25},{25,17},{2,10},{10... | collective-permute-start | bytes 245768 | tf_op jit(solution)/shard_map/ppermute | solution.py:33
  8.8 0.0 collective-permute-start.6
  8.8 0.0 copy-done.5
  8.8 0.0 copy-done.2
  8.8 0.0 copy-done.1
  8.8 0.0 copy-start.3
  8.8 0.0 copy-start.4
  8.8 0.0 copy-start.6
  8.9 5.6 %prepare.1 = (bf16[2,80,6144]{2,1,0:T(8,128)(2,1)S(1)}, bf16[2,6144,512]{2,1,0:T(8,128)(2,1)S(1)}) custom-call(s32[8]{0:T(128)} %assign.7, s32[8]{0:T(128)} %lengths.1, s32[2,6144]{1,0:T(2,128)S(1)} %copy-done.2, bf16[2,64,6144]{2,1,0:T(8,128)(2,1)S(1)} %bitcast.1, s32[32,1]{1,0:T(8,128)S(1)} %copy-done.5, bf16[2,6144,512]{2,1,0:T(8,128)(2,1)} %c_hbm.1), custom_call_target="tpu_custom_call" | custom-call | bytes 25165824 | tf_op jit(solution)/shard_map/prepare/pallas_call | solution.py:350
  14.5 0.0 collective-permute-done.rest_0_
  14.5 0.6 collective-permute-done.1.rest_1_
  15.0 0.0 collective-permute-done.2.rest_2_
  15.0 0.0 collective-permute-start.3
  15.0 0.5 collective-permute-start.4
  15.5 0.0 collective-permute-start.5
  15.6 0.0 collective-permute-done.6.rest_7_
  15.6 0.7 %collective-permute-done.3.rest_4_ = bf16[2,2,16,640]{3,2,1,0:T(8,128)(2,1)S(1)} collective-permute-done((bf16[2,2,16,640]{3,2,1,0:T(8,128)(2,1)S(1)}, bf16[2,2,16,640]{3,2,1,0:T(8,128)(2,1)S(1)}, u32[]{:S(2)}, u32[]{:S(2)}) %collective-permute-start.3) | collective-permute-done | bytes 81952 | tf_op jit(solution)/shard_map/ppermute | solution.py:33
  16.3 0.2 collective-permute-done.4.rest_5_
  16.5 0.4 collective-permute-done.5.rest_6_
  16.8 0.0 copy-done.3
  16.8 0.0 copy-done.4
  16.8 0.0 copy-done.6
  16.8 0.0 copy-start
  16.8 10.9 %attend.1 = (bf16[2,2,4,16,640]{4,3,2,1,0:T(8,128)(2,1)S(1)}, f32[2,2,4,16,640]{4,3,2,1,0:T(8,128)S(1)}) custom-call(s32[8]{0:T(128)} %assign.7, s32[8]{0:T(128)} %new_pos.3, bf16[2,8,512]{2,1,0:T(8,128)(2,1)S(1)} %copy-done.4, bf16[2,8,64]{2,1,0:T(8,128)(2,1)S(1)} %copy-done.6, s32[16,64]{1,0:T(8,128)S(1)} %copy-done.3, ...), custom_call_target="tpu_custom_call" | custom-call | tf_op jit(solution)/shard_map/attend/pallas_call | solution.py:372
  27.7 0.2 collective-permute-start.7
  27.9 1.5 %collective-permute-done.7.got = bf16[2,2,4,16,640]{4,3,2,1,0:T(8,128)(2,1)S(1)} collective-permute-done((bf16[2,2,4,16,640]{4,3,2,1,0:T(8,128)(2,1)S(1)}, bf16[2,2,4,16,640]{4,3,2,1,0:T(8,128)(2,1)S(1)}, u32[]{:S(2)}, u32[]{:S(2)}) %collective-permute-start.7) | collective-permute-done | bytes 327712 | tf_op jit(solution)/shard_map/ppermute | solution.py:33
  29.4 0.7 %pair.1 = (f32[64,640]{1,0:T(8,128)S(1)}, bf16[64,640]{1,0:T(8,128)(2,1)S(1)}, bf16[64,640]{1,0:T(8,128)(2,1)S(1)}, bf16[64,640]{1,0:T(8,128)(2,1)S(1)}) custom-call(f32[2,2,4,16,640]{4,3,2,1,0:T(8,128)S(1)} %get-tuple-element.37.keep, bf16[2,2,4,16,640]{4,3,2,1,0:T(8,128)(2,1)S(1)} %collective-permute-done.7.got), custom_call_target="tpu_custom_call" | custom-call | tf_op jit(solution)/shard_map/pair/pallas_call | solution.py:389
  30.2 2.5 %collective-permute-start.8 = (bf16[64,640]{1,0:T(8,128)(2,1)S(1)}, bf16[64,640]{1,0:T(8,128)(2,1)S(1)}, u32[]{:S(2)}, u32[]{:S(2)}) collective-permute-start(bf16[64,640]{1,0:T(8,128)(2,1)S(1)} %get-tuple-element.39), channel_id=1, source_target_pairs={{0,6},{2,4},{4,2},{6,0},{1,7},{3,5},{5,3},{7,1},{8,14},{10,12},{12... | collective-permute-start | bytes 245768 | tf_op jit(solution)/shard_map/ppermute | solution.py:33
  32.7 0.5 collective-permute-start.9
  33.2 0.5 collective-permute-start.10
  33.7 2.0 %collective-permute-done.8.rest_0_ = bf16[64,640]{1,0:T(8,128)(2,1)S(1)} collective-permute-done((bf16[64,640]{1,0:T(8,128)(2,1)S(1)}, bf16[64,640]{1,0:T(8,128)(2,1)S(1)}, u32[]{:S(2)}, u32[]{:S(2)}) %collective-permute-start.8) | collective-permute-done | bytes 81952 | tf_op jit(solution)/shard_map/ppermute | solution.py:33
  35.7 1.7 %collective-permute-done.9.rest_1_ = bf16[64,640]{1,0:T(8,128)(2,1)S(1)} collective-permute-done((bf16[64,640]{1,0:T(8,128)(2,1)S(1)}, bf16[64,640]{1,0:T(8,128)(2,1)S(1)}, u32[]{:S(2)}, u32[]{:S(2)}) %collective-permute-start.9) | collective-permute-done | bytes 81952 | tf_op jit(solution)/shard_map/ppermute | solution.py:33
  37.4 0.2 collective-permute-done.10.rest_2_
  37.6 0.2 combine.1
  37.9 3.5 %collective-permute-start.11 = (bf16[16,512]{1,0:T(8,128)(2,1)S(1)}, bf16[16,512]{1,0:T(8,128)(2,1)S(1)}, u32[]{:S(2)}, u32[]{:S(2)}) collective-permute-start(bf16[16,512]{1,0:T(8,128)(2,1)S(1)} %get-tuple-element.43), channel_id=1, source_target_pairs={{0,24},{8,16},{16,8},{24,0},{1,25},{9,17},{17,9},{25,1},{2,26},{10... | collective-permute-start | bytes 49160 | tf_op jit(solution)/shard_map/ppermute | solution.py:33
  41.4 0.0 collective-permute-start.12
  41.4 0.9 %collective-permute-start.13 = (bf16[16,512]{1,0:T(8,128)(2,1)S(1)}, bf16[16,512]{1,0:T(8,128)(2,1)S(1)}, u32[]{:S(2)}, u32[]{:S(2)}) collective-permute-start(bf16[16,512]{1,0:T(8,128)(2,1)S(1)} %get-tuple-element.45), channel_id=1, source_target_pairs={{0,8},{8,0},{16,24},{24,16},{1,9},{9,1},{17,25},{25,17},{2,10},{10... | collective-permute-start | bytes 49160 | tf_op jit(solution)/shard_map/ppermute | solution.py:33
  42.3 1.2 %collective-permute-done.11.rest_0_ = bf16[16,512]{1,0:T(8,128)(2,1)S(1)} collective-permute-done((bf16[16,512]{1,0:T(8,128)(2,1)S(1)}, bf16[16,512]{1,0:T(8,128)(2,1)S(1)}, u32[]{:S(2)}, u32[]{:S(2)}) %collective-permute-start.11) | collective-permute-done | bytes 16416 | tf_op jit(solution)/shard_map/ppermute | solution.py:33
  43.5 2.5 %collective-permute-done.12.rest_1_ = bf16[16,512]{1,0:T(8,128)(2,1)S(1)} collective-permute-done((bf16[16,512]{1,0:T(8,128)(2,1)S(1)}, bf16[16,512]{1,0:T(8,128)(2,1)S(1)}, u32[]{:S(2)}, u32[]{:S(2)}) %collective-permute-start.12) | collective-permute-done | bytes 16416 | tf_op jit(solution)/shard_map/ppermute | solution.py:33
  46.0 0.0 collective-permute-done.13.rest_2_
  46.0 0.0 copy-done
  46.0 0.4 value.1.rest_6_
  46.4 1.6 %collective-permute-start.18 = (bf16[4,16,128]{2,1,0:T(8,128)(2,1)S(1)}, bf16[4,16,128]{2,1,0:T(8,128)(2,1)S(1)}, u32[]{:S(2)}, u32[]{:S(2)}) collective-permute-start(bf16[4,16,128]{2,1,0:T(8,128)(2,1)S(1)} %value.1.rest_6_), channel_id=1, source_target_pairs={{0,2},{2,0},{4,6},{6,4},{1,3},{3,1},{5,7},{7,5},{8,10},{10,8},{12,... | collective-permute-start | bytes 49160 | tf_op jit(solution)/shard_map/ppermute | solution.py:33
  48.0 0.7 %collective-permute-start.16 = (bf16[4,16,128]{2,1,0:T(8,128)(2,1)S(1)}, bf16[4,16,128]{2,1,0:T(8,128)(2,1)S(1)}, u32[]{:S(2)}, u32[]{:S(2)}) collective-permute-start(bf16[4,16,128]{2,1,0:T(8,128)(2,1)S(1)} %value.1.rest_6_), channel_id=1, source_target_pairs={{0,4},{2,6},{4,0},{6,2},{1,5},{3,7},{5,1},{7,3},{8,12},{10,14},{12... | collective-permute-start | bytes 49160 | tf_op jit(solution)/shard_map/ppermute | solution.py:33
  48.8 1.2 %collective-permute-start.14 = (bf16[4,16,128]{2,1,0:T(8,128)(2,1)S(1)}, bf16[4,16,128]{2,1,0:T(8,128)(2,1)S(1)}, u32[]{:S(2)}, u32[]{:S(2)}) collective-permute-start(bf16[4,16,128]{2,1,0:T(8,128)(2,1)S(1)} %value.1.rest_6_), channel_id=1, source_target_pairs={{0,6},{2,4},{4,2},{6,0},{1,7},{3,5},{5,3},{7,1},{8,14},{10,12},{12... | collective-permute-start | bytes 49160 | tf_op jit(solution)/shard_map/ppermute | solution.py:33
  50.0 0.0 collective-permute-start.20
  50.0 0.4 collective-permute-done.18.rest_4_
  50.4 0.1 collective-permute-start.19
  50.5 1.3 %collective-permute-done.16.rest_2_ = bf16[4,16,128]{2,1,0:T(8,128)(2,1)S(1)} collective-permute-done((bf16[4,16,128]{2,1,0:T(8,128)(2,1)S(1)}, bf16[4,16,128]{2,1,0:T(8,128)(2,1)S(1)}, u32[]{:S(2)}, u32[]{:S(2)}) %collective-permute-start.16) | collective-permute-done | bytes 16416 | tf_op jit(solution)/shard_map/ppermute | solution.py:33
  51.8 0.0 collective-permute-start.17
  51.8 1.6 %collective-permute-done.14.rest_0_ = bf16[4,16,128]{2,1,0:T(8,128)(2,1)S(1)} collective-permute-done((bf16[4,16,128]{2,1,0:T(8,128)(2,1)S(1)}, bf16[4,16,128]{2,1,0:T(8,128)(2,1)S(1)}, u32[]{:S(2)}, u32[]{:S(2)}) %collective-permute-start.14) | collective-permute-done | bytes 16416 | tf_op jit(solution)/shard_map/ppermute | solution.py:33
  53.4 0.0 collective-permute-start.15
  53.4 0.0 collective-permute-done.20.rest_7_
  53.4 0.0 collective-permute-done.19.rest_5_
  53.4 0.0 collective-permute-done.17.rest_3_
  53.4 1.2 %collective-permute-done.15.rest_1_ = bf16[4,16,128]{2,1,0:T(8,128)(2,1)S(1)} collective-permute-done((bf16[4,16,128]{2,1,0:T(8,128)(2,1)S(1)}, bf16[4,16,128]{2,1,0:T(8,128)(2,1)S(1)}, u32[]{:S(2)}, u32[]{:S(2)}) %collective-permute-start.15) | collective-permute-done | bytes 16416 | tf_op jit(solution)/shard_map/ppermute | solution.py:33
  54.6 1.4 %place.1 = bf16[2,8,32,128]{3,2,1,0:T(8,128)(2,1)} custom-call(s32[8]{0:T(128)} %assign.7, bf16[4,16,128]{2,1,0:T(8,128)(2,1)S(1)} %collective-permute-done.14.rest_0_, bf16[4,16,128]{2,1,0:T(8,128)(2,1)S(1)} %collective-permute-done.15.rest_1_, bf16[4,16,128]{2,1,0:T(8,128)(2,1)S(1)} %collective-permute-done.16.rest_2_, ...), custom_call_target="tpu_custom_call" | custom-call | tf_op jit(solution)/shard_map/place/pallas_call | solution.py:418
Async XLA Ops:
  0.0 8.8 %copy-start.5 = (s32[32,1]{1,0:T(8,128)S(1)}, s32[32,1]{1,0:T(8,128)}, u32[]{:S(2)}) copy-start(s32[32,1]{1,0:T(8,128)} %constant.5.clone.rate) | copy-start | bytes 388
  0.0 8.8 %copy-start.2 = (s32[2,6144]{1,0:T(2,128)S(1)}, s32[2,6144]{1,0:T(2,128)}, u32[]{:S(2)}) copy-start(s32[2,6144]{1,0:T(2,128)} %pos.1) | copy-start | bytes 147460
  0.0 8.8 %copy-start.1 = (bf16[2,6144,64]{1,2,0:T(8,128)(2,1)S(1)}, bf16[2,6144,64]{1,2,0:T(8,128)(2,1)}, u32[]{:S(2)}) copy-start(bf16[2,6144,64]{1,2,0:T(8,128)(2,1)} %param.19) | copy-start | bytes 4718596
  3.0 11.4 %collective-permute-start = (bf16[2,2,16,640]{3,2,1,0:T(8,128)(2,1)S(1)}, bf16[2,2,16,640]{3,2,1,0:T(8,128)(2,1)S(1)}, u32[]{:S(2)}, u32[]{:S(2)}) collective-permute-start(bf16[2,2,16,640]{3,2,1,0:T(8,128)(2,1)S(1)} %get-tuple-element.26), channel_id=1, source_target_pairs={{0,24},{8,16},{16,8},{24,0},{1,25},{9,17},{17,9},{25,1},{2,26},{10... | collective-permute-start | bytes 245768 | tf_op jit(solution)/shard_map/ppermute | solution.py:33
  8.2 6.9 %collective-permute-start.1 = (bf16[2,2,16,640]{3,2,1,0:T(8,128)(2,1)S(1)}, bf16[2,2,16,640]{3,2,1,0:T(8,128)(2,1)S(1)}, u32[]{:S(2)}, u32[]{:S(2)}) collective-permute-start(bf16[2,2,16,640]{3,2,1,0:T(8,128)(2,1)S(1)} %get-tuple-element.27), channel_id=1, source_target_pairs={{0,16},{8,24},{16,0},{24,8},{1,17},{9,25},{17,1},{25,9},{2,18},{10... | collective-permute-start | bytes 245768 | tf_op jit(solution)/shard_map/ppermute | solution.py:33
  8.2 6.9 %collective-permute-start.2 = (bf16[2,2,16,640]{3,2,1,0:T(8,128)(2,1)S(1)}, bf16[2,2,16,640]{3,2,1,0:T(8,128)(2,1)S(1)}, u32[]{:S(2)}, u32[]{:S(2)}) collective-permute-start(bf16[2,2,16,640]{3,2,1,0:T(8,128)(2,1)S(1)} %get-tuple-element.28), channel_id=1, source_target_pairs={{0,8},{8,0},{16,24},{24,16},{1,9},{9,1},{17,25},{25,17},{2,10},{10... | collective-permute-start | bytes 245768 | tf_op jit(solution)/shard_map/ppermute | solution.py:33
  8.8 6.8 %collective-permute-start.6 = (bf16[2,2,16,640]{3,2,1,0:T(8,128)(2,1)S(1)}, bf16[2,2,16,640]{3,2,1,0:T(8,128)(2,1)S(1)}, u32[]{:S(2)}, u32[]{:S(2)}) collective-permute-start(bf16[2,2,16,640]{3,2,1,0:T(8,128)(2,1)S(1)} %get-tuple-element.36.rest_3_), channel_id=1, source_target_pairs={{0,1},{1,0},{2,3},{3,2},{4,5},{5,4},{6,7},{7,6},{8,9},{9,8},{10,11... | collective-permute-start | bytes 245768 | tf_op jit(solution)/shard_map/ppermute | solution.py:33
  8.8 8.0 %copy-start.3 = (s32[16,64]{1,0:T(8,128)S(1)}, s32[16,64]{1,0:T(8,128)}, u32[]{:S(2)}) copy-start(s32[16,64]{1,0:T(8,128)} %constant.4.clone.rate) | copy-start | bytes 12292
  8.8 8.0 %copy-start.4 = (bf16[2,8,512]{2,1,0:T(8,128)(2,1)S(1)}, bf16[2,8,512]{2,1,0:T(8,128)(2,1)}, u32[]{:S(2)}) copy-start(bf16[2,8,512]{2,1,0:T(8,128)(2,1)} %new_lat.1) | copy-start | bytes 49156
  8.8 8.0 %copy-start.6 = (bf16[2,8,64]{2,1,0:T(8,128)(2,1)S(1)}, bf16[2,8,64]{2,1,0:T(8,128)(2,1)}, u32[]{:S(2)}) copy-start(bf16[2,8,64]{2,1,0:T(8,128)(2,1)} %new_rope.1) | copy-start | bytes 6148
  15.0 1.3 %collective-permute-start.3 = (bf16[2,2,16,640]{3,2,1,0:T(8,128)(2,1)S(1)}, bf16[2,2,16,640]{3,2,1,0:T(8,128)(2,1)S(1)}, u32[]{:S(2)}, u32[]{:S(2)}) collective-permute-start(bf16[2,2,16,640]{3,2,1,0:T(8,128)(2,1)S(1)} %collective-permute-done.rest_0_), channel_id=1, source_target_pairs={{0,1},{1,0},{2,3},{3,2},{4,5},{5,4},{6,7},{7,6},{8,9},{9,8},{10,11... | collective-permute-start | bytes 245768 | tf_op jit(solution)/shard_map/ppermute | solution.py:33
  15.0 1.4 %collective-permute-start.4 = (bf16[2,2,16,640]{3,2,1,0:T(8,128)(2,1)S(1)}, bf16[2,2,16,640]{3,2,1,0:T(8,128)(2,1)S(1)}, u32[]{:S(2)}, u32[]{:S(2)}) collective-permute-start(bf16[2,2,16,640]{3,2,1,0:T(8,128)(2,1)S(1)} %collective-permute-done.1.rest_1_), channel_id=1, source_target_pairs={{0,1},{1,0},{2,3},{3,2},{4,5},{5,4},{6,7},{7,6},{8,9},{9,8},{10,11... | collective-permute-start | bytes 245768 | tf_op jit(solution)/shard_map/ppermute | solution.py:33
  15.5 1.3 %collective-permute-start.5 = (bf16[2,2,16,640]{3,2,1,0:T(8,128)(2,1)S(1)}, bf16[2,2,16,640]{3,2,1,0:T(8,128)(2,1)S(1)}, u32[]{:S(2)}, u32[]{:S(2)}) collective-permute-start(bf16[2,2,16,640]{3,2,1,0:T(8,128)(2,1)S(1)} %collective-permute-done.2.rest_2_), channel_id=1, source_target_pairs={{0,1},{1,0},{2,3},{3,2},{4,5},{5,4},{6,7},{7,6},{8,9},{9,8},{10,11... | collective-permute-start | bytes 245768 | tf_op jit(solution)/shard_map/ppermute | solution.py:33
  16.8 29.2 %copy-start = (bf16[32,512,128]{2,1,0:T(8,128)(2,1)S(1)}, bf16[32,512,128]{2,1,0:T(8,128)(2,1)}, u32[]{:S(2)}) copy-start(bf16[32,512,128]{2,1,0:T(8,128)(2,1)} %w.1) | copy-start | bytes 12582916
  27.7 1.7 %collective-permute-start.7 = (bf16[2,2,4,16,640]{4,3,2,1,0:T(8,128)(2,1)S(1)}, bf16[2,2,4,16,640]{4,3,2,1,0:T(8,128)(2,1)S(1)}, u32[]{:S(2)}, u32[]{:S(2)}) collective-permute-start(bf16[2,2,4,16,640]{4,3,2,1,0:T(8,128)(2,1)S(1)} %get-tuple-element.38), channel_id=1, source_target_pairs={{0,1},{1,0},{2,3},{3,2},{4,5},{5,4},{6,7},{7,6},{8,9},{9,8},{10,11... | collective-permute-start | bytes 983048 | tf_op jit(solution)/shard_map/ppermute | solution.py:33
  30.2 5.5 %collective-permute-start.8 = (bf16[64,640]{1,0:T(8,128)(2,1)S(1)}, bf16[64,640]{1,0:T(8,128)(2,1)S(1)}, u32[]{:S(2)}, u32[]{:S(2)}) collective-permute-start(bf16[64,640]{1,0:T(8,128)(2,1)S(1)} %get-tuple-element.39), channel_id=1, source_target_pairs={{0,6},{2,4},{4,2},{6,0},{1,7},{3,5},{5,3},{7,1},{8,14},{10,12},{12... | collective-permute-start | bytes 245768 | tf_op jit(solution)/shard_map/ppermute | solution.py:33
  32.7 4.7 %collective-permute-start.9 = (bf16[64,640]{1,0:T(8,128)(2,1)S(1)}, bf16[64,640]{1,0:T(8,128)(2,1)S(1)}, u32[]{:S(2)}, u32[]{:S(2)}) collective-permute-start(bf16[64,640]{1,0:T(8,128)(2,1)S(1)} %get-tuple-element.40), channel_id=1, source_target_pairs={{0,4},{2,6},{4,0},{6,2},{1,5},{3,7},{5,1},{7,3},{8,12},{10,14},{12... | collective-permute-start | bytes 245768 | tf_op jit(solution)/shard_map/ppermute | solution.py:33
  33.2 4.4 %collective-permute-start.10 = (bf16[64,640]{1,0:T(8,128)(2,1)S(1)}, bf16[64,640]{1,0:T(8,128)(2,1)S(1)}, u32[]{:S(2)}, u32[]{:S(2)}) collective-permute-start(bf16[64,640]{1,0:T(8,128)(2,1)S(1)} %get-tuple-element.41), channel_id=1, source_target_pairs={{0,2},{2,0},{4,6},{6,4},{1,3},{3,1},{5,7},{7,5},{8,10},{10,8},{12,... | collective-permute-start | bytes 245768 | tf_op jit(solution)/shard_map/ppermute | solution.py:33
  37.9 5.6 %collective-permute-start.11 = (bf16[16,512]{1,0:T(8,128)(2,1)S(1)}, bf16[16,512]{1,0:T(8,128)(2,1)S(1)}, u32[]{:S(2)}, u32[]{:S(2)}) collective-permute-start(bf16[16,512]{1,0:T(8,128)(2,1)S(1)} %get-tuple-element.43), channel_id=1, source_target_pairs={{0,24},{8,16},{16,8},{24,0},{1,25},{9,17},{17,9},{25,1},{2,26},{10... | collective-permute-start | bytes 49160 | tf_op jit(solution)/shard_map/ppermute | solution.py:33
  41.4 4.6 %collective-permute-start.12 = (bf16[16,512]{1,0:T(8,128)(2,1)S(1)}, bf16[16,512]{1,0:T(8,128)(2,1)S(1)}, u32[]{:S(2)}, u32[]{:S(2)}) collective-permute-start(bf16[16,512]{1,0:T(8,128)(2,1)S(1)} %get-tuple-element.44), channel_id=1, source_target_pairs={{0,16},{8,24},{16,0},{24,8},{1,17},{9,25},{17,1},{25,9},{2,18},{10... | collective-permute-start | bytes 49160 | tf_op jit(solution)/shard_map/ppermute | solution.py:33
  41.4 4.6 %collective-permute-start.13 = (bf16[16,512]{1,0:T(8,128)(2,1)S(1)}, bf16[16,512]{1,0:T(8,128)(2,1)S(1)}, u32[]{:S(2)}, u32[]{:S(2)}) collective-permute-start(bf16[16,512]{1,0:T(8,128)(2,1)S(1)} %get-tuple-element.45), channel_id=1, source_target_pairs={{0,8},{8,0},{16,24},{24,16},{1,9},{9,1},{17,25},{25,17},{2,10},{10... | collective-permute-start | bytes 49160 | tf_op jit(solution)/shard_map/ppermute | solution.py:33
  46.4 4.0 %collective-permute-start.18 = (bf16[4,16,128]{2,1,0:T(8,128)(2,1)S(1)}, bf16[4,16,128]{2,1,0:T(8,128)(2,1)S(1)}, u32[]{:S(2)}, u32[]{:S(2)}) collective-permute-start(bf16[4,16,128]{2,1,0:T(8,128)(2,1)S(1)} %value.1.rest_6_), channel_id=1, source_target_pairs={{0,2},{2,0},{4,6},{6,4},{1,3},{3,1},{5,7},{7,5},{8,10},{10,8},{12,... | collective-permute-start | bytes 49160 | tf_op jit(solution)/shard_map/ppermute | solution.py:33
  48.0 3.7 %collective-permute-start.16 = (bf16[4,16,128]{2,1,0:T(8,128)(2,1)S(1)}, bf16[4,16,128]{2,1,0:T(8,128)(2,1)S(1)}, u32[]{:S(2)}, u32[]{:S(2)}) collective-permute-start(bf16[4,16,128]{2,1,0:T(8,128)(2,1)S(1)} %value.1.rest_6_), channel_id=1, source_target_pairs={{0,4},{2,6},{4,0},{6,2},{1,5},{3,7},{5,1},{7,3},{8,12},{10,14},{12... | collective-permute-start | bytes 49160 | tf_op jit(solution)/shard_map/ppermute | solution.py:33
  48.8 4.6 %collective-permute-start.14 = (bf16[4,16,128]{2,1,0:T(8,128)(2,1)S(1)}, bf16[4,16,128]{2,1,0:T(8,128)(2,1)S(1)}, u32[]{:S(2)}, u32[]{:S(2)}) collective-permute-start(bf16[4,16,128]{2,1,0:T(8,128)(2,1)S(1)} %value.1.rest_6_), channel_id=1, source_target_pairs={{0,6},{2,4},{4,2},{6,0},{1,7},{3,5},{5,3},{7,1},{8,14},{10,12},{12... | collective-permute-start | bytes 49160 | tf_op jit(solution)/shard_map/ppermute | solution.py:33
  50.0 3.4 %collective-permute-start.20 = (bf16[4,16,128]{2,1,0:T(8,128)(2,1)S(1)}, bf16[4,16,128]{2,1,0:T(8,128)(2,1)S(1)}, u32[]{:S(2)}, u32[]{:S(2)}) collective-permute-start(bf16[4,16,128]{2,1,0:T(8,128)(2,1)S(1)} %value.1.rest_6_), channel_id=1, source_target_pairs={{0,1},{1,0},{2,3},{3,2},{4,5},{5,4},{6,7},{7,6},{8,9},{9,8},{10,11... | collective-permute-start | bytes 49160 | tf_op jit(solution)/shard_map/ppermute | solution.py:33
  50.4 3.0 %collective-permute-start.19 = (bf16[4,16,128]{2,1,0:T(8,128)(2,1)S(1)}, bf16[4,16,128]{2,1,0:T(8,128)(2,1)S(1)}, u32[]{:S(2)}, u32[]{:S(2)}) collective-permute-start(bf16[4,16,128]{2,1,0:T(8,128)(2,1)S(1)} %collective-permute-done.18.rest_4_), channel_id=1, source_target_pairs={{0,1},{1,0},{2,3},{3,2},{4,5},{5,4},{6,7},{7,6},{8,9},{9,8},{10,11... | collective-permute-start | bytes 49160 | tf_op jit(solution)/shard_map/ppermute | solution.py:33
  51.8 1.6 %collective-permute-start.17 = (bf16[4,16,128]{2,1,0:T(8,128)(2,1)S(1)}, bf16[4,16,128]{2,1,0:T(8,128)(2,1)S(1)}, u32[]{:S(2)}, u32[]{:S(2)}) collective-permute-start(bf16[4,16,128]{2,1,0:T(8,128)(2,1)S(1)} %collective-permute-done.16.rest_2_), channel_id=1, source_target_pairs={{0,1},{1,0},{2,3},{3,2},{4,5},{5,4},{6,7},{7,6},{8,9},{9,8},{10,11... | collective-permute-start | bytes 49160 | tf_op jit(solution)/shard_map/ppermute | solution.py:33
  53.4 1.2 %collective-permute-start.15 = (bf16[4,16,128]{2,1,0:T(8,128)(2,1)S(1)}, bf16[4,16,128]{2,1,0:T(8,128)(2,1)S(1)}, u32[]{:S(2)}, u32[]{:S(2)}) collective-permute-start(bf16[4,16,128]{2,1,0:T(8,128)(2,1)S(1)} %collective-permute-done.14.rest_0_), channel_id=1, source_target_pairs={{0,1},{1,0},{2,3},{3,2},{4,5},{5,4},{6,7},{7,6},{8,9},{9,8},{10,11... | collective-permute-start | bytes 49160 | tf_op jit(solution)/shard_map/ppermute | solution.py:33

commit v4 on v3

--- a/solution.py
+++ b/solution.py
@@ -72,11 +72,17 @@
     return tile
 
 
-def absorb_kernel(dims, assign, new_pos, qn, qr, rate, w_hbm, *rest):
+def absorb_kernel(dims, assign, new_pos, rate, qn_hbm, qr_hbm, w_hbm, *rest):
     R, J, T, HC, DL = dims
-    outs, wbuf, sem = rest[:R], rest[R], rest[R + 1]
+    outs, wbuf, qn, qr, sem = rest[:R], *rest[R:]
     g, c = lax.axis_index("req"), lax.axis_index("core")
     piece = HC // 4
+    inputs = [
+        pltpu.make_async_copy(qn_hbm, qn, sem.at[4]),
+        pltpu.make_async_copy(qr_hbm, qr, sem.at[5]),
+    ]
+    for copy in inputs:
+        copy.start()
     copies = []
     for i in range(4):
         copies.append(
@@ -90,8 +96,6 @@
     tokens = [(k, j, t) for k in range(R) for j in range(J) for t in range(T)]
     who = [assign[(g ^ k) * J + j] for k, j, t in tokens]
     half = pl.ds(pl.multiple_of(c * HC, HC), HC)
-    x = jnp.stack([qn[t, who[i], half, :].astype(F32) for i, (k, j, t) in enumerate(tokens)])
-    x = jnp.swapaxes(x, 0, 1).astype(BF)
     row = lax.broadcasted_iota(jnp.int32, (len(tokens), DR), 0)
     pos = jnp.zeros((len(tokens), DR), jnp.int32)
     for i, (k, j, t) in enumerate(tokens):
@@ -99,11 +103,16 @@
     sine, cosine = sin_cos(pos * rate[...])
     lane = lax.broadcasted_iota(jnp.int32, (len(tokens), DR), 1)
     sine = jnp.where(lane < DR // 2, -sine, sine)
-    one = (lax.broadcasted_iota(jnp.int32, (HC, LANES - DR), 1) == 0).astype(F32)
+    lane = lax.broadcasted_iota(jnp.int32, (HC, LANES - DR), 1)
+    for copy in inputs:
+        copy.wait()
+    x = jnp.stack([qn[t, who[i], half, :].astype(F32) for i, (k, j, t) in enumerate(tokens)])
+    x = jnp.swapaxes(x, 0, 1).astype(BF)
     for i, (k, j, t) in enumerate(tokens):
         v = qr[t, who[i], half, :].astype(F32)
         swapped = jnp.concatenate([v[:, DR // 2 :], v[:, : DR // 2]], axis=1)
         turned = v * cosine[i : i + 1] + swapped * sine[i : i + 1]
+        one = ((lane == 0) | ((lane > t) & (lane < T))).astype(F32)
         outs[k][j, t, :, DL:] = jnp.concatenate([turned, one], axis=1).astype(BF)
     ys = []
     for h in range(HC):
@@ -115,8 +124,11 @@
         outs[k][j, t, :, :DL] = y[i]
 
 
-def prepare_kernel(dims, cuts, assign, lengths, pos, rope, rate, c_hbm, out, c_out, sem):
-    J, CAP = dims
+def prepare_kernel(
+    dims, cuts, assign, lengths, new_pos, new_lat, new_rope, rate_row,
+    pos, rope, rate, c_hbm, out, c_out, sem,
+):
+    J, T, CAP, DL = dims
     g = lax.axis_index("req")
     shard = lax.axis_index("chip") * lax.axis_size("core") + lax.axis_index("core")
     half = DR // 2
@@ -146,39 +158,6 @@
             return carry
 
         lax.fori_loop(0, cuts, rotate, 0)
-    for copy in copies:
-        copy.wait()
-
-
-def attend_kernel(
-    dims, B, assign, new_pos, new_lat, new_rope, rate, keys, cbuf, *rest
-):
-    R, J, T, HC, DL, CAP = dims
-    own, other = rest[:R][::-1], rest[R : 2 * R][::-1]
-    send, keep, q, sbuf, acc = rest[2 * R :]
-    nb = CAP // B
-    NQ = T * R * 2 * HC
-    g, c = lax.axis_index("req"), lax.axis_index("core")
-    first_shard = (lax.axis_index("chip") == 0) & (c == 0)
-
-    for j in range(J):
-        for t in range(T):
-            for k in range(R):
-                mine, theirs = own[k][j, t], other[k][j, t]
-                base = (t * R + k) * 2 * HC
-                q[j, base : base + HC, :] = jnp.where(c == 0, mine, theirs)
-                q[j, base + HC : base + 2 * HC, :] = jnp.where(c == 0, theirs, mine)
-    nt = (((1,), (1,)), ((), ()))
-
-    def score(j, i):
-        rows = pl.ds(i * B, B)
-        return lax.dot_general(
-            q[j, :, :DL], cbuf[j, rows], nt, preferred_element_type=F32
-        ) + jnp.dot(
-            q[j, :, DL : DL + KEYS], keys[j, :, rows], preferred_element_type=F32
-        )
-
-    sbuf[0] = score(0, 0)
     for j in range(J):
         r = assign[g * J + j]
         pick = lax.broadcasted_iota(jnp.int32, new_lat.shape[1:], 0) == r
@@ -191,48 +170,93 @@
             jnp.sum(jnp.where(pick, new_rope[u].astype(F32), 0.0), axis=0, keepdims=True)
             for u in range(T)
         ]
-        lat = jnp.concatenate(lat + [jnp.zeros((LANES - T, DL), F32)], axis=0).astype(BF)
+        lat = jnp.concatenate(lat + [jnp.zeros((LANES - T, DL), F32)], axis=0)
+        c_out[j, CAP:, :] = lat.astype(BF)
         rop = jnp.concatenate(rop + [jnp.zeros((8 - T, DR), F32)], axis=0)
         step = lax.broadcasted_iota(jnp.int32, (8, DR), 0)
         lane = lax.broadcasted_iota(jnp.int32, (8, DR), 1)
-        sine, cosine = sin_cos((new_pos[r] + step) * rate[:8])
+        sine, cosine = sin_cos((new_pos[r] + step) * rate_row[:8])
         sine = jnp.where(lane < DR // 2, -sine, sine)
         swapped = jnp.concatenate([rop[:, DR // 2 :], rop[:, : DR // 2]], axis=1)
         rop = rop * cosine + swapped * sine
-        rop = jnp.concatenate([rop, jnp.zeros((8, LANES - DR), F32)], axis=1)
-        rop = jnp.concatenate([rop, jnp.zeros((LANES - 8, LANES), F32)], axis=0).astype(BF)
-        s = lax.dot_general(q[j, :, :DL], lat, nt, preferred_element_type=F32)
-        s = s + lax.dot_general(q[j, :, DL:], rop, nt, preferred_element_type=F32)
-        u = lax.broadcasted_iota(jnp.int32, (NQ, LANES), 1)
-        t_of = lax.broadcasted_iota(jnp.int32, (NQ, LANES), 0) // (NQ // T)
-        valid = (u <= t_of) & (u < T) & first_shard
-        m = jnp.max(jnp.where(valid, s, LOW), axis=1, keepdims=True)
-        p = jnp.where(valid, jnp.exp2(s * EXPO - m * EXPO), 0.0)
-        l = jnp.sum(p, axis=1, keepdims=True)
-        acc[j] = jnp.dot(p.astype(BF), lat, preferred_element_type=F32)
-        for i in range(nb):
-            at = j * nb + i
-            if at + 1 < J * nb:
-                sbuf[(at + 1) % 2] = score((at + 1) // nb, (at + 1) % nb)
-            s = sbuf[at % 2]
-            top = jnp.maximum(m, jnp.max(s, axis=1, keepdims=True))
+        rop = jnp.concatenate([rop, jnp.zeros((LANES - 8, DR), F32)], axis=0)
+        u = lax.broadcasted_iota(jnp.int32, (LANES, LANES - DR), 0)
+        lane = lax.broadcasted_iota(jnp.int32, (LANES, LANES - DR), 1)
+        absent = (lane == 0) & ((u >= T) | (shard > 0))
+        later = (lane > 0) & (lane == u) & (u < T)
+        rop = jnp.concatenate([rop, jnp.where(absent | later, LOW, 0.0)], axis=1)
+        out[j, :, CAP:] = jnp.transpose(rop)[:KEYS].astype(BF)
+    for copy in copies:
+        copy.wait()
+
+
+def units(R, c):
+    found = [(0, c), (R - 1, c)]
+    for i in range(1, R // 2):
+        found += [(2 * i - c, 0), (2 * i - c, 1)]
+    return found
+
+
+def attend_kernel(dims, B, keys, cbuf, *rest):
+    R, J, T, HC, DL, CAP = dims
+    own, other = rest[:R][::-1], rest[R : 2 * R][::-1]
+    send, keep, q, sbuf, acc = rest[2 * R :]
+    nb = CAP // B
+    NQ = T * R * 2 * HC
+    c = lax.axis_index("core")
+    for j in range(J):
+        for t in range(T):
+            for k in range(R):
+                mine, theirs = own[k][j, t], other[k][j, t]
+                base = (t * R + k) * 2 * HC
+                q[j, base : base + HC, :] = jnp.where(c == 0, mine, theirs)
+                q[j, base + HC : base + 2 * HC, :] = jnp.where(c == 0, theirs, mine)
+    nt = (((1,), (1,)), ((), ()))
+    blocks = [
+        (j, pl.ds(i * B, B + (LANES if i == nb - 1 else 0))) for j in range(J) for i in range(nb)
+    ]
+
+    def score(n):
+        j, rows = blocks[n]
+        s = lax.dot_general(q[j, :, :DL], cbuf[j, rows], nt, preferred_element_type=F32)
+        s = s + jnp.dot(
+            q[j, :, DL : DL + KEYS], keys[j, :, rows], preferred_element_type=F32
+        )
+        sbuf[n % 2, :, : rows.size] = s
+
+    score(0)
+    for n, (j, rows) in enumerate(blocks):
+        if n + 1 < len(blocks):
+            score(n + 1)
+        s = sbuf[n % 2, :, : rows.size]
+        top = jnp.max(s, axis=1, keepdims=True)
+        if n % nb:
+            top = jnp.maximum(m, top)
+        p = jnp.exp2(s * EXPO - top * EXPO)
+        part = jnp.sum(p, axis=1, keepdims=True)
+        value = jnp.dot(p.astype(BF), cbuf[j, rows], preferred_element_type=F32)
+        if n % nb:
             shrink = jnp.exp2((m - top) * EXPO)
-            p = jnp.exp2(s * EXPO - top * EXPO)
-            l = l * shrink + jnp.sum(p, axis=1, keepdims=True)
-            acc[j] = acc[j] * shrink + jnp.dot(
-                p.astype(BF), cbuf[j, pl.ds(i * B, B)], preferred_element_type=F32
-            )
-            m = top
+            l = l * shrink + part
+            acc[j] = acc[j] * shrink + value
+        else:
+            l = part
+            acc[j] = value
+        m = top
+        if n % nb < nb - 1:
+            continue
         whole = stat_lanes(NQ, (m, l))
         parts = stat_lanes(NQ, split3(m) + split3(l))
         for t in range(T):
-            for k in range(R):
-                base = (t * R + k) * 2 * HC
-                lo, hi = slice(base, base + HC), slice(base + HC, base + 2 * HC)
-                keep[j, t, k, :, :DL] = jnp.where(c == 0, acc[j, lo], acc[j, hi])
-                send[j, t, k, :, :DL] = jnp.where(c == 0, acc[j, hi], acc[j, lo]).astype(BF)
-                keep[j, t, k, :, DL:] = jnp.where(c == 0, whole[lo], whole[hi])
-                send[j, t, k, :, DL:] = jnp.where(c == 0, parts[hi], parts[lo]).astype(BF)
+            for slot in range(R):
+                lo, hi = [
+                    slice((t * R + k) * 2 * HC + h * HC, (t * R + k) * 2 * HC + (h + 1) * HC)
+                    for k, h in (units(R, 0)[slot], units(R, 1)[slot])
+                ]
+                keep[j, t, slot, :, :DL] = jnp.where(c == 0, acc[j, lo], acc[j, hi])
+                send[j, t, slot, :, :DL] = jnp.where(c == 0, acc[j, hi], acc[j, lo]).astype(BF)
+                keep[j, t, slot, :, DL:] = jnp.where(c == 0, whole[lo], whole[hi])
+                send[j, t, slot, :, DL:] = jnp.where(c == 0, parts[hi], parts[lo]).astype(BF)
 
 
 def stats_of(x, DL):
@@ -270,27 +294,39 @@
 
 
 def combine_kernel(dims, *rest):
-    R, HB, DL = dims
-    outs = rest[len(rest) - R :]
-    *got, own = rest[: len(rest) - R]
+    CH, DL = dims
+    outs = rest[CH:]
+    *got, own = rest[:CH]
     x = [own[...]] + [v[...].astype(F32) for v in got]
     ms, ls = zip(*[(x[0][:, DL : DL + 1], x[0][:, DL + 1 : DL + 2])] + [stats_of(v, DL) for v in x[1:]])
     m = functools.reduce(jnp.maximum, ms)
     ws = [jnp.exp2((v - m) * EXPO) for v in ms]
     total = sum(w_ * l for w_, l in zip(ws, ls))
     o = (sum(w_ * v[:, :DL] for w_, v in zip(ws, x)) / total).astype(BF)
-    for k in range(R):
-        outs[k][...] = o[k * HB : (k + 1) * HB]
+    at = 0
+    for out in outs:
+        out[...] = o[at : at + out.shape[0]]
+        at += out.shape[0]
 
 
 def value_kernel(dims, w, *rest):
     R, HC, HS, HB = dims
-    got, out = rest[:R][::-1], rest[R]
-    first = lax.axis_index("core") * HC + lax.rem(lax.axis_index("chip"), HS) * HB
-    x = jnp.stack([v[...].astype(F32) for v in got])
-    x = jnp.swapaxes(x, 0, 1).astype(BF)
-    ys = [jnp.dot(x[h], w[first + h], preferred_element_type=F32) for h in range(HB)]
-    out[...] = jnp.swapaxes(jnp.stack(ys), 0, 1).astype(BF)
+    n = R // 2 - 1
+    far, *pairs, near, out = rest
+    pairs = pairs[::-1]
+    c = lax.axis_index("core")
+    part = lax.rem(lax.axis_index("chip"), HS)
+    ys = []
+    for h in range(2):
+        x = [v[...] for v in (near, far)] + [v[h * HB : (h + 1) * HB] for v in pairs]
+        x = jnp.swapaxes(jnp.stack([v.astype(F32) for v in x]), 0, 1).astype(BF)
+        first = h * HC + part * HB
+        y = [jnp.dot(x[e], w[first + e], preferred_element_type=F32) for e in range(HB)]
+        ys.append(jnp.swapaxes(jnp.stack(y), 0, 1).astype(BF))
+        for i in range(n):
+            out[2 + 2 * i + h] = ys[h][2 + i]
+    for slot in range(2):
+        out[slot] = jnp.where(c == 0, ys[0][slot], ys[1][slot])
 
 
 def place_kernel(dims, assign, *rest):
@@ -302,18 +338,21 @@
         j, t = token // T, lax.rem(token, T)
         for b in range(2):
             block = blocks[2 * (CH - 1 - n) + b]
-            first = (c ^ b) * HC + lax.rem(chip ^ n, HS) * HB
-            for k in range(R):
+            core, part = c ^ b, lax.rem(chip ^ n, HS)
+            for slot in range(R):
+                (k, h), (k1, h1) = units(R, 0)[slot], units(R, 1)[slot]
+                k = k + core * (k1 - k)
+                first = (h + core * (h1 - h)) * HC + part * HB
                 request = assign[(g ^ k) * J + j]
                 if HS == 1:
                     rows = pl.ds(pl.multiple_of(first, HB), HB)
-                    out[t, request, rows, :] = block[k]
+                    out[t, request, rows, :] = block[slot]
                     continue
                 for at in range(0, 2 * HC, HB):
 
                     @pl.when(first == at)
                     def _():
-                        out[t, request, at : at + HB, :] = block[k]
+                        out[t, request, at : at + HB, :] = block[slot]
 
 
 def body(
@@ -337,23 +376,28 @@
     blocks = pl.pallas_call(
         functools.partial(absorb_kernel, (R, J, T, HC, DL)),
         out_shape=[jax.ShapeDtypeStruct((J, T, HC, W), BF)] * R,
-        in_specs=[SMEM, SMEM, VMEM, VMEM, VMEM, HBM],
+        in_specs=[SMEM, SMEM, VMEM, HBM, HBM, HBM],
         out_specs=[VMEM] * R,
-        scratch_shapes=[pltpu.VMEM((HC, DN, DL), BF), pltpu.SemaphoreType.DMA((4,))],
+        scratch_shapes=[
+            pltpu.VMEM((HC, DN, DL), BF),
+            pltpu.VMEM(q_nope.shape, BF),
+            pltpu.VMEM(q_rope.shape, BF),
+            pltpu.SemaphoreType.DMA((6,)),
+        ],
         compiler_params=big,
         name="absorb",
-    )(assignment, new_pos, in_hbm(q_nope), in_hbm(q_rope), in_hbm(rate_row), in_hbm(w_uk))
+    )(assignment, new_pos, in_hbm(rate_row), in_hbm(q_nope), in_hbm(q_rope), in_hbm(w_uk))
     arrived = hops(blocks, "req")
     near = hop(blocks[0], "core", 1)
 
     cuts = CAP // 512
     keys, cached = pl.pallas_call(
-        functools.partial(prepare_kernel, (J, CAP), cuts),
+        functools.partial(prepare_kernel, (J, T, CAP, DL), cuts),
         out_shape=[
-            jax.ShapeDtypeStruct((J, KEYS, CAP), BF),
-            jax.ShapeDtypeStruct((J, CAP, DL), BF),
+            jax.ShapeDtypeStruct((J, KEYS, CAP + LANES), BF),
+            jax.ShapeDtypeStruct((J, CAP + LANES, DL), BF),
         ],
-        in_specs=[SMEM, SMEM, VMEM, VMEM, VMEM, HBM],
+        in_specs=[SMEM, SMEM, SMEM] + [VMEM] * 6 + [HBM],
         out_specs=[VMEM, VMEM],
         scratch_shapes=[pltpu.SemaphoreType.DMA((J, cuts))],
         compiler_params=pltpu.CompilerParams(vmem_limit_bytes=8 << 20),
@@ -361,7 +405,10 @@
             flops=0, bytes_accessed=4 * J * CAP * DL, transcendentals=0
         ),
         name="prepare",
-    )(assignment, lengths, positions, jnp.swapaxes(rope_cache, 1, 2), rate_col, in_hbm(latent_cache))
+    )(
+        assignment, lengths, new_pos, new_latent, new_rope, rate_row,
+        positions, jnp.swapaxes(rope_cache, 1, 2), rate_col, in_hbm(latent_cache),
+    )
 
     arrived, keys, cached = lax.optimization_barrier((arrived, keys, cached))
     own = arrived + [blocks[0]]
@@ -375,16 +422,16 @@
             jax.ShapeDtypeStruct((J, T, R, HC, W), BF),
             jax.ShapeDtypeStruct((J, T, R, HC, W), F32),
         ],
-        in_specs=[SMEM, SMEM] + [VMEM] * (5 + 2 * R),
+        in_specs=[VMEM] * (2 + 2 * R),
         out_specs=[VMEM, VMEM],
         scratch_shapes=[
             pltpu.VMEM((J, NQ, W), BF),
-            pltpu.VMEM((2, NQ, B), F32),
+            pltpu.VMEM((2, NQ, B + LANES), F32),
             pltpu.VMEM((J, NQ, DL), F32),
         ],
         compiler_params=pltpu.CompilerParams(vmem_limit_bytes=16 << 20),
         name="attend",
-    )(assignment, new_pos, new_latent, new_rope, rate_row, keys, cached, *own, *other)
+    )(keys, cached, *own, *other)
     got = hop(send, "core", 1)
     pieces = pl.pallas_call(
         functools.partial(pair_kernel, (R, J, T, HC, HS, CH, DL)),
@@ -395,19 +442,30 @@
         name="pair",
     )(keep, got)
     shares = hops(pieces, "chip") + [pieces[0]]
+    sizes = [HB, HB] + [2 * HB] * (R // 2 - 1)
     latents = pl.pallas_call(
-        functools.partial(combine_kernel, (R, HB, DL)),
-        out_shape=[jax.ShapeDtypeStruct((HB, DL), BF)] * R,
+        functools.partial(combine_kernel, (CH, DL)),
+        out_shape=[jax.ShapeDtypeStruct((n, DL), BF) for n in sizes],
         in_specs=[VMEM] * CH,
-        out_specs=[VMEM] * R,
+        out_specs=[VMEM] * len(sizes),
         compiler_params=big,
         name="combine",
     )(*shares)
-    returned = hops(latents, "req") + [latents[0]]
+    far = hop(latents[1], "req", R - 1)
+    crossed = [
+        lax.ppermute(
+            latents[1 + i],
+            ("req", "core"),
+            [(2 * g + c, 2 * (g ^ (2 * i - c)) + c) for g in range(R) for c in range(2)],
+        )
+        for i in reversed(range(1, R // 2))
+    ]
+    returned = [far] + crossed + [latents[0]]
+
     values = pl.pallas_call(
         functools.partial(value_kernel, (R, HC, HS, HB)),
         out_shape=jax.ShapeDtypeStruct((R, HB, DV), BF),
-        in_specs=[VMEM] * (1 + R),
+        in_specs=[VMEM] * (1 + len(returned)),
         out_specs=VMEM,
         compiler_params=big,
         name="value",

time: 56.2 us -> 54.4 us (0.968)
  Pallas kernels: 22.3 us -> 21.1 us
  starting transfers between devices: 18.2 us -> 17.3 us
    ppermute x21 -> x19, starting transfers between devices: 18.2 us -> 15.4 us  [hop(): return lax.ppermute(x, axis, [(i, i ^ n) for i in range(size)])]
    ppermute x0 -> x1, starting transfers between devices: none -> 1.91 us  [body(): lax.ppermute(latents[1 + i], ('req', 'core'), [(2 * g + c, 2 * (g ^ 2 * i...]
    pallas_call x1, Pallas kernels: 10.9 us -> 9.7 us  [body(): pl.pallas_call(functools.partial(attend_kernel, (R, J, T, HC, DL, CAP), B...]
    ppermute x21 -> x19, waiting for transfers between devices: 15.4 us -> 15.6 us  [hop(): return lax.ppermute(x, axis, [(i, i ^ n) for i in range(size)])]
  transfers between devices with their start and end apart: 21 -> 20, of which waited for: 14 -> 13; matrix products, arithmetic and copies ran while one was open for 0% -> 0% of each run, Pallas kernels for 10% -> 10%
where the time goes in v4:
time: 54.4 us; the launch traced here: 54.2 us
  Pallas kernels  21.1 us (39%)
  starting transfers between devices  17.3 us (32%)
  waiting for transfers between devices  15.6 us (29%)
    ppermute x19, waiting for transfers between devices, hop(): return lax.ppermute(x, axis, [(i, i ^ n) for i in range(size)])  15.6 us
    ppermute x19, starting transfers between devices, hop(): return lax.ppermute(x, axis, [(i, i ^ n) for i in range(size)])  15.4 us
    pallas_call x1, Pallas kernels, body(): pl.pallas_call(functools.partial(attend_kernel, (R, J, T, HC, DL, CAP), B...  9.7 us
    pallas_call x1, Pallas kernels, body(): pl.pallas_call(functools.partial(prepare_kernel, (J, T, CAP, DL), cuts),...  5.47 us
    pallas_call x1, Pallas kernels, body(): pl.pallas_call(functools.partial(absorb_kernel, (R, J, T, HC, DL)), out_s...  2.84 us
    ppermute x1, starting transfers between devices, body(): lax.ppermute(latents[1 + i], ('req', 'core'), [(2 * g + c, 2 * (g ^ 2 * i...  1.91 us
    pallas_call x1, Pallas kernels, body(): pl.pallas_call(functools.partial(place_kernel, (R, J, T, HC, HS, HB, CH))...  1.42 us
  transfers between devices with their start and end apart: 20, of which 13 were waited for; matrix products, arithmetic and copies ran while one was open for 0% of the time, Pallas kernels for 10%

profile of v4, /device:TPU:0, one launch (start us, length us, event | category | flops | bytes accessed | tf_op | source)
XLA Modules:
  0.0 54.2 jit_solution(2448644199555946373)
XLA Ops:
  0.0 0.0 copy-start.3
  0.0 0.0 copy-start.5
  0.0 0.0 copy-start.6
  0.0 0.0 copy-start.4
  0.0 0.0 copy-start.2
  0.0 0.0 copy-start.1
  0.0 2.8 %absorb.1 = (bf16[2,2,16,640]{3,2,1,0:T(8,128)(2,1)S(1)}, bf16[2,2,16,640]{3,2,1,0:T(8,128)(2,1)S(1)}, bf16[2,2,16,640]{3,2,1,0:T(8,128)(2,1)S(1)}, bf16[2,2,16,640]{3,2,1,0:T(8,128)(2,1)S(1)}) custom-call(s32[8]{0:T(128)} %assign.5, s32[8]{0:T(128)} %new_pos.3, s32[16,64]{1,0:T(8,128)} %constant.4.clone.rate.rate_row, bf16[2,8,32,128]{3,2,1,0:T(8,128)(2,1)} %qn_hbm.1, ...), custom_call_target="tpu_custom_call" | custom-call | tf_op jit(solution)/shard_map/absorb/pallas_call | solution.py:376
  2.9 5.1 %collective-permute-start = (bf16[2,2,16,640]{3,2,1,0:T(8,128)(2,1)S(1)}, bf16[2,2,16,640]{3,2,1,0:T(8,128)(2,1)S(1)}, u32[]{:S(2)}, u32[]{:S(2)}) collective-permute-start(bf16[2,2,16,640]{3,2,1,0:T(8,128)(2,1)S(1)} %get-tuple-element.25), channel_id=1, source_target_pairs={{0,24},{8,16},{16,8},{24,0},{1,25},{9,17},{17,9},{25,1},{2,26},{10... | collective-permute-start | bytes 245768 | tf_op jit(solution)/shard_map/ppermute | solution.py:33
  8.0 0.0 collective-permute-start.1
  8.0 0.6 %collective-permute-start.2 = (bf16[2,2,16,640]{3,2,1,0:T(8,128)(2,1)S(1)}, bf16[2,2,16,640]{3,2,1,0:T(8,128)(2,1)S(1)}, u32[]{:S(2)}, u32[]{:S(2)}) collective-permute-start(bf16[2,2,16,640]{3,2,1,0:T(8,128)(2,1)S(1)} %get-tuple-element.27), channel_id=1, source_target_pairs={{0,8},{8,0},{16,24},{24,16},{1,9},{9,1},{17,25},{25,17},{2,10},{10... | collective-permute-start | bytes 245768 | tf_op jit(solution)/shard_map/ppermute | solution.py:33
  8.6 0.0 collective-permute-start.6
  8.6 0.0 copy-done.3
  8.7 0.0 copy-done.5
  8.7 0.0 copy-done.6
  8.7 0.0 copy-done.4
  8.7 0.0 copy-done.2
  8.7 0.0 copy-done.1
  8.7 5.5 %prepare.1 = (bf16[2,80,6272]{2,1,0:T(8,128)(2,1)S(1)}, bf16[2,6272,512]{2,1,0:T(8,128)(2,1)S(1)}) custom-call(s32[8]{0:T(128)} %assign.5, s32[8]{0:T(128)} %lengths.1, s32[8]{0:T(128)} %new_pos.3, bf16[2,8,512]{2,1,0:T(8,128)(2,1)S(1)} %copy-done.4, bf16[2,8,64]{2,1,0:T(8,128)(2,1)S(1)} %copy-done.6, s32[16,64]{1,0:T(8,128)S(1)} %copy-done.3, ...), custom_call_target="tpu_custom_call" | custom-call | bytes 25165824 | tf_op jit(solution)/shard_map/prepare/pallas_call | solution.py:394
  14.2 0.0 collective-permute-done.rest_0_
  14.2 0.7 %collective-permute-done.1.rest_1_ = bf16[2,2,16,640]{3,2,1,0:T(8,128)(2,1)S(1)} collective-permute-done((bf16[2,2,16,640]{3,2,1,0:T(8,128)(2,1)S(1)}, bf16[2,2,16,640]{3,2,1,0:T(8,128)(2,1)S(1)}, u32[]{:S(2)}, u32[]{:S(2)}) %collective-permute-start.1) | collective-permute-done | bytes 81952 | tf_op jit(solution)/shard_map/ppermute | solution.py:33
  14.9 0.0 collective-permute-done.2.rest_2_
  14.9 0.0 collective-permute-start.3
  14.9 0.5 collective-permute-start.4
  15.4 0.0 collective-permute-start.5
  15.4 0.0 collective-permute-done.6.rest_7_
  15.4 0.8 %collective-permute-done.3.rest_4_ = bf16[2,2,16,640]{3,2,1,0:T(8,128)(2,1)S(1)} collective-permute-done((bf16[2,2,16,640]{3,2,1,0:T(8,128)(2,1)S(1)}, bf16[2,2,16,640]{3,2,1,0:T(8,128)(2,1)S(1)}, u32[]{:S(2)}, u32[]{:S(2)}) %collective-permute-start.3) | collective-permute-done | bytes 81952 | tf_op jit(solution)/shard_map/ppermute | solution.py:33
  16.1 0.2 collective-permute-done.4.rest_5_
  16.3 0.4 collective-permute-done.5.rest_6_
  16.7 0.0 copy-start
  16.7 9.7 %attend.1 = (bf16[2,2,4,16,640]{4,3,2,1,0:T(8,128)(2,1)S(1)}, f32[2,2,4,16,640]{4,3,2,1,0:T(8,128)S(1)}) custom-call(bf16[2,80,6272]{2,1,0:T(8,128)(2,1)S(1)} %get-tuple-element.30.keys, bf16[2,6272,512]{2,1,0:T(8,128)(2,1)S(1)} %get-tuple-element.31.cbuf, bf16[2,2,16,640]{3,2,1,0:T(8,128)(2,1)S(1)} %collective-permute-done.rest_0_, ...), custom_call_target="tpu_custom_call" | custom-call | tf_op jit(solution)/shard_map/attend/pallas_call | solution.py:419
  26.4 0.2 collective-permute-start.7
  26.6 1.5 %collective-permute-done.7.got = bf16[2,2,4,16,640]{4,3,2,1,0:T(8,128)(2,1)S(1)} collective-permute-done((bf16[2,2,4,16,640]{4,3,2,1,0:T(8,128)(2,1)S(1)}, bf16[2,2,4,16,640]{4,3,2,1,0:T(8,128)(2,1)S(1)}, u32[]{:S(2)}, u32[]{:S(2)}) %collective-permute-start.7) | collective-permute-done | bytes 327712 | tf_op jit(solution)/shard_map/ppermute | solution.py:33
  28.1 0.8 %pair.1 = (f32[64,640]{1,0:T(8,128)S(1)}, bf16[64,640]{1,0:T(8,128)(2,1)S(1)}, bf16[64,640]{1,0:T(8,128)(2,1)S(1)}, bf16[64,640]{1,0:T(8,128)(2,1)S(1)}) custom-call(f32[2,2,4,16,640]{4,3,2,1,0:T(8,128)S(1)} %get-tuple-element.36.keep, bf16[2,2,4,16,640]{4,3,2,1,0:T(8,128)(2,1)S(1)} %collective-permute-done.7.got), custom_call_target="tpu_custom_call" | custom-call | tf_op jit(solution)/shard_map/pair/pallas_call | solution.py:436
  28.8 2.5 %collective-permute-start.8 = (bf16[64,640]{1,0:T(8,128)(2,1)S(1)}, bf16[64,640]{1,0:T(8,128)(2,1)S(1)}, u32[]{:S(2)}, u32[]{:S(2)}) collective-permute-start(bf16[64,640]{1,0:T(8,128)(2,1)S(1)} %get-tuple-element.38), channel_id=1, source_target_pairs={{0,6},{2,4},{4,2},{6,0},{1,7},{3,5},{5,3},{7,1},{8,14},{10,12},{12... | collective-permute-start | bytes 245768 | tf_op jit(solution)/shard_map/ppermute | solution.py:33
  31.3 0.5 collective-permute-start.9
  31.8 0.5 collective-permute-start.10
  32.4 2.0 %collective-permute-done.8.rest_0_ = bf16[64,640]{1,0:T(8,128)(2,1)S(1)} collective-permute-done((bf16[64,640]{1,0:T(8,128)(2,1)S(1)}, bf16[64,640]{1,0:T(8,128)(2,1)S(1)}, u32[]{:S(2)}, u32[]{:S(2)}) %collective-permute-start.8) | collective-permute-done | bytes 81952 | tf_op jit(solution)/shard_map/ppermute | solution.py:33
  34.3 1.7 %collective-permute-done.9.rest_1_ = bf16[64,640]{1,0:T(8,128)(2,1)S(1)} collective-permute-done((bf16[64,640]{1,0:T(8,128)(2,1)S(1)}, bf16[64,640]{1,0:T(8,128)(2,1)S(1)}, u32[]{:S(2)}, u32[]{:S(2)}) %collective-permute-start.9) | collective-permute-done | bytes 81952 | tf_op jit(solution)/shard_map/ppermute | solution.py:33
  36.0 0.2 collective-permute-done.10.rest_2_
  36.3 0.2 combine.1
  36.5 1.9 %collective-permute-start.12 = (bf16[32,512]{1,0:T(8,128)(2,1)S(1)}, bf16[32,512]{1,0:T(8,128)(2,1)S(1)}, u32[]{:S(2)}, u32[]{:S(2)}) collective-permute-start(bf16[32,512]{1,0:T(8,128)(2,1)S(1)} %get-tuple-element.43), channel_id=1, source_target_pairs={{0,16},{1,9},{8,24},{9,1},{16,0},{17,25},{24,8},{25,17},{2,18},{3,... | collective-permute-start | bytes 98312 | tf_op jit(solution)/shard_map/ppermute | solution.py:456
  38.5 1.5 %collective-permute-start.11 = (bf16[16,512]{1,0:T(8,128)(2,1)S(1)}, bf16[16,512]{1,0:T(8,128)(2,1)S(1)}, u32[]{:S(2)}, u32[]{:S(2)}) collective-permute-start(bf16[16,512]{1,0:T(8,128)(2,1)S(1)} %get-tuple-element.42), channel_id=1, source_target_pairs={{0,24},{8,16},{16,8},{24,0},{1,25},{9,17},{17,9},{25,1},{2,26},{10... | collective-permute-start | bytes 49160 | tf_op jit(solution)/shard_map/ppermute | solution.py:33
  40.0 4.0 %collective-permute-done.11.rest_0_ = bf16[16,512]{1,0:T(8,128)(2,1)S(1)} collective-permute-done((bf16[16,512]{1,0:T(8,128)(2,1)S(1)}, bf16[16,512]{1,0:T(8,128)(2,1)S(1)}, u32[]{:S(2)}, u32[]{:S(2)}) %collective-permute-start.11) | collective-permute-done | bytes 16416 | tf_op jit(solution)/shard_map/ppermute | solution.py:33
  44.0 0.0 collective-permute-done.12.rest_1_
  44.0 0.0 copy-done
  44.0 0.7 %value.1.rest_6_ = bf16[4,16,128]{2,1,0:T(8,128)(2,1)S(1)} custom-call(bf16[32,512,128]{2,1,0:T(8,128)(2,1)S(1)} %copy-done, bf16[16,512]{1,0:T(8,128)(2,1)S(1)} %collective-permute-done.11.rest_0_, bf16[32,512]{1,0:T(8,128)(2,1)S(1)} %collective-permute-done.12.rest_1_, bf16[16,512]{1,0:T(8,128)(2,1)S(1)} %get-tuple-element.44.rest_2_), custom_call_target="tpu_custom_call" | custom-call | tf_op jit(solution)/shard_map/value/pallas_call | solution.py:465
  44.7 1.6 %collective-permute-start.17 = (bf16[4,16,128]{2,1,0:T(8,128)(2,1)S(1)}, bf16[4,16,128]{2,1,0:T(8,128)(2,1)S(1)}, u32[]{:S(2)}, u32[]{:S(2)}) collective-permute-start(bf16[4,16,128]{2,1,0:T(8,128)(2,1)S(1)} %value.1.rest_6_), channel_id=1, source_target_pairs={{0,2},{2,0},{4,6},{6,4},{1,3},{3,1},{5,7},{7,5},{8,10},{10,8},{12,... | collective-permute-start | bytes 49160 | tf_op jit(solution)/shard_map/ppermute | solution.py:33
  46.3 0.7 %collective-permute-start.15 = (bf16[4,16,128]{2,1,0:T(8,128)(2,1)S(1)}, bf16[4,16,128]{2,1,0:T(8,128)(2,1)S(1)}, u32[]{:S(2)}, u32[]{:S(2)}) collective-permute-start(bf16[4,16,128]{2,1,0:T(8,128)(2,1)S(1)} %value.1.rest_6_), channel_id=1, source_target_pairs={{0,4},{2,6},{4,0},{6,2},{1,5},{3,7},{5,1},{7,3},{8,12},{10,14},{12... | collective-permute-start | bytes 49160 | tf_op jit(solution)/shard_map/ppermute | solution.py:33
  47.0 1.2 %collective-permute-start.13 = (bf16[4,16,128]{2,1,0:T(8,128)(2,1)S(1)}, bf16[4,16,128]{2,1,0:T(8,128)(2,1)S(1)}, u32[]{:S(2)}, u32[]{:S(2)}) collective-permute-start(bf16[4,16,128]{2,1,0:T(8,128)(2,1)S(1)} %value.1.rest_6_), channel_id=1, source_target_pairs={{0,6},{2,4},{4,2},{6,0},{1,7},{3,5},{5,3},{7,1},{8,14},{10,12},{12... | collective-permute-start | bytes 49160 | tf_op jit(solution)/shard_map/ppermute | solution.py:33
  48.2 0.0 collective-permute-start.19
  48.2 0.2 collective-permute-done.17.rest_4_
  48.5 0.3 collective-permute-start.18
  48.7 1.3 %collective-permute-done.15.rest_2_ = bf16[4,16,128]{2,1,0:T(8,128)(2,1)S(1)} collective-permute-done((bf16[4,16,128]{2,1,0:T(8,128)(2,1)S(1)}, bf16[4,16,128]{2,1,0:T(8,128)(2,1)S(1)}, u32[]{:S(2)}, u32[]{:S(2)}) %collective-permute-start.15) | collective-permute-done | bytes 16416 | tf_op jit(solution)/shard_map/ppermute | solution.py:33
  50.0 0.0 collective-permute-start.16
  50.0 1.6 %collective-permute-done.13.rest_0_ = bf16[4,16,128]{2,1,0:T(8,128)(2,1)S(1)} collective-permute-done((bf16[4,16,128]{2,1,0:T(8,128)(2,1)S(1)}, bf16[4,16,128]{2,1,0:T(8,128)(2,1)S(1)}, u32[]{:S(2)}, u32[]{:S(2)}) %collective-permute-start.13) | collective-permute-done | bytes 16416 | tf_op jit(solution)/shard_map/ppermute | solution.py:33
  51.6 0.0 collective-permute-start.14
  51.6 0.0 collective-permute-done.19.rest_7_
  51.6 0.0 collective-permute-done.18.rest_5_
  51.6 0.0 collective-permute-done.16.rest_3_
  51.7 1.2 %collective-permute-done.14.rest_1_ = bf16[4,16,128]{2,1,0:T(8,128)(2,1)S(1)} collective-permute-done((bf16[4,16,128]{2,1,0:T(8,128)(2,1)S(1)}, bf16[4,16,128]{2,1,0:T(8,128)(2,1)S(1)}, u32[]{:S(2)}, u32[]{:S(2)}) %collective-permute-start.14) | collective-permute-done | bytes 16416 | tf_op jit(solution)/shard_map/ppermute | solution.py:33
  52.8 1.4 %place.1 = bf16[2,8,32,128]{3,2,1,0:T(8,128)(2,1)} custom-call(s32[8]{0:T(128)} %assign.5, bf16[4,16,128]{2,1,0:T(8,128)(2,1)S(1)} %collective-permute-done.13.rest_0_, bf16[4,16,128]{2,1,0:T(8,128)(2,1)S(1)} %collective-permute-done.14.rest_1_, bf16[4,16,128]{2,1,0:T(8,128)(2,1)S(1)} %collective-permute-done.15.rest_2_, ...), custom_call_target="tpu_custom_call" | custom-call | tf_op jit(solution)/shard_map/place/pallas_call | solution.py:476
Async XLA Ops:
  0.0 8.6 %copy-start.3 = (s32[16,64]{1,0:T(8,128)S(1)}, s32[16,64]{1,0:T(8,128)}, u32[]{:S(2)}) copy-start(s32[16,64]{1,0:T(8,128)} %constant.4.clone.rate.rate_row) | copy-start | bytes 12292
  0.0 8.7 %copy-start.5 = (s32[32,1]{1,0:T(8,128)S(1)}, s32[32,1]{1,0:T(8,128)}, u32[]{:S(2)}) copy-start(s32[32,1]{1,0:T(8,128)} %constant.5.clone.rate) | copy-start | bytes 388
  0.0 8.7 %copy-start.6 = (bf16[2,8,64]{2,1,0:T(8,128)(2,1)S(1)}, bf16[2,8,64]{2,1,0:T(8,128)(2,1)}, u32[]{:S(2)}) copy-start(bf16[2,8,64]{2,1,0:T(8,128)(2,1)} %new_rope.1) | copy-start | bytes 6148
  0.0 8.7 %copy-start.4 = (bf16[2,8,512]{2,1,0:T(8,128)(2,1)S(1)}, bf16[2,8,512]{2,1,0:T(8,128)(2,1)}, u32[]{:S(2)}) copy-start(bf16[2,8,512]{2,1,0:T(8,128)(2,1)} %new_lat.1) | copy-start | bytes 49156
  0.0 8.7 %copy-start.2 = (s32[2,6144]{1,0:T(2,128)S(1)}, s32[2,6144]{1,0:T(2,128)}, u32[]{:S(2)}) copy-start(s32[2,6144]{1,0:T(2,128)} %pos.1) | copy-start | bytes 147460
  0.0 8.7 %copy-start.1 = (bf16[2,6144,64]{1,2,0:T(8,128)(2,1)S(1)}, bf16[2,6144,64]{1,2,0:T(8,128)(2,1)}, u32[]{:S(2)}) copy-start(bf16[2,6144,64]{1,2,0:T(8,128)(2,1)} %param.19) | copy-start | bytes 4718596
  2.9 11.3 %collective-permute-start = (bf16[2,2,16,640]{3,2,1,0:T(8,128)(2,1)S(1)}, bf16[2,2,16,640]{3,2,1,0:T(8,128)(2,1)S(1)}, u32[]{:S(2)}, u32[]{:S(2)}) collective-permute-start(bf16[2,2,16,640]{3,2,1,0:T(8,128)(2,1)S(1)} %get-tuple-element.25), channel_id=1, source_target_pairs={{0,24},{8,16},{16,8},{24,0},{1,25},{9,17},{17,9},{25,1},{2,26},{10... | collective-permute-start | bytes 245768 | tf_op jit(solution)/shard_map/ppermute | solution.py:33
  8.0 6.9 %collective-permute-start.1 = (bf16[2,2,16,640]{3,2,1,0:T(8,128)(2,1)S(1)}, bf16[2,2,16,640]{3,2,1,0:T(8,128)(2,1)S(1)}, u32[]{:S(2)}, u32[]{:S(2)}) collective-permute-start(bf16[2,2,16,640]{3,2,1,0:T(8,128)(2,1)S(1)} %get-tuple-element.26), channel_id=1, source_target_pairs={{0,16},{8,24},{16,0},{24,8},{1,17},{9,25},{17,1},{25,9},{2,18},{10... | collective-permute-start | bytes 245768 | tf_op jit(solution)/shard_map/ppermute | solution.py:33
  8.0 6.9 %collective-permute-start.2 = (bf16[2,2,16,640]{3,2,1,0:T(8,128)(2,1)S(1)}, bf16[2,2,16,640]{3,2,1,0:T(8,128)(2,1)S(1)}, u32[]{:S(2)}, u32[]{:S(2)}) collective-permute-start(bf16[2,2,16,640]{3,2,1,0:T(8,128)(2,1)S(1)} %get-tuple-element.27), channel_id=1, source_target_pairs={{0,8},{8,0},{16,24},{24,16},{1,9},{9,1},{17,25},{25,17},{2,10},{10... | collective-permute-start | bytes 245768 | tf_op jit(solution)/shard_map/ppermute | solution.py:33
  8.6 6.7 %collective-permute-start.6 = (bf16[2,2,16,640]{3,2,1,0:T(8,128)(2,1)S(1)}, bf16[2,2,16,640]{3,2,1,0:T(8,128)(2,1)S(1)}, u32[]{:S(2)}, u32[]{:S(2)}) collective-permute-start(bf16[2,2,16,640]{3,2,1,0:T(8,128)(2,1)S(1)} %get-tuple-element.35.rest_3_), channel_id=1, source_target_pairs={{0,1},{1,0},{2,3},{3,2},{4,5},{5,4},{6,7},{7,6},{8,9},{9,8},{10,11... | collective-permute-start | bytes 245768 | tf_op jit(solution)/shard_map/ppermute | solution.py:33
  14.9 1.3 %collective-permute-start.3 = (bf16[2,2,16,640]{3,2,1,0:T(8,128)(2,1)S(1)}, bf16[2,2,16,640]{3,2,1,0:T(8,128)(2,1)S(1)}, u32[]{:S(2)}, u32[]{:S(2)}) collective-permute-start(bf16[2,2,16,640]{3,2,1,0:T(8,128)(2,1)S(1)} %collective-permute-done.rest_0_), channel_id=1, source_target_pairs={{0,1},{1,0},{2,3},{3,2},{4,5},{5,4},{6,7},{7,6},{8,9},{9,8},{10,11... | collective-permute-start | bytes 245768 | tf_op jit(solution)/shard_map/ppermute | solution.py:33
  14.9 1.4 %collective-permute-start.4 = (bf16[2,2,16,640]{3,2,1,0:T(8,128)(2,1)S(1)}, bf16[2,2,16,640]{3,2,1,0:T(8,128)(2,1)S(1)}, u32[]{:S(2)}, u32[]{:S(2)}) collective-permute-start(bf16[2,2,16,640]{3,2,1,0:T(8,128)(2,1)S(1)} %collective-permute-done.1.rest_1_), channel_id=1, source_target_pairs={{0,1},{1,0},{2,3},{3,2},{4,5},{5,4},{6,7},{7,6},{8,9},{9,8},{10,11... | collective-permute-start | bytes 245768 | tf_op jit(solution)/shard_map/ppermute | solution.py:33
  15.4 1.3 %collective-permute-start.5 = (bf16[2,2,16,640]{3,2,1,0:T(8,128)(2,1)S(1)}, bf16[2,2,16,640]{3,2,1,0:T(8,128)(2,1)S(1)}, u32[]{:S(2)}, u32[]{:S(2)}) collective-permute-start(bf16[2,2,16,640]{3,2,1,0:T(8,128)(2,1)S(1)} %collective-permute-done.2.rest_2_), channel_id=1, source_target_pairs={{0,1},{1,0},{2,3},{3,2},{4,5},{5,4},{6,7},{7,6},{8,9},{9,8},{10,11... | collective-permute-start | bytes 245768 | tf_op jit(solution)/shard_map/ppermute | solution.py:33
  16.7 27.3 %copy-start = (bf16[32,512,128]{2,1,0:T(8,128)(2,1)S(1)}, bf16[32,512,128]{2,1,0:T(8,128)(2,1)}, u32[]{:S(2)}) copy-start(bf16[32,512,128]{2,1,0:T(8,128)(2,1)} %w.1) | copy-start | bytes 12582916
  26.4 1.7 %collective-permute-start.7 = (bf16[2,2,4,16,640]{4,3,2,1,0:T(8,128)(2,1)S(1)}, bf16[2,2,4,16,640]{4,3,2,1,0:T(8,128)(2,1)S(1)}, u32[]{:S(2)}, u32[]{:S(2)}) collective-permute-start(bf16[2,2,4,16,640]{4,3,2,1,0:T(8,128)(2,1)S(1)} %get-tuple-element.37), channel_id=1, source_target_pairs={{0,1},{1,0},{2,3},{3,2},{4,5},{5,4},{6,7},{7,6},{8,9},{9,8},{10,11... | collective-permute-start | bytes 983048 | tf_op jit(solution)/shard_map/ppermute | solution.py:33
  28.8 5.5 %collective-permute-start.8 = (bf16[64,640]{1,0:T(8,128)(2,1)S(1)}, bf16[64,640]{1,0:T(8,128)(2,1)S(1)}, u32[]{:S(2)}, u32[]{:S(2)}) collective-permute-start(bf16[64,640]{1,0:T(8,128)(2,1)S(1)} %get-tuple-element.38), channel_id=1, source_target_pairs={{0,6},{2,4},{4,2},{6,0},{1,7},{3,5},{5,3},{7,1},{8,14},{10,12},{12... | collective-permute-start | bytes 245768 | tf_op jit(solution)/shard_map/ppermute | solution.py:33
  31.3 4.7 %collective-permute-start.9 = (bf16[64,640]{1,0:T(8,128)(2,1)S(1)}, bf16[64,640]{1,0:T(8,128)(2,1)S(1)}, u32[]{:S(2)}, u32[]{:S(2)}) collective-permute-start(bf16[64,640]{1,0:T(8,128)(2,1)S(1)} %get-tuple-element.39), channel_id=1, source_target_pairs={{0,4},{2,6},{4,0},{6,2},{1,5},{3,7},{5,1},{7,3},{8,12},{10,14},{12... | collective-permute-start | bytes 245768 | tf_op jit(solution)/shard_map/ppermute | solution.py:33
  31.8 4.4 %collective-permute-start.10 = (bf16[64,640]{1,0:T(8,128)(2,1)S(1)}, bf16[64,640]{1,0:T(8,128)(2,1)S(1)}, u32[]{:S(2)}, u32[]{:S(2)}) collective-permute-start(bf16[64,640]{1,0:T(8,128)(2,1)S(1)} %get-tuple-element.40), channel_id=1, source_target_pairs={{0,2},{2,0},{4,6},{6,4},{1,3},{3,1},{5,7},{7,5},{8,10},{10,8},{12,... | collective-permute-start | bytes 245768 | tf_op jit(solution)/shard_map/ppermute | solution.py:33
  36.5 7.4 %collective-permute-start.12 = (bf16[32,512]{1,0:T(8,128)(2,1)S(1)}, bf16[32,512]{1,0:T(8,128)(2,1)S(1)}, u32[]{:S(2)}, u32[]{:S(2)}) collective-permute-start(bf16[32,512]{1,0:T(8,128)(2,1)S(1)} %get-tuple-element.43), channel_id=1, source_target_pairs={{0,16},{1,9},{8,24},{9,1},{16,0},{17,25},{24,8},{25,17},{2,18},{3,... | collective-permute-start | bytes 98312 | tf_op jit(solution)/shard_map/ppermute | solution.py:456
  38.5 5.5 %collective-permute-start.11 = (bf16[16,512]{1,0:T(8,128)(2,1)S(1)}, bf16[16,512]{1,0:T(8,128)(2,1)S(1)}, u32[]{:S(2)}, u32[]{:S(2)}) collective-permute-start(bf16[16,512]{1,0:T(8,128)(2,1)S(1)} %get-tuple-element.42), channel_id=1, source_target_pairs={{0,24},{8,16},{16,8},{24,0},{1,25},{9,17},{17,9},{25,1},{2,26},{10... | collective-permute-start | bytes 49160 | tf_op jit(solution)/shard_map/ppermute | solution.py:33
  44.7 3.8 %collective-permute-start.17 = (bf16[4,16,128]{2,1,0:T(8,128)(2,1)S(1)}, bf16[4,16,128]{2,1,0:T(8,128)(2,1)S(1)}, u32[]{:S(2)}, u32[]{:S(2)}) collective-permute-start(bf16[4,16,128]{2,1,0:T(8,128)(2,1)S(1)} %value.1.rest_6_), channel_id=1, source_target_pairs={{0,2},{2,0},{4,6},{6,4},{1,3},{3,1},{5,7},{7,5},{8,10},{10,8},{12,... | collective-permute-start | bytes 49160 | tf_op jit(solution)/shard_map/ppermute | solution.py:33
  46.3 3.7 %collective-permute-start.15 = (bf16[4,16,128]{2,1,0:T(8,128)(2,1)S(1)}, bf16[4,16,128]{2,1,0:T(8,128)(2,1)S(1)}, u32[]{:S(2)}, u32[]{:S(2)}) collective-permute-start(bf16[4,16,128]{2,1,0:T(8,128)(2,1)S(1)} %value.1.rest_6_), channel_id=1, source_target_pairs={{0,4},{2,6},{4,0},{6,2},{1,5},{3,7},{5,1},{7,3},{8,12},{10,14},{12... | collective-permute-start | bytes 49160 | tf_op jit(solution)/shard_map/ppermute | solution.py:33
  47.0 4.6 %collective-permute-start.13 = (bf16[4,16,128]{2,1,0:T(8,128)(2,1)S(1)}, bf16[4,16,128]{2,1,0:T(8,128)(2,1)S(1)}, u32[]{:S(2)}, u32[]{:S(2)}) collective-permute-start(bf16[4,16,128]{2,1,0:T(8,128)(2,1)S(1)} %value.1.rest_6_), channel_id=1, source_target_pairs={{0,6},{2,4},{4,2},{6,0},{1,7},{3,5},{5,3},{7,1},{8,14},{10,12},{12... | collective-permute-start | bytes 49160 | tf_op jit(solution)/shard_map/ppermute | solution.py:33
  48.2 3.4 %collective-permute-start.19 = (bf16[4,16,128]{2,1,0:T(8,128)(2,1)S(1)}, bf16[4,16,128]{2,1,0:T(8,128)(2,1)S(1)}, u32[]{:S(2)}, u32[]{:S(2)}) collective-permute-start(bf16[4,16,128]{2,1,0:T(8,128)(2,1)S(1)} %value.1.rest_6_), channel_id=1, source_target_pairs={{0,1},{1,0},{2,3},{3,2},{4,5},{5,4},{6,7},{7,6},{8,9},{9,8},{10,11... | collective-permute-start | bytes 49160 | tf_op jit(solution)/shard_map/ppermute | solution.py:33
  48.5 3.2 %collective-permute-start.18 = (bf16[4,16,128]{2,1,0:T(8,128)(2,1)S(1)}, bf16[4,16,128]{2,1,0:T(8,128)(2,1)S(1)}, u32[]{:S(2)}, u32[]{:S(2)}) collective-permute-start(bf16[4,16,128]{2,1,0:T(8,128)(2,1)S(1)} %collective-permute-done.17.rest_4_), channel_id=1, source_target_pairs={{0,1},{1,0},{2,3},{3,2},{4,5},{5,4},{6,7},{7,6},{8,9},{9,8},{10,11... | collective-permute-start | bytes 49160 | tf_op jit(solution)/shard_map/ppermute | solution.py:33
  50.0 1.6 %collective-permute-start.16 = (bf16[4,16,128]{2,1,0:T(8,128)(2,1)S(1)}, bf16[4,16,128]{2,1,0:T(8,128)(2,1)S(1)}, u32[]{:S(2)}, u32[]{:S(2)}) collective-permute-start(bf16[4,16,128]{2,1,0:T(8,128)(2,1)S(1)} %collective-permute-done.15.rest_2_), channel_id=1, source_target_pairs={{0,1},{1,0},{2,3},{3,2},{4,5},{5,4},{6,7},{7,6},{8,9},{9,8},{10,11... | collective-permute-start | bytes 49160 | tf_op jit(solution)/shard_map/ppermute | solution.py:33
  51.6 1.2 %collective-permute-start.14 = (bf16[4,16,128]{2,1,0:T(8,128)(2,1)S(1)}, bf16[4,16,128]{2,1,0:T(8,128)(2,1)S(1)}, u32[]{:S(2)}, u32[]{:S(2)}) collective-permute-start(bf16[4,16,128]{2,1,0:T(8,128)(2,1)S(1)} %collective-permute-done.13.rest_0_), channel_id=1, source_target_pairs={{0,1},{1,0},{2,3},{3,2},{4,5},{5,4},{6,7},{7,6},{8,9},{9,8},{10,11... | collective-permute-start | bytes 49160 | tf_op jit(solution)/shard_map/ppermute | solution.py:33

commit v5 on v4

--- a/solution.py
+++ b/solution.py
@@ -191,9 +191,9 @@
 
 
 def units(R, c):
-    found = [(0, c), (R - 1, c)]
+    found = [(0, c), (1, c)]
     for i in range(1, R // 2):
-        found += [(2 * i - c, 0), (2 * i - c, 1)]
+        found += [(2 * i + c, 0), (2 * i + c, 1)]
     return found
 
 
@@ -312,13 +312,13 @@
 def value_kernel(dims, w, *rest):
     R, HC, HS, HB = dims
     n = R // 2 - 1
-    far, *pairs, near, out = rest
+    *pairs, beside, near, out = rest
     pairs = pairs[::-1]
     c = lax.axis_index("core")
     part = lax.rem(lax.axis_index("chip"), HS)
     ys = []
     for h in range(2):
-        x = [v[...] for v in (near, far)] + [v[h * HB : (h + 1) * HB] for v in pairs]
+        x = [v[...] for v in (near, beside)] + [v[h * HB : (h + 1) * HB] for v in pairs]
         x = jnp.swapaxes(jnp.stack([v.astype(F32) for v in x]), 0, 1).astype(BF)
         first = h * HC + part * HB
         y = [jnp.dot(x[e], w[first + e], preferred_element_type=F32) for e in range(HB)]
@@ -331,13 +331,13 @@
 
 def place_kernel(dims, assign, *rest):
     R, J, T, HC, HS, HB, CH = dims
-    blocks, out = rest[: 2 * CH], rest[2 * CH]
+    *blocks, beside, mine, out = rest
     g, chip, c = lax.axis_index("req"), lax.axis_index("chip"), lax.axis_index("core")
     for n in range(CH):
         token = (chip ^ n) // HS
         j, t = token // T, lax.rem(token, T)
         for b in range(2):
-            block = blocks[2 * (CH - 1 - n) + b]
+            block = (mine, beside)[n].at[b] if n < 2 else blocks[2 * (n - 2) + b]
             core, part = c ^ b, lax.rem(chip ^ n, HS)
             for slot in range(R):
                 (k, h), (k1, h1) = units(R, 0)[slot], units(R, 1)[slot]
@@ -451,16 +451,15 @@
         compiler_params=big,
         name="combine",
     )(*shares)
-    far = hop(latents[1], "req", R - 1)
-    crossed = [
+    returned = [
         lax.ppermute(
             latents[1 + i],
             ("req", "core"),
-            [(2 * g + c, 2 * (g ^ (2 * i - c)) + c) for g in range(R) for c in range(2)],
+            [(2 * g + c, 2 * (g ^ (2 * i + c)) + c) for g in range(R) for c in range(2)],
         )
         for i in reversed(range(1, R // 2))
     ]
-    returned = [far] + crossed + [latents[0]]
+    returned += [hop(latents[1], "req", 1), latents[0]]
 
     values = pl.pallas_call(
         functools.partial(value_kernel, (R, HC, HS, HB)),
@@ -471,12 +470,15 @@
         name="value",
     )(w_uv, *returned)
     gathered = []
-    for block in hops([values] * CH, "chip") + [values]:
+    for n in range(2, CH):
+        block = hop(values, "chip", n)
         gathered += [block, hop(block, "core", 1)]
+    both = jnp.stack([values, hop(values, "core", 1)])
+    gathered += [hop(both, "chip", 1), both]
     return pl.pallas_call(
         functools.partial(place_kernel, (R, J, T, HC, HS, HB, CH)),
         out_shape=jax.ShapeDtypeStruct((T, REQS, HL, DV), BF),
-        in_specs=[SMEM] + [VMEM] * (2 * CH),
+        in_specs=[SMEM] + [VMEM] * len(gathered),
         out_specs=VMEM,
         compiler_params=big,
         name="place",

time: 54.4 us -> 51.7 us (0.950)
  waiting for transfers between devices: 15.6 us -> 12.6 us
    ppermute x19 -> x18, waiting for transfers between devices: 15.6 us -> 12.6 us  [hop(): return lax.ppermute(x, axis, [(i, i ^ n) for i in range(size)])]
    ppermute x19 -> x18, starting transfers between devices: 15.4 us -> 15.8 us  [hop(): return lax.ppermute(x, axis, [(i, i ^ n) for i in range(size)])]
  transfers between devices with their start and end apart: 20 -> 19, of which waited for: 13 -> 14; matrix products, arithmetic and copies ran while one was open for 0% -> 0% of each run, Pallas kernels for 10% -> 11%
where the time goes in v5:
time: 51.7 us; the launch traced here: 51.5 us
  Pallas kernels  21.1 us (41%)
  starting transfers between devices  17.7 us (34%)
  waiting for transfers between devices  12.6 us (24%)
    ppermute x18, starting transfers between devices, hop(): return lax.ppermute(x, axis, [(i, i ^ n) for i in range(size)])  15.8 us
    ppermute x18, waiting for transfers between devices, hop(): return lax.ppermute(x, axis, [(i, i ^ n) for i in range(size)])  12.6 us
    pallas_call x1, Pallas kernels, body(): pl.pallas_call(functools.partial(attend_kernel, (R, J, T, HC, DL, CAP), B...  9.72 us
    pallas_call x1, Pallas kernels, body(): pl.pallas_call(functools.partial(prepare_kernel, (J, T, CAP, DL), cuts),...  5.47 us
    pallas_call x1, Pallas kernels, body(): pl.pallas_call(functools.partial(absorb_kernel, (R, J, T, HC, DL)), out_s...  2.84 us
    ppermute x1, starting transfers between devices, body(): lax.ppermute(latents[1 + i], ('req', 'core'), [(2 * g + c, 2 * (g ^ 2 * i...  1.91 us
    pallas_call x1, Pallas kernels, body(): pl.pallas_call(functools.partial(place_kernel, (R, J, T, HC, HS, HB, CH))...  1.42 us
  transfers between devices with their start and end apart: 19, of which 14 were waited for; matrix products, arithmetic and copies ran while one was open for 0% of the time, Pallas kernels for 11%

profile of v5, /device:TPU:0, one launch (start us, length us, event | category | flops | bytes accessed | tf_op | source)
XLA Modules:
  0.0 51.5 jit_solution(9826162603077661136)
XLA Ops:
  0.0 0.0 copy-start.3
  0.0 0.0 copy-start.5
  0.0 0.0 copy-start.6
  0.0 0.0 copy-start.4
  0.0 0.0 copy-start.2
  0.0 0.0 copy-start.1
  0.0 2.8 %absorb.1 = (bf16[2,2,16,640]{3,2,1,0:T(8,128)(2,1)S(1)}, bf16[2,2,16,640]{3,2,1,0:T(8,128)(2,1)S(1)}, bf16[2,2,16,640]{3,2,1,0:T(8,128)(2,1)S(1)}, bf16[2,2,16,640]{3,2,1,0:T(8,128)(2,1)S(1)}) custom-call(s32[8]{0:T(128)} %assign.5, s32[8]{0:T(128)} %new_pos.3, s32[16,64]{1,0:T(8,128)} %constant.4.clone.rate.rate_row, bf16[2,8,32,128]{3,2,1,0:T(8,128)(2,1)} %qn_hbm.1, ...), custom_call_target="tpu_custom_call" | custom-call | tf_op jit(solution)/shard_map/absorb/pallas_call | solution.py:376
  2.9 5.1 %collective-permute-start = (bf16[2,2,16,640]{3,2,1,0:T(8,128)(2,1)S(1)}, bf16[2,2,16,640]{3,2,1,0:T(8,128)(2,1)S(1)}, u32[]{:S(2)}, u32[]{:S(2)}) collective-permute-start(bf16[2,2,16,640]{3,2,1,0:T(8,128)(2,1)S(1)} %get-tuple-element.25), channel_id=1, source_target_pairs={{0,24},{8,16},{16,8},{24,0},{1,25},{9,17},{17,9},{25,1},{2,26},{10... | collective-permute-start | bytes 245768 | tf_op jit(solution)/shard_map/ppermute | solution.py:33
  8.0 0.0 collective-permute-start.1
  8.0 0.6 %collective-permute-start.2 = (bf16[2,2,16,640]{3,2,1,0:T(8,128)(2,1)S(1)}, bf16[2,2,16,640]{3,2,1,0:T(8,128)(2,1)S(1)}, u32[]{:S(2)}, u32[]{:S(2)}) collective-permute-start(bf16[2,2,16,640]{3,2,1,0:T(8,128)(2,1)S(1)} %get-tuple-element.27), channel_id=1, source_target_pairs={{0,8},{8,0},{16,24},{24,16},{1,9},{9,1},{17,25},{25,17},{2,10},{10... | collective-permute-start | bytes 245768 | tf_op jit(solution)/shard_map/ppermute | solution.py:33
  8.6 0.0 collective-permute-start.6
  8.6 0.0 copy-done.3
  8.7 0.0 copy-done.5
  8.7 0.0 copy-done.6
  8.7 0.0 copy-done.4
  8.7 0.0 copy-done.2
  8.7 0.0 copy-done.1
  8.7 5.5 %prepare.1 = (bf16[2,80,6272]{2,1,0:T(8,128)(2,1)S(1)}, bf16[2,6272,512]{2,1,0:T(8,128)(2,1)S(1)}) custom-call(s32[8]{0:T(128)} %assign.5, s32[8]{0:T(128)} %lengths.1, s32[8]{0:T(128)} %new_pos.3, bf16[2,8,512]{2,1,0:T(8,128)(2,1)S(1)} %copy-done.4, bf16[2,8,64]{2,1,0:T(8,128)(2,1)S(1)} %copy-done.6, s32[16,64]{1,0:T(8,128)S(1)} %copy-done.3, ...), custom_call_target="tpu_custom_call" | custom-call | bytes 25165824 | tf_op jit(solution)/shard_map/prepare/pallas_call | solution.py:394
  14.2 0.0 collective-permute-done.rest_0_
  14.2 0.7 %collective-permute-done.1.rest_1_ = bf16[2,2,16,640]{3,2,1,0:T(8,128)(2,1)S(1)} collective-permute-done((bf16[2,2,16,640]{3,2,1,0:T(8,128)(2,1)S(1)}, bf16[2,2,16,640]{3,2,1,0:T(8,128)(2,1)S(1)}, u32[]{:S(2)}, u32[]{:S(2)}) %collective-permute-start.1) | collective-permute-done | bytes 81952 | tf_op jit(solution)/shard_map/ppermute | solution.py:33
  14.9 0.0 collective-permute-done.2.rest_2_
  14.9 0.0 collective-permute-start.3
  14.9 0.5 collective-permute-start.4
  15.4 0.0 collective-permute-start.5
  15.4 0.0 collective-permute-done.6.rest_7_
  15.4 0.8 %collective-permute-done.3.rest_4_ = bf16[2,2,16,640]{3,2,1,0:T(8,128)(2,1)S(1)} collective-permute-done((bf16[2,2,16,640]{3,2,1,0:T(8,128)(2,1)S(1)}, bf16[2,2,16,640]{3,2,1,0:T(8,128)(2,1)S(1)}, u32[]{:S(2)}, u32[]{:S(2)}) %collective-permute-start.3) | collective-permute-done | bytes 81952 | tf_op jit(solution)/shard_map/ppermute | solution.py:33
  16.1 0.2 collective-permute-done.4.rest_5_
  16.3 0.4 collective-permute-done.5.rest_6_
  16.7 0.0 copy-start
  16.7 9.7 %attend.1 = (bf16[2,2,4,16,640]{4,3,2,1,0:T(8,128)(2,1)S(1)}, f32[2,2,4,16,640]{4,3,2,1,0:T(8,128)S(1)}) custom-call(bf16[2,80,6272]{2,1,0:T(8,128)(2,1)S(1)} %get-tuple-element.30.keys, bf16[2,6272,512]{2,1,0:T(8,128)(2,1)S(1)} %get-tuple-element.31.cbuf, bf16[2,2,16,640]{3,2,1,0:T(8,128)(2,1)S(1)} %collective-permute-done.rest_0_, ...), custom_call_target="tpu_custom_call" | custom-call | tf_op jit(solution)/shard_map/attend/pallas_call | solution.py:419
  26.4 0.2 collective-permute-start.7
  26.6 1.5 %collective-permute-done.7.got = bf16[2,2,4,16,640]{4,3,2,1,0:T(8,128)(2,1)S(1)} collective-permute-done((bf16[2,2,4,16,640]{4,3,2,1,0:T(8,128)(2,1)S(1)}, bf16[2,2,4,16,640]{4,3,2,1,0:T(8,128)(2,1)S(1)}, u32[]{:S(2)}, u32[]{:S(2)}) %collective-permute-start.7) | collective-permute-done | bytes 327712 | tf_op jit(solution)/shard_map/ppermute | solution.py:33
  28.1 0.8 %pair.1 = (f32[64,640]{1,0:T(8,128)S(1)}, bf16[64,640]{1,0:T(8,128)(2,1)S(1)}, bf16[64,640]{1,0:T(8,128)(2,1)S(1)}, bf16[64,640]{1,0:T(8,128)(2,1)S(1)}) custom-call(f32[2,2,4,16,640]{4,3,2,1,0:T(8,128)S(1)} %get-tuple-element.36.keep, bf16[2,2,4,16,640]{4,3,2,1,0:T(8,128)(2,1)S(1)} %collective-permute-done.7.got), custom_call_target="tpu_custom_call" | custom-call | tf_op jit(solution)/shard_map/pair/pallas_call | solution.py:436
  28.8 2.5 %collective-permute-start.8 = (bf16[64,640]{1,0:T(8,128)(2,1)S(1)}, bf16[64,640]{1,0:T(8,128)(2,1)S(1)}, u32[]{:S(2)}, u32[]{:S(2)}) collective-permute-start(bf16[64,640]{1,0:T(8,128)(2,1)S(1)} %get-tuple-element.38), channel_id=1, source_target_pairs={{0,6},{2,4},{4,2},{6,0},{1,7},{3,5},{5,3},{7,1},{8,14},{10,12},{12... | collective-permute-start | bytes 245768 | tf_op jit(solution)/shard_map/ppermute | solution.py:33
  31.4 0.5 %collective-permute-start.9 = (bf16[64,640]{1,0:T(8,128)(2,1)S(1)}, bf16[64,640]{1,0:T(8,128)(2,1)S(1)}, u32[]{:S(2)}, u32[]{:S(2)}) collective-permute-start(bf16[64,640]{1,0:T(8,128)(2,1)S(1)} %get-tuple-element.39), channel_id=1, source_target_pairs={{0,4},{2,6},{4,0},{6,2},{1,5},{3,7},{5,1},{7,3},{8,12},{10,14},{12... | collective-permute-start | bytes 245768 | tf_op jit(solution)/shard_map/ppermute | solution.py:33
  31.9 0.5 %collective-permute-start.10 = (bf16[64,640]{1,0:T(8,128)(2,1)S(1)}, bf16[64,640]{1,0:T(8,128)(2,1)S(1)}, u32[]{:S(2)}, u32[]{:S(2)}) collective-permute-start(bf16[64,640]{1,0:T(8,128)(2,1)S(1)} %get-tuple-element.40), channel_id=1, source_target_pairs={{0,2},{2,0},{4,6},{6,4},{1,3},{3,1},{5,7},{7,5},{8,10},{10,8},{12,... | collective-permute-start | bytes 245768 | tf_op jit(solution)/shard_map/ppermute | solution.py:33
  32.4 2.0 %collective-permute-done.8.rest_0_ = bf16[64,640]{1,0:T(8,128)(2,1)S(1)} collective-permute-done((bf16[64,640]{1,0:T(8,128)(2,1)S(1)}, bf16[64,640]{1,0:T(8,128)(2,1)S(1)}, u32[]{:S(2)}, u32[]{:S(2)}) %collective-permute-start.8) | collective-permute-done | bytes 81952 | tf_op jit(solution)/shard_map/ppermute | solution.py:33
  34.4 1.7 %collective-permute-done.9.rest_1_ = bf16[64,640]{1,0:T(8,128)(2,1)S(1)} collective-permute-done((bf16[64,640]{1,0:T(8,128)(2,1)S(1)}, bf16[64,640]{1,0:T(8,128)(2,1)S(1)}, u32[]{:S(2)}, u32[]{:S(2)}) %collective-permute-start.9) | collective-permute-done | bytes 81952 | tf_op jit(solution)/shard_map/ppermute | solution.py:33
  36.1 0.2 collective-permute-done.10.rest_2_
  36.3 0.2 combine.1
  36.6 1.9 %collective-permute-start.11 = (bf16[32,512]{1,0:T(8,128)(2,1)S(1)}, bf16[32,512]{1,0:T(8,128)(2,1)S(1)}, u32[]{:S(2)}, u32[]{:S(2)}) collective-permute-start(bf16[32,512]{1,0:T(8,128)(2,1)S(1)} %get-tuple-element.42), channel_id=1, source_target_pairs={{0,16},{1,25},{8,24},{9,17},{16,0},{17,9},{24,8},{25,1},{2,18},{3,... | collective-permute-start | bytes 98312 | tf_op jit(solution)/shard_map/ppermute | solution.py:455
  38.5 2.0 %collective-permute-start.12 = (bf16[16,512]{1,0:T(8,128)(2,1)S(1)}, bf16[16,512]{1,0:T(8,128)(2,1)S(1)}, u32[]{:S(2)}, u32[]{:S(2)}) collective-permute-start(bf16[16,512]{1,0:T(8,128)(2,1)S(1)} %get-tuple-element.43), channel_id=1, source_target_pairs={{0,8},{8,0},{16,24},{24,16},{1,9},{9,1},{17,25},{25,17},{2,10},{10... | collective-permute-start | bytes 49160 | tf_op jit(solution)/shard_map/ppermute | solution.py:33
  40.5 1.8 %collective-permute-done.12.rest_1_ = bf16[16,512]{1,0:T(8,128)(2,1)S(1)} collective-permute-done((bf16[16,512]{1,0:T(8,128)(2,1)S(1)}, bf16[16,512]{1,0:T(8,128)(2,1)S(1)}, u32[]{:S(2)}, u32[]{:S(2)}) %collective-permute-start.12) | collective-permute-done | bytes 16416 | tf_op jit(solution)/shard_map/ppermute | solution.py:33
  42.3 0.0 collective-permute-done.11.rest_0_
  42.3 0.0 copy-done
  42.3 0.7 %value.1 = bf16[4,16,128]{2,1,0:T(8,128)(2,1)S(1)} custom-call(bf16[32,512,128]{2,1,0:T(8,128)(2,1)S(1)} %copy-done, bf16[32,512]{1,0:T(8,128)(2,1)S(1)} %collective-permute-done.11.rest_0_, bf16[16,512]{1,0:T(8,128)(2,1)S(1)} %collective-permute-done.12.rest_1_, bf16[16,512]{1,0:T(8,128)(2,1)S(1)} %get-tuple-element.44.rest_2_), custom_call_target="tpu_custom_call" | custom-call | tf_op jit(solution)/shard_map/value/pallas_call | solution.py:464
  42.9 0.1 collective-permute-start.17
  43.0 1.7 %collective-permute-start.15 = (bf16[4,16,128]{2,1,0:T(8,128)(2,1)S(1)}, bf16[4,16,128]{2,1,0:T(8,128)(2,1)S(1)}, u32[]{:S(2)}, u32[]{:S(2)}) collective-permute-start(bf16[4,16,128]{2,1,0:T(8,128)(2,1)S(1)} %value.1), channel_id=1, source_target_pairs={{0,6},{2,4},{4,2},{6,0},{1,7},{3,5},{5,3},{7,1},{8,14},{10,12},{12... | collective-permute-start | bytes 49160 | tf_op jit(solution)/shard_map/ppermute | solution.py:33
  44.7 1.4 %collective-permute-start.13 = (bf16[4,16,128]{2,1,0:T(8,128)(2,1)S(1)}, bf16[4,16,128]{2,1,0:T(8,128)(2,1)S(1)}, u32[]{:S(2)}, u32[]{:S(2)}) collective-permute-start(bf16[4,16,128]{2,1,0:T(8,128)(2,1)S(1)} %value.1), channel_id=1, source_target_pairs={{0,4},{2,6},{4,0},{6,2},{1,5},{3,7},{5,1},{7,3},{8,12},{10,14},{12... | collective-permute-start | bytes 49160 | tf_op jit(solution)/shard_map/ppermute | solution.py:33
  46.1 0.0 collective-permute-done.17
  46.1 0.5 collective-permute-start.18
  46.7 1.2 %collective-permute-done.15.rest_2_ = bf16[4,16,128]{2,1,0:T(8,128)(2,1)S(1)} collective-permute-done((bf16[4,16,128]{2,1,0:T(8,128)(2,1)S(1)}, bf16[4,16,128]{2,1,0:T(8,128)(2,1)S(1)}, u32[]{:S(2)}, u32[]{:S(2)}) %collective-permute-start.15) | collective-permute-done | bytes 16416 | tf_op jit(solution)/shard_map/ppermute | solution.py:33
  47.8 0.0 collective-permute-start.16
  47.8 0.6 %collective-permute-done.13.rest_0_ = bf16[4,16,128]{2,1,0:T(8,128)(2,1)S(1)} collective-permute-done((bf16[4,16,128]{2,1,0:T(8,128)(2,1)S(1)}, bf16[4,16,128]{2,1,0:T(8,128)(2,1)S(1)}, u32[]{:S(2)}, u32[]{:S(2)}) %collective-permute-start.13) | collective-permute-done | bytes 16416 | tf_op jit(solution)/shard_map/ppermute | solution.py:33
  48.5 0.0 collective-permute-start.14
  48.5 0.6 %collective-permute-done.16.rest_3_ = bf16[4,16,128]{2,1,0:T(8,128)(2,1)S(1)} collective-permute-done((bf16[4,16,128]{2,1,0:T(8,128)(2,1)S(1)}, bf16[4,16,128]{2,1,0:T(8,128)(2,1)S(1)}, u32[]{:S(2)}, u32[]{:S(2)}) %collective-permute-start.16) | collective-permute-done | bytes 16416 | tf_op jit(solution)/shard_map/ppermute | solution.py:33
  49.0 0.6 %collective-permute-done.14.rest_1_ = bf16[4,16,128]{2,1,0:T(8,128)(2,1)S(1)} collective-permute-done((bf16[4,16,128]{2,1,0:T(8,128)(2,1)S(1)}, bf16[4,16,128]{2,1,0:T(8,128)(2,1)S(1)}, u32[]{:S(2)}, u32[]{:S(2)}) %collective-permute-start.14) | collective-permute-done | bytes 16416 | tf_op jit(solution)/shard_map/ppermute | solution.py:33
  49.6 0.5 collective-permute-done.18.rest_4_
  50.1 1.4 %place.1 = bf16[2,8,32,128]{3,2,1,0:T(8,128)(2,1)} custom-call(s32[8]{0:T(128)} %assign.5, bf16[4,16,128]{2,1,0:T(8,128)(2,1)S(1)} %collective-permute-done.13.rest_0_, bf16[4,16,128]{2,1,0:T(8,128)(2,1)S(1)} %collective-permute-done.14.rest_1_, bf16[4,16,128]{2,1,0:T(8,128)(2,1)S(1)} %collective-permute-done.15.rest_2_, ...), custom_call_target="tpu_custom_call" | custom-call | tf_op jit(solution)/shard_map/place/pallas_call | solution.py:478
  (1 shorter events, 0.0 us)
Async XLA Ops:
  0.0 8.6 %copy-start.3 = (s32[16,64]{1,0:T(8,128)S(1)}, s32[16,64]{1,0:T(8,128)}, u32[]{:S(2)}) copy-start(s32[16,64]{1,0:T(8,128)} %constant.4.clone.rate.rate_row) | copy-start | bytes 12292
  0.0 8.7 %copy-start.5 = (s32[32,1]{1,0:T(8,128)S(1)}, s32[32,1]{1,0:T(8,128)}, u32[]{:S(2)}) copy-start(s32[32,1]{1,0:T(8,128)} %constant.5.clone.rate) | copy-start | bytes 388
  0.0 8.7 %copy-start.6 = (bf16[2,8,64]{2,1,0:T(8,128)(2,1)S(1)}, bf16[2,8,64]{2,1,0:T(8,128)(2,1)}, u32[]{:S(2)}) copy-start(bf16[2,8,64]{2,1,0:T(8,128)(2,1)} %new_rope.1) | copy-start | bytes 6148
  0.0 8.7 %copy-start.4 = (bf16[2,8,512]{2,1,0:T(8,128)(2,1)S(1)}, bf16[2,8,512]{2,1,0:T(8,128)(2,1)}, u32[]{:S(2)}) copy-start(bf16[2,8,512]{2,1,0:T(8,128)(2,1)} %new_lat.1) | copy-start | bytes 49156
  0.0 8.7 %copy-start.2 = (s32[2,6144]{1,0:T(2,128)S(1)}, s32[2,6144]{1,0:T(2,128)}, u32[]{:S(2)}) copy-start(s32[2,6144]{1,0:T(2,128)} %pos.1) | copy-start | bytes 147460
  0.0 8.7 %copy-start.1 = (bf16[2,6144,64]{1,2,0:T(8,128)(2,1)S(1)}, bf16[2,6144,64]{1,2,0:T(8,128)(2,1)}, u32[]{:S(2)}) copy-start(bf16[2,6144,64]{1,2,0:T(8,128)(2,1)} %param.19) | copy-start | bytes 4718596
  2.9 11.3 %collective-permute-start = (bf16[2,2,16,640]{3,2,1,0:T(8,128)(2,1)S(1)}, bf16[2,2,16,640]{3,2,1,0:T(8,128)(2,1)S(1)}, u32[]{:S(2)}, u32[]{:S(2)}) collective-permute-start(bf16[2,2,16,640]{3,2,1,0:T(8,128)(2,1)S(1)} %get-tuple-element.25), channel_id=1, source_target_pairs={{0,24},{8,16},{16,8},{24,0},{1,25},{9,17},{17,9},{25,1},{2,26},{10... | collective-permute-start | bytes 245768 | tf_op jit(solution)/shard_map/ppermute | solution.py:33
  8.0 6.9 %collective-permute-start.1 = (bf16[2,2,16,640]{3,2,1,0:T(8,128)(2,1)S(1)}, bf16[2,2,16,640]{3,2,1,0:T(8,128)(2,1)S(1)}, u32[]{:S(2)}, u32[]{:S(2)}) collective-permute-start(bf16[2,2,16,640]{3,2,1,0:T(8,128)(2,1)S(1)} %get-tuple-element.26), channel_id=1, source_target_pairs={{0,16},{8,24},{16,0},{24,8},{1,17},{9,25},{17,1},{25,9},{2,18},{10... | collective-permute-start | bytes 245768 | tf_op jit(solution)/shard_map/ppermute | solution.py:33
  8.0 6.9 %collective-permute-start.2 = (bf16[2,2,16,640]{3,2,1,0:T(8,128)(2,1)S(1)}, bf16[2,2,16,640]{3,2,1,0:T(8,128)(2,1)S(1)}, u32[]{:S(2)}, u32[]{:S(2)}) collective-permute-start(bf16[2,2,16,640]{3,2,1,0:T(8,128)(2,1)S(1)} %get-tuple-element.27), channel_id=1, source_target_pairs={{0,8},{8,0},{16,24},{24,16},{1,9},{9,1},{17,25},{25,17},{2,10},{10... | collective-permute-start | bytes 245768 | tf_op jit(solution)/shard_map/ppermute | solution.py:33
  8.6 6.7 %collective-permute-start.6 = (bf16[2,2,16,640]{3,2,1,0:T(8,128)(2,1)S(1)}, bf16[2,2,16,640]{3,2,1,0:T(8,128)(2,1)S(1)}, u32[]{:S(2)}, u32[]{:S(2)}) collective-permute-start(bf16[2,2,16,640]{3,2,1,0:T(8,128)(2,1)S(1)} %get-tuple-element.35.rest_3_), channel_id=1, source_target_pairs={{0,1},{1,0},{2,3},{3,2},{4,5},{5,4},{6,7},{7,6},{8,9},{9,8},{10,11... | collective-permute-start | bytes 245768 | tf_op jit(solution)/shard_map/ppermute | solution.py:33
  14.9 1.3 %collective-permute-start.3 = (bf16[2,2,16,640]{3,2,1,0:T(8,128)(2,1)S(1)}, bf16[2,2,16,640]{3,2,1,0:T(8,128)(2,1)S(1)}, u32[]{:S(2)}, u32[]{:S(2)}) collective-permute-start(bf16[2,2,16,640]{3,2,1,0:T(8,128)(2,1)S(1)} %collective-permute-done.rest_0_), channel_id=1, source_target_pairs={{0,1},{1,0},{2,3},{3,2},{4,5},{5,4},{6,7},{7,6},{8,9},{9,8},{10,11... | collective-permute-start | bytes 245768 | tf_op jit(solution)/shard_map/ppermute | solution.py:33
  14.9 1.4 %collective-permute-start.4 = (bf16[2,2,16,640]{3,2,1,0:T(8,128)(2,1)S(1)}, bf16[2,2,16,640]{3,2,1,0:T(8,128)(2,1)S(1)}, u32[]{:S(2)}, u32[]{:S(2)}) collective-permute-start(bf16[2,2,16,640]{3,2,1,0:T(8,128)(2,1)S(1)} %collective-permute-done.1.rest_1_), channel_id=1, source_target_pairs={{0,1},{1,0},{2,3},{3,2},{4,5},{5,4},{6,7},{7,6},{8,9},{9,8},{10,11... | collective-permute-start | bytes 245768 | tf_op jit(solution)/shard_map/ppermute | solution.py:33
  15.4 1.3 %collective-permute-start.5 = (bf16[2,2,16,640]{3,2,1,0:T(8,128)(2,1)S(1)}, bf16[2,2,16,640]{3,2,1,0:T(8,128)(2,1)S(1)}, u32[]{:S(2)}, u32[]{:S(2)}) collective-permute-start(bf16[2,2,16,640]{3,2,1,0:T(8,128)(2,1)S(1)} %collective-permute-done.2.rest_2_), channel_id=1, source_target_pairs={{0,1},{1,0},{2,3},{3,2},{4,5},{5,4},{6,7},{7,6},{8,9},{9,8},{10,11... | collective-permute-start | bytes 245768 | tf_op jit(solution)/shard_map/ppermute | solution.py:33
  16.7 25.6 %copy-start = (bf16[32,512,128]{2,1,0:T(8,128)(2,1)S(1)}, bf16[32,512,128]{2,1,0:T(8,128)(2,1)}, u32[]{:S(2)}) copy-start(bf16[32,512,128]{2,1,0:T(8,128)(2,1)} %w.1) | copy-start | bytes 12582916
  26.4 1.7 %collective-permute-start.7 = (bf16[2,2,4,16,640]{4,3,2,1,0:T(8,128)(2,1)S(1)}, bf16[2,2,4,16,640]{4,3,2,1,0:T(8,128)(2,1)S(1)}, u32[]{:S(2)}, u32[]{:S(2)}) collective-permute-start(bf16[2,2,4,16,640]{4,3,2,1,0:T(8,128)(2,1)S(1)} %get-tuple-element.37), channel_id=1, source_target_pairs={{0,1},{1,0},{2,3},{3,2},{4,5},{5,4},{6,7},{7,6},{8,9},{9,8},{10,11... | collective-permute-start | bytes 983048 | tf_op jit(solution)/shard_map/ppermute | solution.py:33
  28.8 5.5 %collective-permute-start.8 = (bf16[64,640]{1,0:T(8,128)(2,1)S(1)}, bf16[64,640]{1,0:T(8,128)(2,1)S(1)}, u32[]{:S(2)}, u32[]{:S(2)}) collective-permute-start(bf16[64,640]{1,0:T(8,128)(2,1)S(1)} %get-tuple-element.38), channel_id=1, source_target_pairs={{0,6},{2,4},{4,2},{6,0},{1,7},{3,5},{5,3},{7,1},{8,14},{10,12},{12... | collective-permute-start | bytes 245768 | tf_op jit(solution)/shard_map/ppermute | solution.py:33
  31.4 4.7 %collective-permute-start.9 = (bf16[64,640]{1,0:T(8,128)(2,1)S(1)}, bf16[64,640]{1,0:T(8,128)(2,1)S(1)}, u32[]{:S(2)}, u32[]{:S(2)}) collective-permute-start(bf16[64,640]{1,0:T(8,128)(2,1)S(1)} %get-tuple-element.39), channel_id=1, source_target_pairs={{0,4},{2,6},{4,0},{6,2},{1,5},{3,7},{5,1},{7,3},{8,12},{10,14},{12... | collective-permute-start | bytes 245768 | tf_op jit(solution)/shard_map/ppermute | solution.py:33
  31.9 4.4 %collective-permute-start.10 = (bf16[64,640]{1,0:T(8,128)(2,1)S(1)}, bf16[64,640]{1,0:T(8,128)(2,1)S(1)}, u32[]{:S(2)}, u32[]{:S(2)}) collective-permute-start(bf16[64,640]{1,0:T(8,128)(2,1)S(1)} %get-tuple-element.40), channel_id=1, source_target_pairs={{0,2},{2,0},{4,6},{6,4},{1,3},{3,1},{5,7},{7,5},{8,10},{10,8},{12,... | collective-permute-start | bytes 245768 | tf_op jit(solution)/shard_map/ppermute | solution.py:33
  36.6 5.7 %collective-permute-start.11 = (bf16[32,512]{1,0:T(8,128)(2,1)S(1)}, bf16[32,512]{1,0:T(8,128)(2,1)S(1)}, u32[]{:S(2)}, u32[]{:S(2)}) collective-permute-start(bf16[32,512]{1,0:T(8,128)(2,1)S(1)} %get-tuple-element.42), channel_id=1, source_target_pairs={{0,16},{1,25},{8,24},{9,17},{16,0},{17,9},{24,8},{25,1},{2,18},{3,... | collective-permute-start | bytes 98312 | tf_op jit(solution)/shard_map/ppermute | solution.py:455
  38.5 3.8 %collective-permute-start.12 = (bf16[16,512]{1,0:T(8,128)(2,1)S(1)}, bf16[16,512]{1,0:T(8,128)(2,1)S(1)}, u32[]{:S(2)}, u32[]{:S(2)}) collective-permute-start(bf16[16,512]{1,0:T(8,128)(2,1)S(1)} %get-tuple-element.43), channel_id=1, source_target_pairs={{0,8},{8,0},{16,24},{24,16},{1,9},{9,1},{17,25},{25,17},{2,10},{10... | collective-permute-start | bytes 49160 | tf_op jit(solution)/shard_map/ppermute | solution.py:33
  42.9 3.2 %collective-permute-start.17 = (bf16[4,16,128]{2,1,0:T(8,128)(2,1)S(1)}, bf16[4,16,128]{2,1,0:T(8,128)(2,1)S(1)}, u32[]{:S(2)}, u32[]{:S(2)}) collective-permute-start(bf16[4,16,128]{2,1,0:T(8,128)(2,1)S(1)} %value.1), channel_id=1, source_target_pairs={{0,1},{1,0},{2,3},{3,2},{4,5},{5,4},{6,7},{7,6},{8,9},{9,8},{10,11... | collective-permute-start | bytes 49160 | tf_op jit(solution)/shard_map/ppermute | solution.py:33
  43.0 4.8 %collective-permute-start.15 = (bf16[4,16,128]{2,1,0:T(8,128)(2,1)S(1)}, bf16[4,16,128]{2,1,0:T(8,128)(2,1)S(1)}, u32[]{:S(2)}, u32[]{:S(2)}) collective-permute-start(bf16[4,16,128]{2,1,0:T(8,128)(2,1)S(1)} %value.1), channel_id=1, source_target_pairs={{0,6},{2,4},{4,2},{6,0},{1,7},{3,5},{5,3},{7,1},{8,14},{10,12},{12... | collective-permute-start | bytes 49160 | tf_op jit(solution)/shard_map/ppermute | solution.py:33
  44.7 3.7 %collective-permute-start.13 = (bf16[4,16,128]{2,1,0:T(8,128)(2,1)S(1)}, bf16[4,16,128]{2,1,0:T(8,128)(2,1)S(1)}, u32[]{:S(2)}, u32[]{:S(2)}) collective-permute-start(bf16[4,16,128]{2,1,0:T(8,128)(2,1)S(1)} %value.1), channel_id=1, source_target_pairs={{0,4},{2,6},{4,0},{6,2},{1,5},{3,7},{5,1},{7,3},{8,12},{10,14},{12... | collective-permute-start | bytes 49160 | tf_op jit(solution)/shard_map/ppermute | solution.py:33
  46.1 4.0 %collective-permute-start.18 = (bf16[2,4,16,128]{3,2,1,0:T(8,128)(2,1)S(1)}, bf16[2,4,16,128]{3,2,1,0:T(8,128)(2,1)S(1)}, u32[]{:S(2)}, u32[]{:S(2)}) collective-permute-start(bf16[2,4,16,128]{3,2,1,0:T(8,128)(2,1)S(1)} %pad_maximum_fusion.rest_5_), channel_id=1, source_target_pairs={{0,2},{2,0},{4,6},{6,4},{1,3},{3,1},{5,7},{7,5},{8,10},{10,8},{12,... | collective-permute-start | bytes 98312 | tf_op jit(solution)/shard_map/ppermute | solution.py:33
  47.8 1.2 %collective-permute-start.16 = (bf16[4,16,128]{2,1,0:T(8,128)(2,1)S(1)}, bf16[4,16,128]{2,1,0:T(8,128)(2,1)S(1)}, u32[]{:S(2)}, u32[]{:S(2)}) collective-permute-start(bf16[4,16,128]{2,1,0:T(8,128)(2,1)S(1)} %collective-permute-done.15.rest_2_), channel_id=1, source_target_pairs={{0,1},{1,0},{2,3},{3,2},{4,5},{5,4},{6,7},{7,6},{8,9},{9,8},{10,11... | collective-permute-start | bytes 49160 | tf_op jit(solution)/shard_map/ppermute | solution.py:33
  48.5 1.2 %collective-permute-start.14 = (bf16[4,16,128]{2,1,0:T(8,128)(2,1)S(1)}, bf16[4,16,128]{2,1,0:T(8,128)(2,1)S(1)}, u32[]{:S(2)}, u32[]{:S(2)}) collective-permute-start(bf16[4,16,128]{2,1,0:T(8,128)(2,1)S(1)} %collective-permute-done.13.rest_0_), channel_id=1, source_target_pairs={{0,1},{1,0},{2,3},{3,2},{4,5},{5,4},{6,7},{7,6},{8,9},{9,8},{10,11... | collective-permute-start | bytes 49160 | tf_op jit(solution)/shard_map/ppermute | solution.py:33

commit v6 on v5

--- a/solution.py
+++ b/solution.py
@@ -201,7 +201,6 @@
     R, J, T, HC, DL, CAP = dims
     own, other = rest[:R][::-1], rest[R : 2 * R][::-1]
     send, keep, q, sbuf, acc = rest[2 * R :]
-    nb = CAP // B
     NQ = T * R * 2 * HC
     c = lax.axis_index("core")
     for j in range(J):
@@ -212,8 +211,10 @@
                 q[j, base : base + HC, :] = jnp.where(c == 0, mine, theirs)
                 q[j, base + HC : base + 2 * HC, :] = jnp.where(c == 0, theirs, mine)
     nt = (((1,), (1,)), ((), ()))
+    cuts = [0, *range(B // 2, CAP, B), CAP + LANES]
+    nb = len(cuts) - 1
     blocks = [
-        (j, pl.ds(i * B, B + (LANES if i == nb - 1 else 0))) for j in range(J) for i in range(nb)
+        (j, pl.ds(cuts[i], cuts[i + 1] - cuts[i])) for j in range(J) for i in range(nb)
     ]
 
     def score(n):
@@ -370,6 +371,7 @@
     rates = turn_rates(DR)
     rate_row = jnp.asarray(np.tile(np.concatenate([rates, rates])[None], (R * J * T, 1)))
     rate_col = jnp.asarray(rates[:, None])
+    places = assignment
     assignment, new_pos, lengths = in_hbm(assignment), in_hbm(new_pos), in_hbm(lengths)
     big = pltpu.CompilerParams(vmem_limit_bytes=8 << 20)
 
@@ -482,7 +484,7 @@
         out_specs=VMEM,
         compiler_params=big,
         name="place",
-    )(assignment, *gathered)
+    )(places, *gathered)
 
 
 def solution(mesh):

time: 51.7 us -> 51.6 us (level)
  no operation moved by 1% of the time
where the time goes in v6:
time: 51.6 us; the launch traced here: 51.4 us
  Pallas kernels  20.9 us (41%)
  starting transfers between devices  17.7 us (34%)
  waiting for transfers between devices  12.6 us (24%)
    ppermute x18, starting transfers between devices, hop(): return lax.ppermute(x, axis, [(i, i ^ n) for i in range(size)])  15.8 us
    ppermute x18, waiting for transfers between devices, hop(): return lax.ppermute(x, axis, [(i, i ^ n) for i in range(size)])  12.6 us
    pallas_call x1, Pallas kernels, body(): pl.pallas_call(functools.partial(attend_kernel, (R, J, T, HC, DL, CAP), B...  9.67 us
    pallas_call x1, Pallas kernels, body(): pl.pallas_call(functools.partial(prepare_kernel, (J, T, CAP, DL), cuts),...  5.47 us
    pallas_call x1, Pallas kernels, body(): pl.pallas_call(functools.partial(absorb_kernel, (R, J, T, HC, DL)), out_s...  2.84 us
    ppermute x1, starting transfers between devices, body(): lax.ppermute(latents[1 + i], ('req', 'core'), [(2 * g + c, 2 * (g ^ 2 * i...  1.92 us
    pallas_call x1, Pallas kernels, body(): pl.pallas_call(functools.partial(place_kernel, (R, J, T, HC, HS, HB, CH))...  1.3 us
  transfers between devices with their start and end apart: 19, of which 14 were waited for; matrix products, arithmetic and copies ran while one was open for 0% of the time, Pallas kernels for 11%

profile of v6, /device:TPU:0, one launch (start us, length us, event | category | flops | bytes accessed | tf_op | source)
XLA Modules:
  0.0 51.4 jit_solution(8590070391355092816)
XLA Ops:
  0.0 0.0 copy-start.3
  0.0 0.0 copy-start.5
  0.0 0.0 copy-start.7
  0.0 0.0 copy-start.4
  0.0 0.0 copy-start.2
  0.0 0.0 copy-start.1
  0.0 2.8 %absorb.1 = (bf16[2,2,16,640]{3,2,1,0:T(8,128)(2,1)S(1)}, bf16[2,2,16,640]{3,2,1,0:T(8,128)(2,1)S(1)}, bf16[2,2,16,640]{3,2,1,0:T(8,128)(2,1)S(1)}, bf16[2,2,16,640]{3,2,1,0:T(8,128)(2,1)S(1)}) custom-call(s32[8]{0:T(128)} %assign.5, s32[8]{0:T(128)} %new_pos.3, s32[16,64]{1,0:T(8,128)} %constant.4.clone.rate.rate_row, bf16[2,8,32,128]{3,2,1,0:T(8,128)(2,1)} %qn_hbm.1, ...), custom_call_target="tpu_custom_call" | custom-call | tf_op jit(solution)/shard_map/absorb/pallas_call | solution.py:378
  2.9 5.1 %collective-permute-start = (bf16[2,2,16,640]{3,2,1,0:T(8,128)(2,1)S(1)}, bf16[2,2,16,640]{3,2,1,0:T(8,128)(2,1)S(1)}, u32[]{:S(2)}, u32[]{:S(2)}) collective-permute-start(bf16[2,2,16,640]{3,2,1,0:T(8,128)(2,1)S(1)} %get-tuple-element.25), channel_id=1, source_target_pairs={{0,24},{8,16},{16,8},{24,0},{1,25},{9,17},{17,9},{25,1},{2,26},{10... | collective-permute-start | bytes 245768 | tf_op jit(solution)/shard_map/ppermute | solution.py:33
  8.0 0.0 collective-permute-start.1
  8.0 0.6 %collective-permute-start.2 = (bf16[2,2,16,640]{3,2,1,0:T(8,128)(2,1)S(1)}, bf16[2,2,16,640]{3,2,1,0:T(8,128)(2,1)S(1)}, u32[]{:S(2)}, u32[]{:S(2)}) collective-permute-start(bf16[2,2,16,640]{3,2,1,0:T(8,128)(2,1)S(1)} %get-tuple-element.27), channel_id=1, source_target_pairs={{0,8},{8,0},{16,24},{24,16},{1,9},{9,1},{17,25},{25,17},{2,10},{10... | collective-permute-start | bytes 245768 | tf_op jit(solution)/shard_map/ppermute | solution.py:33
  8.6 0.0 collective-permute-start.6
  8.6 0.0 copy-done.3
  8.7 0.0 copy-done.5
  8.7 0.0 copy-done.7
  8.7 0.0 copy-done.4
  8.7 0.0 copy-done.2
  8.7 0.0 copy-done.1
  8.7 5.5 %prepare.1 = (bf16[2,80,6272]{2,1,0:T(8,128)(2,1)S(1)}, bf16[2,6272,512]{2,1,0:T(8,128)(2,1)S(1)}) custom-call(s32[8]{0:T(128)} %assign.5, s32[8]{0:T(128)} %lengths.1, s32[8]{0:T(128)} %new_pos.3, bf16[2,8,512]{2,1,0:T(8,128)(2,1)S(1)} %copy-done.4, bf16[2,8,64]{2,1,0:T(8,128)(2,1)S(1)} %copy-done.7, s32[16,64]{1,0:T(8,128)S(1)} %copy-done.3, ...), custom_call_target="tpu_custom_call" | custom-call | bytes 25165824 | tf_op jit(solution)/shard_map/prepare/pallas_call | solution.py:396
  14.2 0.0 collective-permute-done.rest_0_
  14.2 0.7 %collective-permute-done.1.rest_1_ = bf16[2,2,16,640]{3,2,1,0:T(8,128)(2,1)S(1)} collective-permute-done((bf16[2,2,16,640]{3,2,1,0:T(8,128)(2,1)S(1)}, bf16[2,2,16,640]{3,2,1,0:T(8,128)(2,1)S(1)}, u32[]{:S(2)}, u32[]{:S(2)}) %collective-permute-start.1) | collective-permute-done | bytes 81952 | tf_op jit(solution)/shard_map/ppermute | solution.py:33
  14.9 0.0 collective-permute-done.2.rest_2_
  14.9 0.0 collective-permute-start.3
  14.9 0.5 collective-permute-start.4
  15.4 0.0 collective-permute-start.5
  15.4 0.0 collective-permute-done.6.rest_7_
  15.4 0.8 %collective-permute-done.3.rest_4_ = bf16[2,2,16,640]{3,2,1,0:T(8,128)(2,1)S(1)} collective-permute-done((bf16[2,2,16,640]{3,2,1,0:T(8,128)(2,1)S(1)}, bf16[2,2,16,640]{3,2,1,0:T(8,128)(2,1)S(1)}, u32[]{:S(2)}, u32[]{:S(2)}) %collective-permute-start.3) | collective-permute-done | bytes 81952 | tf_op jit(solution)/shard_map/ppermute | solution.py:33
  16.1 0.2 collective-permute-done.4.rest_5_
  16.3 0.4 collective-permute-done.5.rest_6_
  16.7 0.0 copy-start
  16.7 9.7 %attend.1 = (bf16[2,2,4,16,640]{4,3,2,1,0:T(8,128)(2,1)S(1)}, f32[2,2,4,16,640]{4,3,2,1,0:T(8,128)S(1)}) custom-call(bf16[2,80,6272]{2,1,0:T(8,128)(2,1)S(1)} %get-tuple-element.30.keys, bf16[2,6272,512]{2,1,0:T(8,128)(2,1)S(1)} %get-tuple-element.31.cbuf, bf16[2,2,16,640]{3,2,1,0:T(8,128)(2,1)S(1)} %collective-permute-done.rest_0_, ...), custom_call_target="tpu_custom_call" | custom-call | tf_op jit(solution)/shard_map/attend/pallas_call | solution.py:421
  26.3 0.0 copy-start.6
  26.4 0.2 collective-permute-start.7
  26.6 1.5 %collective-permute-done.7.got = bf16[2,2,4,16,640]{4,3,2,1,0:T(8,128)(2,1)S(1)} collective-permute-done((bf16[2,2,4,16,640]{4,3,2,1,0:T(8,128)(2,1)S(1)}, bf16[2,2,4,16,640]{4,3,2,1,0:T(8,128)(2,1)S(1)}, u32[]{:S(2)}, u32[]{:S(2)}) %collective-permute-start.7) | collective-permute-done | bytes 327712 | tf_op jit(solution)/shard_map/ppermute | solution.py:33
  28.0 0.8 %pair.1 = (f32[64,640]{1,0:T(8,128)S(1)}, bf16[64,640]{1,0:T(8,128)(2,1)S(1)}, bf16[64,640]{1,0:T(8,128)(2,1)S(1)}, bf16[64,640]{1,0:T(8,128)(2,1)S(1)}) custom-call(f32[2,2,4,16,640]{4,3,2,1,0:T(8,128)S(1)} %get-tuple-element.36.keep, bf16[2,2,4,16,640]{4,3,2,1,0:T(8,128)(2,1)S(1)} %collective-permute-done.7.got), custom_call_target="tpu_custom_call" | custom-call | tf_op jit(solution)/shard_map/pair/pallas_call | solution.py:438
  28.8 2.5 %collective-permute-start.8 = (bf16[64,640]{1,0:T(8,128)(2,1)S(1)}, bf16[64,640]{1,0:T(8,128)(2,1)S(1)}, u32[]{:S(2)}, u32[]{:S(2)}) collective-permute-start(bf16[64,640]{1,0:T(8,128)(2,1)S(1)} %get-tuple-element.38), channel_id=1, source_target_pairs={{0,6},{2,4},{4,2},{6,0},{1,7},{3,5},{5,3},{7,1},{8,14},{10,12},{12... | collective-permute-start | bytes 245768 | tf_op jit(solution)/shard_map/ppermute | solution.py:33
  31.3 0.5 collective-permute-start.9
  31.8 0.5 %collective-permute-start.10 = (bf16[64,640]{1,0:T(8,128)(2,1)S(1)}, bf16[64,640]{1,0:T(8,128)(2,1)S(1)}, u32[]{:S(2)}, u32[]{:S(2)}) collective-permute-start(bf16[64,640]{1,0:T(8,128)(2,1)S(1)} %get-tuple-element.40), channel_id=1, source_target_pairs={{0,2},{2,0},{4,6},{6,4},{1,3},{3,1},{5,7},{7,5},{8,10},{10,8},{12,... | collective-permute-start | bytes 245768 | tf_op jit(solution)/shard_map/ppermute | solution.py:33
  32.4 2.0 %collective-permute-done.8.rest_0_ = bf16[64,640]{1,0:T(8,128)(2,1)S(1)} collective-permute-done((bf16[64,640]{1,0:T(8,128)(2,1)S(1)}, bf16[64,640]{1,0:T(8,128)(2,1)S(1)}, u32[]{:S(2)}, u32[]{:S(2)}) %collective-permute-start.8) | collective-permute-done | bytes 81952 | tf_op jit(solution)/shard_map/ppermute | solution.py:33
  34.3 1.7 %collective-permute-done.9.rest_1_ = bf16[64,640]{1,0:T(8,128)(2,1)S(1)} collective-permute-done((bf16[64,640]{1,0:T(8,128)(2,1)S(1)}, bf16[64,640]{1,0:T(8,128)(2,1)S(1)}, u32[]{:S(2)}, u32[]{:S(2)}) %collective-permute-start.9) | collective-permute-done | bytes 81952 | tf_op jit(solution)/shard_map/ppermute | solution.py:33
  36.0 0.2 collective-permute-done.10.rest_2_
  36.3 0.2 combine.1
  36.5 1.9 %collective-permute-start.11 = (bf16[32,512]{1,0:T(8,128)(2,1)S(1)}, bf16[32,512]{1,0:T(8,128)(2,1)S(1)}, u32[]{:S(2)}, u32[]{:S(2)}) collective-permute-start(bf16[32,512]{1,0:T(8,128)(2,1)S(1)} %get-tuple-element.42), channel_id=1, source_target_pairs={{0,16},{1,25},{8,24},{9,17},{16,0},{17,9},{24,8},{25,1},{2,18},{3,... | collective-permute-start | bytes 98312 | tf_op jit(solution)/shard_map/ppermute | solution.py:457
  38.4 2.0 %collective-permute-start.12 = (bf16[16,512]{1,0:T(8,128)(2,1)S(1)}, bf16[16,512]{1,0:T(8,128)(2,1)S(1)}, u32[]{:S(2)}, u32[]{:S(2)}) collective-permute-start(bf16[16,512]{1,0:T(8,128)(2,1)S(1)} %get-tuple-element.43), channel_id=1, source_target_pairs={{0,8},{8,0},{16,24},{24,16},{1,9},{9,1},{17,25},{25,17},{2,10},{10... | collective-permute-start | bytes 49160 | tf_op jit(solution)/shard_map/ppermute | solution.py:33
  40.5 1.8 %collective-permute-done.12.rest_1_ = bf16[16,512]{1,0:T(8,128)(2,1)S(1)} collective-permute-done((bf16[16,512]{1,0:T(8,128)(2,1)S(1)}, bf16[16,512]{1,0:T(8,128)(2,1)S(1)}, u32[]{:S(2)}, u32[]{:S(2)}) %collective-permute-start.12) | collective-permute-done | bytes 16416 | tf_op jit(solution)/shard_map/ppermute | solution.py:33
  42.2 0.0 collective-permute-done.11.rest_0_
  42.2 0.0 copy-done
  42.2 0.7 %value.1 = bf16[4,16,128]{2,1,0:T(8,128)(2,1)S(1)} custom-call(bf16[32,512,128]{2,1,0:T(8,128)(2,1)S(1)} %copy-done, bf16[32,512]{1,0:T(8,128)(2,1)S(1)} %collective-permute-done.11.rest_0_, bf16[16,512]{1,0:T(8,128)(2,1)S(1)} %collective-permute-done.12.rest_1_, bf16[16,512]{1,0:T(8,128)(2,1)S(1)} %get-tuple-element.44.rest_2_), custom_call_target="tpu_custom_call" | custom-call | tf_op jit(solution)/shard_map/value/pallas_call | solution.py:466
  42.9 0.1 collective-permute-start.17
  43.0 1.7 %collective-permute-start.15 = (bf16[4,16,128]{2,1,0:T(8,128)(2,1)S(1)}, bf16[4,16,128]{2,1,0:T(8,128)(2,1)S(1)}, u32[]{:S(2)}, u32[]{:S(2)}) collective-permute-start(bf16[4,16,128]{2,1,0:T(8,128)(2,1)S(1)} %value.1), channel_id=1, source_target_pairs={{0,6},{2,4},{4,2},{6,0},{1,7},{3,5},{5,3},{7,1},{8,14},{10,12},{12... | collective-permute-start | bytes 49160 | tf_op jit(solution)/shard_map/ppermute | solution.py:33
  44.7 1.4 %collective-permute-start.13 = (bf16[4,16,128]{2,1,0:T(8,128)(2,1)S(1)}, bf16[4,16,128]{2,1,0:T(8,128)(2,1)S(1)}, u32[]{:S(2)}, u32[]{:S(2)}) collective-permute-start(bf16[4,16,128]{2,1,0:T(8,128)(2,1)S(1)} %value.1), channel_id=1, source_target_pairs={{0,4},{2,6},{4,0},{6,2},{1,5},{3,7},{5,1},{7,3},{8,12},{10,14},{12... | collective-permute-start | bytes 49160 | tf_op jit(solution)/shard_map/ppermute | solution.py:33
  46.1 0.0 collective-permute-done.17
  46.1 0.5 collective-permute-start.18
  46.6 1.2 %collective-permute-done.15.rest_2_ = bf16[4,16,128]{2,1,0:T(8,128)(2,1)S(1)} collective-permute-done((bf16[4,16,128]{2,1,0:T(8,128)(2,1)S(1)}, bf16[4,16,128]{2,1,0:T(8,128)(2,1)S(1)}, u32[]{:S(2)}, u32[]{:S(2)}) %collective-permute-start.15) | collective-permute-done | bytes 16416 | tf_op jit(solution)/shard_map/ppermute | solution.py:33
  47.8 0.0 collective-permute-start.16
  47.8 0.6 %collective-permute-done.13.rest_0_ = bf16[4,16,128]{2,1,0:T(8,128)(2,1)S(1)} collective-permute-done((bf16[4,16,128]{2,1,0:T(8,128)(2,1)S(1)}, bf16[4,16,128]{2,1,0:T(8,128)(2,1)S(1)}, u32[]{:S(2)}, u32[]{:S(2)}) %collective-permute-start.13) | collective-permute-done | bytes 16416 | tf_op jit(solution)/shard_map/ppermute | solution.py:33
  48.4 0.0 collective-permute-start.14
  48.4 0.5 %collective-permute-done.16.rest_3_ = bf16[4,16,128]{2,1,0:T(8,128)(2,1)S(1)} collective-permute-done((bf16[4,16,128]{2,1,0:T(8,128)(2,1)S(1)}, bf16[4,16,128]{2,1,0:T(8,128)(2,1)S(1)}, u32[]{:S(2)}, u32[]{:S(2)}) %collective-permute-start.16) | collective-permute-done | bytes 16416 | tf_op jit(solution)/shard_map/ppermute | solution.py:33
  49.0 0.6 %collective-permute-done.14.rest_1_ = bf16[4,16,128]{2,1,0:T(8,128)(2,1)S(1)} collective-permute-done((bf16[4,16,128]{2,1,0:T(8,128)(2,1)S(1)}, bf16[4,16,128]{2,1,0:T(8,128)(2,1)S(1)}, u32[]{:S(2)}, u32[]{:S(2)}) %collective-permute-start.14) | collective-permute-done | bytes 16416 | tf_op jit(solution)/shard_map/ppermute | solution.py:33
  49.6 0.5 collective-permute-done.18.rest_4_
  50.1 0.0 copy-done.6
  50.1 1.3 %place.1 = bf16[2,8,32,128]{3,2,1,0:T(8,128)(2,1)} custom-call(s32[8]{0:T(128)S(1)} %copy-done.6, bf16[4,16,128]{2,1,0:T(8,128)(2,1)S(1)} %collective-permute-done.13.rest_0_, bf16[4,16,128]{2,1,0:T(8,128)(2,1)S(1)} %collective-permute-done.14.rest_1_, bf16[4,16,128]{2,1,0:T(8,128)(2,1)S(1)} %collective-permute-done.15.rest_2_, ...), custom_call_target="tpu_custom_call" | custom-call | tf_op jit(solution)/shard_map/place/pallas_call | solution.py:480
  (1 shorter events, 0.0 us)
Async XLA Ops:
  0.0 8.6 %copy-start.3 = (s32[16,64]{1,0:T(8,128)S(1)}, s32[16,64]{1,0:T(8,128)}, u32[]{:S(2)}) copy-start(s32[16,64]{1,0:T(8,128)} %constant.4.clone.rate.rate_row) | copy-start | bytes 12292
  0.0 8.7 %copy-start.5 = (s32[32,1]{1,0:T(8,128)S(1)}, s32[32,1]{1,0:T(8,128)}, u32[]{:S(2)}) copy-start(s32[32,1]{1,0:T(8,128)} %constant.5.clone.rate) | copy-start | bytes 388
  0.0 8.7 %copy-start.7 = (bf16[2,8,64]{2,1,0:T(8,128)(2,1)S(1)}, bf16[2,8,64]{2,1,0:T(8,128)(2,1)}, u32[]{:S(2)}) copy-start(bf16[2,8,64]{2,1,0:T(8,128)(2,1)} %new_rope.1) | copy-start | bytes 6148
  0.0 8.7 %copy-start.4 = (bf16[2,8,512]{2,1,0:T(8,128)(2,1)S(1)}, bf16[2,8,512]{2,1,0:T(8,128)(2,1)}, u32[]{:S(2)}) copy-start(bf16[2,8,512]{2,1,0:T(8,128)(2,1)} %new_lat.1) | copy-start | bytes 49156
  0.0 8.7 %copy-start.2 = (s32[2,6144]{1,0:T(2,128)S(1)}, s32[2,6144]{1,0:T(2,128)}, u32[]{:S(2)}) copy-start(s32[2,6144]{1,0:T(2,128)} %pos.1) | copy-start | bytes 147460
  0.0 8.7 %copy-start.1 = (bf16[2,6144,64]{1,2,0:T(8,128)(2,1)S(1)}, bf16[2,6144,64]{1,2,0:T(8,128)(2,1)}, u32[]{:S(2)}) copy-start(bf16[2,6144,64]{1,2,0:T(8,128)(2,1)} %param.19) | copy-start | bytes 4718596
  2.9 11.3 %collective-permute-start = (bf16[2,2,16,640]{3,2,1,0:T(8,128)(2,1)S(1)}, bf16[2,2,16,640]{3,2,1,0:T(8,128)(2,1)S(1)}, u32[]{:S(2)}, u32[]{:S(2)}) collective-permute-start(bf16[2,2,16,640]{3,2,1,0:T(8,128)(2,1)S(1)} %get-tuple-element.25), channel_id=1, source_target_pairs={{0,24},{8,16},{16,8},{24,0},{1,25},{9,17},{17,9},{25,1},{2,26},{10... | collective-permute-start | bytes 245768 | tf_op jit(solution)/shard_map/ppermute | solution.py:33
  8.0 6.9 %collective-permute-start.1 = (bf16[2,2,16,640]{3,2,1,0:T(8,128)(2,1)S(1)}, bf16[2,2,16,640]{3,2,1,0:T(8,128)(2,1)S(1)}, u32[]{:S(2)}, u32[]{:S(2)}) collective-permute-start(bf16[2,2,16,640]{3,2,1,0:T(8,128)(2,1)S(1)} %get-tuple-element.26), channel_id=1, source_target_pairs={{0,16},{8,24},{16,0},{24,8},{1,17},{9,25},{17,1},{25,9},{2,18},{10... | collective-permute-start | bytes 245768 | tf_op jit(solution)/shard_map/ppermute | solution.py:33
  8.0 6.9 %collective-permute-start.2 = (bf16[2,2,16,640]{3,2,1,0:T(8,128)(2,1)S(1)}, bf16[2,2,16,640]{3,2,1,0:T(8,128)(2,1)S(1)}, u32[]{:S(2)}, u32[]{:S(2)}) collective-permute-start(bf16[2,2,16,640]{3,2,1,0:T(8,128)(2,1)S(1)} %get-tuple-element.27), channel_id=1, source_target_pairs={{0,8},{8,0},{16,24},{24,16},{1,9},{9,1},{17,25},{25,17},{2,10},{10... | collective-permute-start | bytes 245768 | tf_op jit(solution)/shard_map/ppermute | solution.py:33
  8.6 6.7 %collective-permute-start.6 = (bf16[2,2,16,640]{3,2,1,0:T(8,128)(2,1)S(1)}, bf16[2,2,16,640]{3,2,1,0:T(8,128)(2,1)S(1)}, u32[]{:S(2)}, u32[]{:S(2)}) collective-permute-start(bf16[2,2,16,640]{3,2,1,0:T(8,128)(2,1)S(1)} %get-tuple-element.35.rest_3_), channel_id=1, source_target_pairs={{0,1},{1,0},{2,3},{3,2},{4,5},{5,4},{6,7},{7,6},{8,9},{9,8},{10,11... | collective-permute-start | bytes 245768 | tf_op jit(solution)/shard_map/ppermute | solution.py:33
  14.9 1.3 %collective-permute-start.3 = (bf16[2,2,16,640]{3,2,1,0:T(8,128)(2,1)S(1)}, bf16[2,2,16,640]{3,2,1,0:T(8,128)(2,1)S(1)}, u32[]{:S(2)}, u32[]{:S(2)}) collective-permute-start(bf16[2,2,16,640]{3,2,1,0:T(8,128)(2,1)S(1)} %collective-permute-done.rest_0_), channel_id=1, source_target_pairs={{0,1},{1,0},{2,3},{3,2},{4,5},{5,4},{6,7},{7,6},{8,9},{9,8},{10,11... | collective-permute-start | bytes 245768 | tf_op jit(solution)/shard_map/ppermute | solution.py:33
  14.9 1.4 %collective-permute-start.4 = (bf16[2,2,16,640]{3,2,1,0:T(8,128)(2,1)S(1)}, bf16[2,2,16,640]{3,2,1,0:T(8,128)(2,1)S(1)}, u32[]{:S(2)}, u32[]{:S(2)}) collective-permute-start(bf16[2,2,16,640]{3,2,1,0:T(8,128)(2,1)S(1)} %collective-permute-done.1.rest_1_), channel_id=1, source_target_pairs={{0,1},{1,0},{2,3},{3,2},{4,5},{5,4},{6,7},{7,6},{8,9},{9,8},{10,11... | collective-permute-start | bytes 245768 | tf_op jit(solution)/shard_map/ppermute | solution.py:33
  15.4 1.3 %collective-permute-start.5 = (bf16[2,2,16,640]{3,2,1,0:T(8,128)(2,1)S(1)}, bf16[2,2,16,640]{3,2,1,0:T(8,128)(2,1)S(1)}, u32[]{:S(2)}, u32[]{:S(2)}) collective-permute-start(bf16[2,2,16,640]{3,2,1,0:T(8,128)(2,1)S(1)} %collective-permute-done.2.rest_2_), channel_id=1, source_target_pairs={{0,1},{1,0},{2,3},{3,2},{4,5},{5,4},{6,7},{7,6},{8,9},{9,8},{10,11... | collective-permute-start | bytes 245768 | tf_op jit(solution)/shard_map/ppermute | solution.py:33
  16.7 25.6 %copy-start = (bf16[32,512,128]{2,1,0:T(8,128)(2,1)S(1)}, bf16[32,512,128]{2,1,0:T(8,128)(2,1)}, u32[]{:S(2)}) copy-start(bf16[32,512,128]{2,1,0:T(8,128)(2,1)} %w.1) | copy-start | bytes 12582916
  26.3 23.8 %copy-start.6 = (s32[8]{0:T(128)S(1)}, s32[8]{0:T(128)}, u32[]{:S(2)}) copy-start(s32[8]{0:T(128)} %assign.5) | copy-start | bytes 100
  26.4 1.7 %collective-permute-start.7 = (bf16[2,2,4,16,640]{4,3,2,1,0:T(8,128)(2,1)S(1)}, bf16[2,2,4,16,640]{4,3,2,1,0:T(8,128)(2,1)S(1)}, u32[]{:S(2)}, u32[]{:S(2)}) collective-permute-start(bf16[2,2,4,16,640]{4,3,2,1,0:T(8,128)(2,1)S(1)} %get-tuple-element.37), channel_id=1, source_target_pairs={{0,1},{1,0},{2,3},{3,2},{4,5},{5,4},{6,7},{7,6},{8,9},{9,8},{10,11... | collective-permute-start | bytes 983048 | tf_op jit(solution)/shard_map/ppermute | solution.py:33
  28.8 5.5 %collective-permute-start.8 = (bf16[64,640]{1,0:T(8,128)(2,1)S(1)}, bf16[64,640]{1,0:T(8,128)(2,1)S(1)}, u32[]{:S(2)}, u32[]{:S(2)}) collective-permute-start(bf16[64,640]{1,0:T(8,128)(2,1)S(1)} %get-tuple-element.38), channel_id=1, source_target_pairs={{0,6},{2,4},{4,2},{6,0},{1,7},{3,5},{5,3},{7,1},{8,14},{10,12},{12... | collective-permute-start | bytes 245768 | tf_op jit(solution)/shard_map/ppermute | solution.py:33
  31.3 4.7 %collective-permute-start.9 = (bf16[64,640]{1,0:T(8,128)(2,1)S(1)}, bf16[64,640]{1,0:T(8,128)(2,1)S(1)}, u32[]{:S(2)}, u32[]{:S(2)}) collective-permute-start(bf16[64,640]{1,0:T(8,128)(2,1)S(1)} %get-tuple-element.39), channel_id=1, source_target_pairs={{0,4},{2,6},{4,0},{6,2},{1,5},{3,7},{5,1},{7,3},{8,12},{10,14},{12... | collective-permute-start | bytes 245768 | tf_op jit(solution)/shard_map/ppermute | solution.py:33
  31.8 4.4 %collective-permute-start.10 = (bf16[64,640]{1,0:T(8,128)(2,1)S(1)}, bf16[64,640]{1,0:T(8,128)(2,1)S(1)}, u32[]{:S(2)}, u32[]{:S(2)}) collective-permute-start(bf16[64,640]{1,0:T(8,128)(2,1)S(1)} %get-tuple-element.40), channel_id=1, source_target_pairs={{0,2},{2,0},{4,6},{6,4},{1,3},{3,1},{5,7},{7,5},{8,10},{10,8},{12,... | collective-permute-start | bytes 245768 | tf_op jit(solution)/shard_map/ppermute | solution.py:33
  36.5 5.7 %collective-permute-start.11 = (bf16[32,512]{1,0:T(8,128)(2,1)S(1)}, bf16[32,512]{1,0:T(8,128)(2,1)S(1)}, u32[]{:S(2)}, u32[]{:S(2)}) collective-permute-start(bf16[32,512]{1,0:T(8,128)(2,1)S(1)} %get-tuple-element.42), channel_id=1, source_target_pairs={{0,16},{1,25},{8,24},{9,17},{16,0},{17,9},{24,8},{25,1},{2,18},{3,... | collective-permute-start | bytes 98312 | tf_op jit(solution)/shard_map/ppermute | solution.py:457
  38.4 3.8 %collective-permute-start.12 = (bf16[16,512]{1,0:T(8,128)(2,1)S(1)}, bf16[16,512]{1,0:T(8,128)(2,1)S(1)}, u32[]{:S(2)}, u32[]{:S(2)}) collective-permute-start(bf16[16,512]{1,0:T(8,128)(2,1)S(1)} %get-tuple-element.43), channel_id=1, source_target_pairs={{0,8},{8,0},{16,24},{24,16},{1,9},{9,1},{17,25},{25,17},{2,10},{10... | collective-permute-start | bytes 49160 | tf_op jit(solution)/shard_map/ppermute | solution.py:33
  42.9 3.2 %collective-permute-start.17 = (bf16[4,16,128]{2,1,0:T(8,128)(2,1)S(1)}, bf16[4,16,128]{2,1,0:T(8,128)(2,1)S(1)}, u32[]{:S(2)}, u32[]{:S(2)}) collective-permute-start(bf16[4,16,128]{2,1,0:T(8,128)(2,1)S(1)} %value.1), channel_id=1, source_target_pairs={{0,1},{1,0},{2,3},{3,2},{4,5},{5,4},{6,7},{7,6},{8,9},{9,8},{10,11... | collective-permute-start | bytes 49160 | tf_op jit(solution)/shard_map/ppermute | solution.py:33
  43.0 4.8 %collective-permute-start.15 = (bf16[4,16,128]{2,1,0:T(8,128)(2,1)S(1)}, bf16[4,16,128]{2,1,0:T(8,128)(2,1)S(1)}, u32[]{:S(2)}, u32[]{:S(2)}) collective-permute-start(bf16[4,16,128]{2,1,0:T(8,128)(2,1)S(1)} %value.1), channel_id=1, source_target_pairs={{0,6},{2,4},{4,2},{6,0},{1,7},{3,5},{5,3},{7,1},{8,14},{10,12},{12... | collective-permute-start | bytes 49160 | tf_op jit(solution)/shard_map/ppermute | solution.py:33
  44.7 3.7 %collective-permute-start.13 = (bf16[4,16,128]{2,1,0:T(8,128)(2,1)S(1)}, bf16[4,16,128]{2,1,0:T(8,128)(2,1)S(1)}, u32[]{:S(2)}, u32[]{:S(2)}) collective-permute-start(bf16[4,16,128]{2,1,0:T(8,128)(2,1)S(1)} %value.1), channel_id=1, source_target_pairs={{0,4},{2,6},{4,0},{6,2},{1,5},{3,7},{5,1},{7,3},{8,12},{10,14},{12... | collective-permute-start | bytes 49160 | tf_op jit(solution)/shard_map/ppermute | solution.py:33
  46.1 4.0 %collective-permute-start.18 = (bf16[2,4,16,128]{3,2,1,0:T(8,128)(2,1)S(1)}, bf16[2,4,16,128]{3,2,1,0:T(8,128)(2,1)S(1)}, u32[]{:S(2)}, u32[]{:S(2)}) collective-permute-start(bf16[2,4,16,128]{3,2,1,0:T(8,128)(2,1)S(1)} %pad_maximum_fusion.rest_5_), channel_id=1, source_target_pairs={{0,2},{2,0},{4,6},{6,4},{1,3},{3,1},{5,7},{7,5},{8,10},{10,8},{12,... | collective-permute-start | bytes 98312 | tf_op jit(solution)/shard_map/ppermute | solution.py:33
  47.8 1.2 %collective-permute-start.16 = (bf16[4,16,128]{2,1,0:T(8,128)(2,1)S(1)}, bf16[4,16,128]{2,1,0:T(8,128)(2,1)S(1)}, u32[]{:S(2)}, u32[]{:S(2)}) collective-permute-start(bf16[4,16,128]{2,1,0:T(8,128)(2,1)S(1)} %collective-permute-done.15.rest_2_), channel_id=1, source_target_pairs={{0,1},{1,0},{2,3},{3,2},{4,5},{5,4},{6,7},{7,6},{8,9},{9,8},{10,11... | collective-permute-start | bytes 49160 | tf_op jit(solution)/shard_map/ppermute | solution.py:33
  48.4 1.2 %collective-permute-start.14 = (bf16[4,16,128]{2,1,0:T(8,128)(2,1)S(1)}, bf16[4,16,128]{2,1,0:T(8,128)(2,1)S(1)}, u32[]{:S(2)}, u32[]{:S(2)}) collective-permute-start(bf16[4,16,128]{2,1,0:T(8,128)(2,1)S(1)} %collective-permute-done.13.rest_0_), channel_id=1, source_target_pairs={{0,1},{1,0},{2,3},{3,2},{4,5},{5,4},{6,7},{7,6},{8,9},{9,8},{10,11... | collective-permute-start | bytes 49160 | tf_op jit(solution)/shard_map/ppermute | solution.py:33
